TPU v7x, 128 devices: a whole 4x4x4 slice. The times are simulated.
128 devices in a mesh: ctx: 16 (over y, z), tp: 8 (over x, core).
Axes of the slice: x: 4, y: 4, z: 4, core: 2. Of those that a mesh axis runs over, the one named last changes fastest.
Arguments:
- queries: bfloat16 [4096, 8192], P('ctx', 'tp'), may hold values from -6 to 6
- new_keys: bfloat16 [4096, 1024], P('ctx', 'tp'), may hold values from -6 to 6
- new_values: bfloat16 [4096, 1024], P('ctx', 'tp'), may hold values from -6 to 6
- positions: int32 [4096], P('ctx'), may hold values from 0 to 262143, as said below
- cache_keys: bfloat16 [32768, 1024], P('ctx', 'tp'), may hold values from -6 to 6
- cache_values: bfloat16 [32768, 1024], P('ctx', 'tp'), may hold values from -6 to 6
- pattern: int32 [64, 4], P('ctx'), may hold values from 0 to 15, all different within a row; in each aligned block of 4 rows (0 to 3, 4 to 7, ...) at most 2 rows name the same one
- out_weight: bfloat16 [8192, 8192], P('tp'), may hold values from -0.0625 to 0.0625
Outputs:
- mixed: bfloat16 [4096, 8192], P(('ctx', 'tp'))
Inputs may be any that keep to these rules, and one draw needn't show every extreme that they name: All 4096 positions are distinct. `pattern`: each row names 4 different segments; among the 4 query blocks of one ctx device at most 2 name the same segment, and 2 do in some devices.
All inputs are finite; a program needn't handle non-finite values.
Results may differ from a plain program's by a relative error of at most 0.0075.
Values may be sent and summed in bfloat16 or wider, within the bound.
No kernel may reach another device: no remote copies, remote signals or barrier semaphores. Data moves between devices by JAX's collectives and lax.ppermute only.
A program may use at most 128 MiB of HBM per device.

v0:
```python
import functools
import math

import jax
import jax.numpy as jnp
from jax import lax
from jax.experimental import pallas as pl
from jax.experimental.pallas import tpu as pltpu
from jax.sharding import PartitionSpec as P


HD = 128
GROUP = 8
SIDE = 4
XN = 4
QB = 64
PIECE = 32
STEP_ROWS = 256
STEP_KEYS = 512
SEG = 2048
NEW = 256
QW = GROUP * HD
META = 16
V_AT = SEG + NEW
RET_W = QW + 128
SEND_W = QW + 128
BASE = 64
NEG = -1e30
SCALE = 1.0 / math.sqrt(HD)
TO_EXP2 = SCALE * math.log2(math.e)
BF = jnp.bfloat16
F32 = jnp.float32
AXES = ("ctx", "tp")


def pairs(kind, shift):
    out = []
    for y in range(SIDE):
        for z in range(SIDE):
            for x in range(XN):
                for c in range(2):
                    to = [y, z, x, c]
                    if kind == "c":
                        to[3] = 1 - c
                    elif kind == "x":
                        to[2] = (x + shift) % XN
                    else:
                        along = (0 if c == 0 else 1) if kind == "k" else (1 if c == 0 else 0)
                        to[along] = (to[along] + shift) % SIDE
                    src = (y * SIDE + z) * 2 * XN + x * 2 + c
                    dst = (to[0] * SIDE + to[1]) * 2 * XN + to[2] * 2 + to[3]
                    out.append((src, dst))
    return out


def move(value, kind, shift):
    return lax.ppermute(value, AXES, pairs(kind, shift))


def digits(positions):
    p = positions.astype(jnp.int32)
    return jnp.stack([p // (BASE * BASE), (p // BASE) % BASE, p % BASE]).astype(BF)


def dot_t(a, b):
    return lax.dot_general(a, b, (((1,), (1,)), ((), ())), preferred_element_type=F32)


def attend_kernel(n_home, n_kv, bases, resume, final, flags, *refs):
    refs = list(refs)
    q_refs = [refs.pop(0) for _ in range(n_home)]
    kv_refs = [refs.pop(0) for _ in range(n_kv)]
    if resume:
        acc_in, ml_in = refs.pop(0), refs.pop(0)
    if final:
        outs = [refs.pop(0) for _ in range(n_home)]
    else:
        acc_out, ml_out = refs.pop(0), refs.pop(0)
    k_scr, v_scr, meta_scr, q_scr, qpos_scr, m_scr, acc_scr, sems = refs
    home_id = pl.program_id(0)
    tokens = NEW
    blocks = NEW // QB

    def fetch(j):
        return (
            pltpu.make_async_copy(kv_refs[j].at[pl.ds(0, V_AT)], k_scr.at[j], sems.at[j, 0]),
            pltpu.make_async_copy(
                kv_refs[j].at[pl.ds(V_AT, V_AT)], v_scr.at[j, :, pl.ds(0, HD)], sems.at[j, 1]
            ),
            pltpu.make_async_copy(
                kv_refs[j].at[pl.ds(2 * V_AT, META)], meta_scr.at[j], sems.at[j, 2]
            ),
        )

    @pl.when(home_id == 0)
    def _():
        for j in range(n_kv):
            for copy in fetch(j):
                copy.start()
        for j in range(n_kv):
            v_scr[j, :, HD:] = jnp.ones((V_AT, HD), BF)

    if n_home == 1:
        q_src = q_refs[0]
    else:
        q_src = q_scr
        for home in range(n_home):

            @pl.when(home_id == home)
            def _(home=home):
                q_scr[...] = q_refs[home][...]

    for h in range(GROUP):
        cols = slice(h * HD, (h + 1) * HD)
        if resume:
            m_scr[:, cols] = jnp.broadcast_to(ml_in[:, h : h + 1], (tokens, HD))
            acc_scr[:, h * 2 * HD : h * 2 * HD + HD] = acc_in[:, cols]
            acc_scr[:, h * 2 * HD + HD : (h + 1) * 2 * HD] = jnp.broadcast_to(
                ml_in[:, GROUP + h : GROUP + h + 1], (tokens, HD)
            )
        else:
            m_scr[:, cols] = jnp.full((tokens, HD), NEG, F32)
            acc_scr[:, h * 2 * HD : (h + 1) * 2 * HD] = jnp.zeros((tokens, 2 * HD), F32)

    @pl.when(home_id == 0)
    def _():
        for j in range(n_kv):
            for copy in fetch(j):
                copy.wait()

    packed = q_src[:, QW:].astype(F32)
    qpos_scr[...] = jnp.broadcast_to(
        packed[:, :1] * (BASE * BASE) + packed[:, 1:2] * BASE + packed[:, 2:3], (tokens, HD)
    )

    def advance(q, m, acc, k, v, mask):
        s = dot_t(q, k)
        if mask is not None:
            s = jnp.where(mask, s, NEG)
        peak = jnp.broadcast_to(jnp.max(s, axis=1, keepdims=True), m.shape)
        top = jnp.maximum(m, peak)
        p = jnp.exp2((s - jnp.concatenate([top] * (s.shape[1] // HD), axis=1)) * TO_EXP2)
        decay = jnp.exp2((m - top) * TO_EXP2)
        acc = acc * jnp.concatenate([decay, decay], axis=1) + jnp.dot(
            p.astype(BF), v, preferred_element_type=F32
        )
        return top, acc

    def fresh(j, carry):
        meta = meta_scr[j].astype(F32)
        parts = [
            jnp.concatenate([meta[2 * n : 2 * n + 1], meta[2 * n + 1 : 2 * n + 2]], axis=1)
            for n in range(3)
        ]
        kpos = parts[0] * (BASE * BASE) + parts[1] * BASE + parts[2]
        qpos = qpos_scr[...]
        mask = kpos <= jnp.concatenate([qpos, qpos], axis=1)
        k = k_scr[j, SEG:, :]
        v = v_scr[j, SEG:, :]
        for h in range(GROUP):
            cols = slice(h * HD, (h + 1) * HD)
            wide = slice(h * 2 * HD, (h + 1) * 2 * HD)
            top, acc = advance(q_src[:, cols], m_scr[:, cols], acc_scr[:, wide], k, v, mask)
            m_scr[:, cols] = top
            acc_scr[:, wide] = acc
        return carry

    per_pass = STEP_ROWS // QB

    def cached(item, carry):
        j, block = item // blocks, item % blocks
        at = ((bases[0] + home_id) * SIDE + bases[1] + j) * blocks + block

        @pl.when(flags[at] > 0)
        def _():
            rows = pl.ds(pl.multiple_of(block * QB, QB), QB)
            for first in range(0, GROUP, per_pass):
                heads = range(first, first + per_pass)
                q = jnp.concatenate([q_src[rows, h * HD : (h + 1) * HD] for h in heads], axis=0)
                m = jnp.concatenate([m_scr[rows, h * HD : (h + 1) * HD] for h in heads], axis=0)
                acc = jnp.concatenate(
                    [acc_scr[rows, h * 2 * HD : (h + 1) * 2 * HD] for h in heads], axis=0
                )
                for n in range(SEG // STEP_KEYS):
                    keys = slice(n * STEP_KEYS, (n + 1) * STEP_KEYS)
                    m, acc = advance(q, m, acc, k_scr[j, keys, :], v_scr[j, keys, :], None)
                for n, h in enumerate(heads):
                    part = slice(n * QB, (n + 1) * QB)
                    m_scr[rows, h * HD : (h + 1) * HD] = m[part]
                    acc_scr[rows, h * 2 * HD : (h + 1) * 2 * HD] = acc[part]

        return carry

    if n_kv == 1:
        fresh(0, 0)
    else:
        lax.fori_loop(0, n_kv, fresh, 0)
    lax.fori_loop(0, n_kv * blocks, cached, 0)

    lane = lax.broadcasted_iota(jnp.int32, (tokens, HD), 1)
    if not final:
        ml = jnp.zeros((tokens, HD), F32)
        for h in range(GROUP):
            acc_out[:, h * HD : (h + 1) * HD] = acc_scr[:, h * 2 * HD : h * 2 * HD + HD]
            ml = jnp.where(lane == h, m_scr[:, h * HD : (h + 1) * HD], ml)
            ml = jnp.where(lane == GROUP + h, acc_scr[:, h * 2 * HD + HD : (h + 1) * 2 * HD], ml)
        ml_out[...] = ml
        return

    def emit(out):
        logs = jnp.zeros((tokens, HD), F32)
        for h in range(GROUP):
            cols = slice(h * HD, (h + 1) * HD)
            total = acc_scr[:, h * 2 * HD + HD : (h + 1) * 2 * HD]
            out[:, cols] = (acc_scr[:, h * 2 * HD : h * 2 * HD + HD] / total).astype(BF)
            log = m_scr[:, cols] * SCALE + jnp.log(total)
            logs = jnp.where(lax.rem(lane, GROUP) == h, log, logs)
        hi = logs.astype(BF).astype(F32)
        mid = (logs - hi).astype(BF).astype(F32)
        parts = jnp.where(lane < GROUP, hi, jnp.where(lane < 2 * GROUP, mid, logs - hi - mid))
        out[:, QW:] = parts.astype(BF)

    for home in range(n_home):
        if n_home == 1:
            emit(outs[0])
        else:
            pl.when(home_id == home)(functools.partial(emit, outs[home]))


def attend(flags, q_list, kv_list, bases, state=None, final=False):
    n_home, n_kv = len(q_list), len(kv_list)
    fixed = lambda shape: pl.BlockSpec(shape, lambda i, f: (0,) * len(shape))
    turn = lambda width: pl.BlockSpec((NEW, width), lambda i, f: (i, 0))
    in_specs = [fixed((NEW, SEND_W))] * n_home + [pl.BlockSpec(memory_space=pl.ANY)] * n_kv
    args = list(q_list) + list(kv_list)
    if state is not None:
        in_specs += [turn(QW), turn(HD)]
        args += list(state)
    if final:
        out_shape = [jax.ShapeDtypeStruct((NEW, RET_W), BF)] * n_home
        out_specs = [fixed((NEW, RET_W))] * n_home
    else:
        out_shape = [
            jax.ShapeDtypeStruct((n_home * NEW, QW), F32),
            jax.ShapeDtypeStruct((n_home * NEW, HD), F32),
        ]
        out_specs = [turn(QW), turn(HD)]
    work = n_home * n_kv * NEW * GROUP * (SEG // 4 + NEW)
    return pl.pallas_call(
        functools.partial(attend_kernel, n_home, n_kv, bases, state is not None, final),
        out_shape=out_shape,
        grid_spec=pltpu.PrefetchScalarGridSpec(
            num_scalar_prefetch=1,
            grid=(n_home,),
            in_specs=in_specs,
            out_specs=out_specs,
            scratch_shapes=[
                pltpu.VMEM((n_kv, V_AT, HD), BF),
                pltpu.VMEM((n_kv, V_AT, 2 * HD), BF),
                pltpu.VMEM((n_kv, META, HD), BF),
                pltpu.VMEM((NEW, SEND_W), BF),
                pltpu.VMEM((NEW, HD), F32),
                pltpu.VMEM((NEW, QW), F32),
                pltpu.VMEM((NEW, 2 * QW), F32),
                pltpu.SemaphoreType.DMA((n_kv, 3)),
            ],
        ),
        compiler_params=pltpu.CompilerParams(vmem_limit_bytes=24 << 20),
        cost_estimate=pl.CostEstimate(
            flops=work * HD * 4 * 2,
            bytes_accessed=n_home * NEW * QW * 8,
            transcendentals=work,
        ),
    )(flags, *args)


def project_kernel(n_parts, core, *refs):
    w_ref, *outs = refs[max(n_parts, 1) :]
    if n_parts == 0:
        att = refs[0]
        keep_ref, send_ref = outs
    else:
        parts = refs[:n_parts]
        keep_ref, send_ref, att = outs

        @pl.when(pl.program_id(0) == 0)
        def _():
            merge(core, parts, att)

    result = jnp.dot(att[...], w_ref[...], preferred_element_type=F32).astype(BF)
    keep_ref[...] = result[: NEW // 2]
    send_ref[...] = result[NEW // 2 :]


def merge(core, parts, att):
    for t in range(NEW // PIECE):
        rows = slice(t * PIECE, (t + 1) * PIECE)
        logs = []
        for part in parts:
            packed = part[rows, QW:].astype(F32)
            logs.append(
                packed[:, :GROUP]
                + packed[:, GROUP : 2 * GROUP]
                + packed[:, 2 * GROUP : 3 * GROUP]
            )
        top = functools.reduce(jnp.maximum, logs)
        shares = [jnp.exp(log - top) for log in logs]
        total = functools.reduce(jnp.add, shares)
        shares = [share / total for share in shares]
        away = jnp.where(core[0] == t % 2, 0, NEW // 2)
        at = pl.multiple_of(away + (t // 2) * PIECE, PIECE)
        for h in range(GROUP):
            mixed = functools.reduce(
                jnp.add,
                [
                    share[:, h : h + 1] * part[rows, h * HD : (h + 1) * HD].astype(F32)
                    for share, part in zip(shares, parts)
                ],
            )
            att[pl.ds(at, PIECE), h * HD : (h + 1) * HD] = mixed.astype(BF)


def project(core, parts, weight, column, columns):
    width = weight.shape[1] // columns
    tile = 1024
    steps = width // tile
    merged = len(parts) == 1
    half = pl.BlockSpec((NEW // 2, tile), lambda n, c: (0, n))
    att_spec = pl.BlockSpec((NEW, QW), lambda n, c: (0, 0))
    out_shape = [jax.ShapeDtypeStruct((NEW // 2, width), BF)] * 2
    out_specs = [half, half]
    if not merged:
        out_shape.append(jax.ShapeDtypeStruct((NEW, QW), BF))
        out_specs.append(att_spec)
    return pl.pallas_call(
        functools.partial(project_kernel, 0 if merged else len(parts)),
        out_shape=out_shape,
        grid_spec=pltpu.PrefetchScalarGridSpec(
            num_scalar_prefetch=1,
            grid=(steps,),
            in_specs=[pl.BlockSpec(part.shape, lambda n, c: (0, 0)) for part in parts]
            + [pl.BlockSpec((QW, tile), lambda n, c: (0, column * steps + n))],
            out_specs=out_specs,
        ),
        compiler_params=pltpu.CompilerParams(vmem_limit_bytes=24 << 20),
        cost_estimate=pl.CostEstimate(
            flops=4 * NEW * QW * width,
            bytes_accessed=QW * width * 2 + NEW * width * 2,
            transcendentals=0,
        ),
    )(core, *parts, weight)


def after(value, *others):
    return lax.optimization_barrier((value, *others))[0]


def per_device(
    queries, new_keys, new_values, positions, cache_keys, cache_values, pattern, out_weight
):
    ctx = lax.axis_index("ctx")
    tp = lax.axis_index("tp")
    core = tp % 2
    x = tp // 2
    y, z = ctx // SIDE, ctx % SIDE

    places = digits(positions)
    picks = pattern.reshape(-1).astype(BF)
    q_own = jnp.concatenate([queries, jnp.pad(places.T, ((0, 0), (0, HD - 3)))], axis=1)
    q_meta = jnp.pad(picks, (0, META * SEND_W - picks.shape[0])).reshape(META, SEND_W)
    q_own = jnp.concatenate([q_own, q_meta], axis=0)
    k_meta = jnp.pad(places.reshape(-1, HD), ((0, META - 3 * NEW // HD), (0, 0)))
    kv_own = jnp.concatenate([cache_keys, new_keys, cache_values, new_values, k_meta], axis=0)

    order = (0, 1, 3, 2)
    q_at = {0: q_own}
    kv_at = {0: kv_own}
    for shift in (1, 3, 2):
        q_at[-shift % SIDE] = move(q_own, "q", shift)

    steps = jnp.array(order, jnp.int32)
    along_y = ((y + steps) % SIDE) * SIDE + z
    along_z = y * SIDE + (z + steps) % SIDE
    segments = jnp.where(core == 0, along_y, along_z).astype(F32)

    def flags_of(rows):
        named = rows.astype(F32).reshape(-1, 1, NEW // QB, picks.shape[0] * QB // NEW)
        hits = jnp.any(named == segments[None, :, None, None], axis=-1)
        return hits.astype(jnp.int32).reshape(-1)

    def state_of(flags, homes, kvs, state=None, final=False):
        return attend(
            flags,
            [q_at[order[n]] for n in homes],
            [kv_at[order[n]] for n in kvs],
            (homes[0], kvs[0]),
            state,
            final,
        )

    away, others = (1, 2, 3), (1, 2, 3)
    own_state = state_of(flags_of(picks[None]), (0,), (0,))
    for shift in (1, 3):
        kv_at[-shift % SIDE] = move(after(kv_own, *own_state), "k", shift)
    flags = flags_of(jnp.stack([q_at[o][NEW, : picks.shape[0]] for o in order]))
    state = state_of(flags, away, (0,))
    kv_at[2] = move(after(kv_own, *state), "k", 2)
    state = state_of(flags, away, (1, 2), state)
    partials = state_of(flags, away, (3,), state, True)
    backs = [move(part, "q", order[n]) for n, part in zip(away, partials)]
    own_state = [after(value, *partials) for value in own_state]
    mine = state_of(flags, (0,), others, own_state, True)

    core_id = core.reshape(1)
    keep0, send0, att = project(core_id, [*mine, *backs], out_weight, 0, 2)
    other0 = move(send0, "c", 0)
    keep1, send1 = project(core_id, [att], out_weight, 1, 2)
    other1 = move(send1, "c", 0)

    def finish(keep, other):
        def group(shift):
            at = ((x + shift) % XN) * PIECE
            return lax.dynamic_slice_in_dim(keep, at, PIECE, 0).astype(
                F32
            ) + lax.dynamic_slice_in_dim(other, at, PIECE, 0).astype(F32)

        arrived = [move(group(shift).astype(BF), "x", shift) for shift in (1, 3, 2)]
        result = group(0)
        for value in arrived:
            result = result + value.astype(F32)
        return result.astype(BF)

    return jnp.concatenate([finish(keep0, other0), finish(keep1, other1)], axis=1)


def solution(mesh):
    placed = (
        P("ctx", "tp"),
        P("ctx", "tp"),
        P("ctx", "tp"),
        P("ctx"),
        P("ctx", "tp"),
        P("ctx", "tp"),
        P("ctx", None),
        P("tp", None),
    )

    return jax.shard_map(
        per_device, mesh=mesh, in_specs=placed, out_specs=P(("ctx", "tp"), None), check_vma=False
    )
```

profile of v0, /device:TPU:1, one launch (start us, length us, event | category | flops | bytes accessed | tf_op | source)
XLA Modules:
  0.0 152.4 jit_solution(5753762116831134537)
XLA Ops:
  0.0 0.8 and_select_fusion.5
  0.8 0.7 fusion.12
  1.4 0.1 convert_element_type.146
  1.5 0.1 reshape.69
  1.6 0.1 copy.19
  1.8 0.0 copy-start.3
  1.8 1.2 fusion.4.refs_0_
  3.0 0.0 copy-start.6
  3.0 0.0 copy-start.5
  3.0 3.8 %collective-permute-start.2 = (bf16[272,1152]{1,0:T(8,128)(2,1)S(1)}, bf16[272,1152]{1,0:T(8,128)(2,1)}, u32[]{:S(2)}, u32[]{:S(2)}) collective-permute-start(bf16[272,1152]{1,0:T(8,128)(2,1)S(1)} %fusion.4.refs_0_), channel_id=1, source_target_pairs={{0,16},{1,65},{2,18},{3,67},{4,20},{5,69},{6,22},{7,71},{8,24},{9,... | collective-permute-start | bytes 1880072 | tf_op jit(solution)/shard_map/ppermute | solution.py:57
  6.8 0.4 collective-permute-start.1
  7.2 2.3 %collective-permute-start = (bf16[272,1152]{1,0:T(8,128)(2,1)S(1)}, bf16[272,1152]{1,0:T(8,128)(2,1)}, u32[]{:S(2)}, u32[]{:S(2)}) collective-permute-start(bf16[272,1152]{1,0:T(8,128)(2,1)S(1)} %fusion.4.refs_0_), channel_id=1, source_target_pairs={{0,24},{1,97},{2,26},{3,99},{4,28},{5,101},{6,30},{7,103},{8,0},{9... | collective-permute-start | bytes 1880072 | tf_op jit(solution)/shard_map/ppermute | solution.py:57
  9.6 0.1 constant_dynamic-update-slice_fusion.2
  9.7 0.2 compare_reduce_fusion.1
  9.9 0.1 reshape.71.flags
  10.0 4.3 %shard_map.91 = (f32[256,1024]{1,0:T(8,128)S(1)}, f32[256,128]{1,0:T(8,128)S(1)}) custom-call(s32[16]{0:T(128)S(1)} %reshape.71.flags, bf16[272,1152]{1,0:T(8,128)(2,1)S(1)} %fusion.4.refs_0_, bf16[4624,128]{1,0:T(8,128)(2,1)S(1)} %constant_dynamic-update-slice_fusion.refs_1_.refs_3_), custom_call_target="tpu_custom_call" | custom-call | flops 1610612736 | bytes 2097152 | tf_op jit(solution)/shard_map/pallas_call | solution.py:249
  14.4 1.0 copy-done
  15.4 1.6 %collective-permute-start.4 = (bf16[4624,128]{1,0:T(8,128)(2,1)S(1)}, bf16[4624,128]{1,0:T(8,128)(2,1)S(1)}, u32[]{:S(2)}, u32[]{:S(2)}) collective-permute-start(bf16[4624,128]{1,0:T(8,128)(2,1)S(1)} %constant_dynamic-update-slice_fusion.refs_1_.refs_3_), channel_id=1, source_target_pairs={{0,32},{1,9},{2,34},{3,11},{4,36},{5,13},{6,38},{7,15},{8,40},{9,1... | collective-permute-start | bytes 3551240 | tf_op jit(solution)/shard_map/ppermute | solution.py:57
  17.0 2.1 %collective-permute-start.3 = (bf16[4624,128]{1,0:T(8,128)(2,1)S(1)}, bf16[4624,128]{1,0:T(8,128)(2,1)}, u32[]{:S(2)}, u32[]{:S(2)}) collective-permute-start(bf16[4624,128]{1,0:T(8,128)(2,1)S(1)} %constant_dynamic-update-slice_fusion.refs_1_.refs_3_), channel_id=1, source_target_pairs={{0,96},{1,25},{2,98},{3,27},{4,100},{5,29},{6,102},{7,31},{8,104},... | collective-permute-start | bytes 3551240 | tf_op jit(solution)/shard_map/ppermute | solution.py:57
  19.1 0.1 stack.23
  19.2 0.0 collective-permute-done.2.refs_2_
  19.2 0.7 slice_reduce_fusion
  19.9 0.1 stack.30
  20.0 1.7 %collective-permute-done.1.refs_1_ = bf16[272,1152]{1,0:T(8,128)(2,1)} collective-permute-done((bf16[272,1152]{1,0:T(8,128)(2,1)S(1)}, bf16[272,1152]{1,0:T(8,128)(2,1)}, u32[]{:S(2)}, u32[]{:S(2)}) %collective-permute-start.1) | collective-permute-done | bytes 626720 | tf_op jit(solution)/shard_map/ppermute | solution.py:57
  21.7 0.7 slice_reduce_fusion.1
  22.4 0.1 stack.29
  22.5 0.0 collective-permute-done.refs_0_
  22.5 0.7 slice_reduce_fusion.2
  23.2 0.1 stack.28
  23.3 0.4 compare_reduce_fusion
  23.7 0.1 reshape.70.flags
  23.8 12.9 %shard_map.92 = (f32[768,1024]{1,0:T(8,128)S(1)}, f32[768,128]{1,0:T(8,128)S(1)}) custom-call(s32[64]{0:T(128)S(1)} %reshape.70.flags, bf16[272,1152]{1,0:T(8,128)(2,1)} %collective-permute-done.refs_0_, bf16[272,1152]{1,0:T(8,128)(2,1)} %collective-permute-done.1.refs_1_, bf16[272,1152]{1,0:T(8,128)(2,1)} %collective-permute-done.2.refs_2_, ...), custom_call_target="tpu_custom_call" | custom-call | flops 4831838208 | bytes 6291456 | tf_op jit(solution)/shard_map/pallas_call | solution.py:249
  36.7 6.2 %collective-permute-start.5 = (bf16[4624,128]{1,0:T(8,128)(2,1)S(1)}, bf16[4624,128]{1,0:T(8,128)(2,1)S(1)}, u32[]{:S(2)}, u32[]{:S(2)}) collective-permute-start(bf16[4624,128]{1,0:T(8,128)(2,1)S(1)} %constant_dynamic-update-slice_fusion.refs_1_.refs_3_), channel_id=1, source_target_pairs={{0,64},{1,17},{2,66},{3,19},{4,68},{5,21},{6,70},{7,23},{8,72},{9,... | collective-permute-start | bytes 3551240 | tf_op jit(solution)/shard_map/ppermute | solution.py:57
  42.9 0.0 collective-permute-done.4.refs_4_.refs_2_
  42.9 0.0 collective-permute-done.3.refs_3_.refs_1_
  42.9 19.4 %shard_map.93 = (f32[768,1024]{1,0:T(8,128)S(1)}, f32[768,128]{1,0:T(8,128)S(1)}) custom-call(s32[64]{0:T(128)S(1)} %reshape.70.flags, bf16[272,1152]{1,0:T(8,128)(2,1)} %collective-permute-done.refs_0_, bf16[272,1152]{1,0:T(8,128)(2,1)} %collective-permute-done.1.refs_1_, bf16[272,1152]{1,0:T(8,128)(2,1)} %collective-permute-done.2.refs_2_, ...), custom_call_target="tpu_custom_call" | custom-call | flops 9663676416 | bytes 6291456 | tf_op jit(solution)/shard_map/pallas_call | solution.py:249
  62.4 0.0 collective-permute-done.5.refs_3_
  62.4 0.0 slice-start
  62.4 15.0 %shard_map.94 = (bf16[256,1152]{1,0:T(8,128)(2,1)S(1)}, bf16[256,1152]{1,0:T(8,128)(2,1)S(1)}, bf16[256,1152]{1,0:T(8,128)(2,1)S(1)}) custom-call(s32[64]{0:T(128)S(1)} %reshape.70.flags, bf16[272,1152]{1,0:T(8,128)(2,1)} %collective-permute-done.refs_0_, bf16[272,1152]{1,0:T(8,128)(2,1)} %collective-permute-done.1.refs_1_, ...), custom_call_target="tpu_custom_call" | custom-call | flops 4831838208 | bytes 6291456 | tf_op jit(solution)/shard_map/pallas_call | solution.py:249
  77.5 5.8 %collective-permute-start.6 = (bf16[256,1152]{1,0:T(8,128)(2,1)S(1)}, bf16[256,1152]{1,0:T(8,128)(2,1)S(1)}, u32[]{:S(2)}, u32[]{:S(2)}) collective-permute-start(bf16[256,1152]{1,0:T(8,128)(2,1)S(1)} %get-tuple-element.31), channel_id=1, source_target_pairs={{0,8},{1,33},{2,10},{3,35},{4,12},{5,37},{6,14},{7,39},{8,16},{9,4... | collective-permute-start | bytes 1769480 | tf_op jit(solution)/shard_map/ppermute | solution.py:57
  83.3 11.4 %collective-permute-start.8 = (bf16[256,1152]{1,0:T(8,128)(2,1)S(1)}, bf16[256,1152]{1,0:T(8,128)(2,1)S(1)}, u32[]{:S(2)}, u32[]{:S(2)}) collective-permute-start(bf16[256,1152]{1,0:T(8,128)(2,1)S(1)} %get-tuple-element.33), channel_id=1, source_target_pairs={{0,16},{1,65},{2,18},{3,67},{4,20},{5,69},{6,22},{7,71},{8,24},{9,... | collective-permute-start | bytes 1769480 | tf_op jit(solution)/shard_map/ppermute | solution.py:57
  94.7 7.6 %shard_map.95.refs_0_ = bf16[256,1152]{1,0:T(8,128)(2,1)S(1)} custom-call(s32[64]{0:T(128)S(1)} %reshape.70.flags, bf16[272,1152]{1,0:T(8,128)(2,1)S(1)} %fusion.4.refs_0_, bf16[4624,128]{1,0:T(8,128)(2,1)} %collective-permute-done.3.refs_3_.refs_1_, bf16[4624,128]{1,0:T(8,128)(2,1)S(1)} %collective-permute-done.4.refs_4_.refs_2_, ...), custom_call_target="tpu_custom_call" | custom-call | flops 4831838208 | bytes 2097152 | tf_op jit(solution)/shard_map/pallas_call | solution.py:249
  102.4 0.0 collective-permute-done.6.refs_1_
  102.4 4.8 %collective-permute-done.8.refs_3_ = bf16[256,1152]{1,0:T(8,128)(2,1)S(1)} collective-permute-done((bf16[256,1152]{1,0:T(8,128)(2,1)S(1)}, bf16[256,1152]{1,0:T(8,128)(2,1)S(1)}, u32[]{:S(2)}, u32[]{:S(2)}) %collective-permute-start.8) | collective-permute-done | bytes 589856 | tf_op jit(solution)/shard_map/ppermute | solution.py:57
  107.2 7.1 %shard_map.96 = (bf16[128,4096]{1,0:T(8,128)(2,1)S(1)}, bf16[128,4096]{1,0:T(8,128)(2,1)}, bf16[256,1024]{1,0:T(8,128)(2,1)S(1)}) custom-call(s32[1]{0:T(128)} %bitcast.core, bf16[256,1152]{1,0:T(8,128)(2,1)S(1)} %shard_map.95.refs_0_, bf16[256,1152]{1,0:T(8,128)(2,1)S(1)} %collective-permute-done.6.refs_1_, ...), custom_call_target="tpu_custom_call" | custom-call | flops 4294967296 | bytes 10485760 | tf_op jit(solution)/shard_map/pallas_call | solution.py:335
  114.3 4.5 %collective-permute-start.9 = (bf16[128,4096]{1,0:T(8,128)(2,1)}, bf16[128,4096]{1,0:T(8,128)(2,1)}, u32[]{:S(2)}, u32[]{:S(2)}) collective-permute-start(bf16[128,4096]{1,0:T(8,128)(2,1)} %get-tuple-element.37), channel_id=1, source_target_pairs={{0,1},{1,0},{2,3},{3,2},{4,5},{5,4},{6,7},{7,6},{8,9},{9,8},{10,11... | collective-permute-start | bytes 3145736 | tf_op jit(solution)/shard_map/ppermute | solution.py:57
  118.7 3.5 %shard_map.97 = (bf16[128,4096]{1,0:T(8,128)(2,1)S(1)}, bf16[128,4096]{1,0:T(8,128)(2,1)S(1)}) custom-call(s32[1]{0:T(128)} %bitcast.core, bf16[256,1024]{1,0:T(8,128)(2,1)S(1)} %get-tuple-element.38.refs_0_, bf16[1024,8192]{1,0:T(8,128)(2,1)S(1)} %bitcast.6), custom_call_target="tpu_custom_call" | custom-call | flops 4294967296 | bytes 10485760 | tf_op jit(solution)/shard_map/pallas_call | solution.py:335
  122.3 0.1 collective-permute-start.13
  122.5 1.3 add_convert_fusion.7
  123.8 1.3 collective-permute-start.10
  125.1 2.5 %collective-permute-start.12 = (bf16[32,4096]{1,0:T(8,128)(2,1)S(1)}, bf16[32,4096]{1,0:T(8,128)(2,1)S(1)}, u32[]{:S(2)}, u32[]{:S(2)}) collective-permute-start(bf16[32,4096]{1,0:T(8,128)(2,1)S(1)} %get-tuple-element.44), channel_id=1, source_target_pairs={{0,4},{1,5},{2,6},{3,7},{4,0},{5,1},{6,2},{7,3},{8,12},{9,13},{10,... | collective-permute-start | bytes 786440 | tf_op jit(solution)/shard_map/ppermute | solution.py:57
  127.6 1.1 collective-permute-start.11
  128.7 1.3 add_convert_fusion.3
  130.0 0.4 collective-permute-start.14
  130.4 0.9 collective-permute-start.16
  131.3 1.3 collective-permute-done.10
  132.6 1.3 collective-permute-start.15
  133.9 5.4 %collective-permute-done.12 = bf16[32,4096]{1,0:T(8,128)(2,1)S(1)} collective-permute-done((bf16[32,4096]{1,0:T(8,128)(2,1)S(1)}, bf16[32,4096]{1,0:T(8,128)(2,1)S(1)}, u32[]{:S(2)}, u32[]{:S(2)}) %collective-permute-start.12) | collective-permute-done | bytes 262176 | tf_op jit(solution)/shard_map/ppermute | solution.py:57
  139.2 1.1 add_convert_fusion.4
  140.4 3.9 %collective-permute-done.14 = bf16[32,4096]{1,0:T(8,128)(2,1)S(1)} collective-permute-done((bf16[32,4096]{1,0:T(8,128)(2,1)S(1)}, bf16[32,4096]{1,0:T(8,128)(2,1)S(1)}, u32[]{:S(2)}, u32[]{:S(2)}) %collective-permute-start.14) | collective-permute-done | bytes 262176 | tf_op jit(solution)/shard_map/ppermute | solution.py:57
  144.3 6.2 %collective-permute-done.16 = bf16[32,4096]{1,0:T(8,128)(2,1)S(1)} collective-permute-done((bf16[32,4096]{1,0:T(8,128)(2,1)S(1)}, bf16[32,4096]{1,0:T(8,128)(2,1)S(1)}, u32[]{:S(2)}, u32[]{:S(2)}) %collective-permute-start.16) | collective-permute-done | bytes 262176 | tf_op jit(solution)/shard_map/ppermute | solution.py:57
  150.5 0.0 collective-permute-done.15
  150.5 1.1 add_convert_fusion
  151.6 0.8 pad_maximum_fusion
  (35 shorter events, 0.2 us)
Async XLA Ops:
  0.0 9.5 %copy-start.2 = (bf16[2048,128]{1,0:T(8,128)(2,1)S(1)}, bf16[2048,128]{1,0:T(8,128)(2,1)}, u32[]{:S(2)}) copy-start(bf16[2048,128]{1,0:T(8,128)(2,1)} %param.13) | copy-start | bytes 1572868
  1.8 7.7 %copy-start.4 = (bf16[256,128]{1,0:T(8,128)(2,1)S(1)}, bf16[256,128]{1,0:T(8,128)(2,1)}, u32[]{:S(2)}) copy-start(bf16[256,128]{1,0:T(8,128)(2,1)} %param.10) | copy-start | bytes 196612
  1.8 7.8 %copy-start.3 = (bf16[2048,128]{1,0:T(8,128)(2,1)S(1)}, bf16[2048,128]{1,0:T(8,128)(2,1)}, u32[]{:S(2)}) copy-start(bf16[2048,128]{1,0:T(8,128)(2,1)} %param.14) | copy-start | bytes 1572868
  3.0 6.7 %copy-start.6 = (s32[4]{0:T(128)S(1)}, s32[4]{0:T(128)}, u32[]{:S(2)}) copy-start(s32[4]{0:T(128)} %constant.143.clone) | copy-start | bytes 52
  3.0 6.7 %copy-start.5 = (bf16[256,128]{1,0:T(8,128)(2,1)S(1)}, bf16[256,128]{1,0:T(8,128)(2,1)}, u32[]{:S(2)}) copy-start(bf16[256,128]{1,0:T(8,128)(2,1)} %param.11) | copy-start | bytes 196612
  3.0 16.2 %collective-permute-start.2 = (bf16[272,1152]{1,0:T(8,128)(2,1)S(1)}, bf16[272,1152]{1,0:T(8,128)(2,1)}, u32[]{:S(2)}, u32[]{:S(2)}) collective-permute-start(bf16[272,1152]{1,0:T(8,128)(2,1)S(1)} %fusion.4.refs_0_), channel_id=1, source_target_pairs={{0,16},{1,65},{2,18},{3,67},{4,20},{5,69},{6,22},{7,71},{8,24},{9,... | collective-permute-start | bytes 1880072 | tf_op jit(solution)/shard_map/ppermute | solution.py:57
  6.8 14.9 %collective-permute-start.1 = (bf16[272,1152]{1,0:T(8,128)(2,1)S(1)}, bf16[272,1152]{1,0:T(8,128)(2,1)}, u32[]{:S(2)}, u32[]{:S(2)}) collective-permute-start(bf16[272,1152]{1,0:T(8,128)(2,1)S(1)} %fusion.4.refs_0_), channel_id=1, source_target_pairs={{0,8},{1,33},{2,10},{3,35},{4,12},{5,37},{6,14},{7,39},{8,16},{9,4... | collective-permute-start | bytes 1880072 | tf_op jit(solution)/shard_map/ppermute | solution.py:57
  7.2 15.3 %collective-permute-start = (bf16[272,1152]{1,0:T(8,128)(2,1)S(1)}, bf16[272,1152]{1,0:T(8,128)(2,1)}, u32[]{:S(2)}, u32[]{:S(2)}) collective-permute-start(bf16[272,1152]{1,0:T(8,128)(2,1)S(1)} %fusion.4.refs_0_), channel_id=1, source_target_pairs={{0,24},{1,97},{2,26},{3,99},{4,28},{5,101},{6,30},{7,103},{8,0},{9... | collective-permute-start | bytes 1880072 | tf_op jit(solution)/shard_map/ppermute | solution.py:57
  14.4 1.0 copy-start
  15.4 27.6 %collective-permute-start.4 = (bf16[4624,128]{1,0:T(8,128)(2,1)S(1)}, bf16[4624,128]{1,0:T(8,128)(2,1)S(1)}, u32[]{:S(2)}, u32[]{:S(2)}) collective-permute-start(bf16[4624,128]{1,0:T(8,128)(2,1)S(1)} %constant_dynamic-update-slice_fusion.refs_1_.refs_3_), channel_id=1, source_target_pairs={{0,32},{1,9},{2,34},{3,11},{4,36},{5,13},{6,38},{7,15},{8,40},{9,1... | collective-permute-start | bytes 3551240 | tf_op jit(solution)/shard_map/ppermute | solution.py:57
  17.0 25.9 %collective-permute-start.3 = (bf16[4624,128]{1,0:T(8,128)(2,1)S(1)}, bf16[4624,128]{1,0:T(8,128)(2,1)}, u32[]{:S(2)}, u32[]{:S(2)}) collective-permute-start(bf16[4624,128]{1,0:T(8,128)(2,1)S(1)} %constant_dynamic-update-slice_fusion.refs_1_.refs_3_), channel_id=1, source_target_pairs={{0,96},{1,25},{2,98},{3,27},{4,100},{5,29},{6,102},{7,31},{8,104},... | collective-permute-start | bytes 3551240 | tf_op jit(solution)/shard_map/ppermute | solution.py:57
  36.7 25.6 %collective-permute-start.5 = (bf16[4624,128]{1,0:T(8,128)(2,1)S(1)}, bf16[4624,128]{1,0:T(8,128)(2,1)S(1)}, u32[]{:S(2)}, u32[]{:S(2)}) collective-permute-start(bf16[4624,128]{1,0:T(8,128)(2,1)S(1)} %constant_dynamic-update-slice_fusion.refs_1_.refs_3_), channel_id=1, source_target_pairs={{0,64},{1,17},{2,66},{3,19},{4,68},{5,21},{6,70},{7,23},{8,72},{9,... | collective-permute-start | bytes 3551240 | tf_op jit(solution)/shard_map/ppermute | solution.py:57
  62.4 32.3 %copy-start.1 = (f32[256,1024]{1,0:T(8,128)S(1)}, f32[256,1024]{1,0:T(8,128)}, u32[]{:S(2)}) copy-start(f32[256,1024]{1,0:T(8,128)} %copy-done) | copy-start | bytes 3145732
  62.4 44.7 %slice-start = ((s8[16777216]{0:T(1024)(128)(4,1)}), s8[4194304]{0:T(1024)(128)(4,1)S(1)}, s32[]{:S(2)}) async-start(s8[16777216]{0:T(1024)(128)(4,1)} %bitcast.5), calls=%async_computation | async-start | bytes 8388608
  62.4 44.7 %slice-start.1 = ((s8[16777216]{0:T(1024)(128)(4,1)}), s8[4194304]{0:T(1024)(128)(4,1)S(1)}, s32[]{:S(2)}) async-start(s8[16777216]{0:T(1024)(128)(4,1)} %bitcast.5), calls=%async_computation.1 | async-start | bytes 8388608
  77.5 24.9 %collective-permute-start.6 = (bf16[256,1152]{1,0:T(8,128)(2,1)S(1)}, bf16[256,1152]{1,0:T(8,128)(2,1)S(1)}, u32[]{:S(2)}, u32[]{:S(2)}) collective-permute-start(bf16[256,1152]{1,0:T(8,128)(2,1)S(1)} %get-tuple-element.31), channel_id=1, source_target_pairs={{0,8},{1,33},{2,10},{3,35},{4,12},{5,37},{6,14},{7,39},{8,16},{9,4... | collective-permute-start | bytes 1769480 | tf_op jit(solution)/shard_map/ppermute | solution.py:57
  83.3 23.9 %slice-start.2 = ((s8[16777216]{0:T(1024)(128)(4,1)}), s8[4194304]{0:T(1024)(128)(4,1)S(1)}, s32[]{:S(2)}) async-start(s8[16777216]{0:T(1024)(128)(4,1)} %bitcast.5), calls=%async_computation.2 | async-start | bytes 8388608
  83.3 19.1 %collective-permute-start.7 = (bf16[256,1152]{1,0:T(8,128)(2,1)S(1)}, bf16[256,1152]{1,0:T(8,128)(2,1)S(1)}, u32[]{:S(2)}, u32[]{:S(2)}) collective-permute-start(bf16[256,1152]{1,0:T(8,128)(2,1)S(1)} %get-tuple-element.32), channel_id=1, source_target_pairs={{0,24},{1,97},{2,26},{3,99},{4,28},{5,101},{6,30},{7,103},{8,0},{9... | collective-permute-start | bytes 1769480 | tf_op jit(solution)/shard_map/ppermute | solution.py:57
  83.3 23.9 %slice-start.3 = ((s8[16777216]{0:T(1024)(128)(4,1)}), s8[4194304]{0:T(1024)(128)(4,1)S(1)}, s32[]{:S(2)}) async-start(s8[16777216]{0:T(1024)(128)(4,1)} %bitcast.5), calls=%async_computation.3 | async-start | bytes 8388608
  83.3 23.8 %collective-permute-start.8 = (bf16[256,1152]{1,0:T(8,128)(2,1)S(1)}, bf16[256,1152]{1,0:T(8,128)(2,1)S(1)}, u32[]{:S(2)}, u32[]{:S(2)}) collective-permute-start(bf16[256,1152]{1,0:T(8,128)(2,1)S(1)} %get-tuple-element.33), channel_id=1, source_target_pairs={{0,16},{1,65},{2,18},{3,67},{4,20},{5,69},{6,22},{7,71},{8,24},{9,... | collective-permute-start | bytes 1769480 | tf_op jit(solution)/shard_map/ppermute | solution.py:57
  114.3 8.2 %collective-permute-start.9 = (bf16[128,4096]{1,0:T(8,128)(2,1)}, bf16[128,4096]{1,0:T(8,128)(2,1)}, u32[]{:S(2)}, u32[]{:S(2)}) collective-permute-start(bf16[128,4096]{1,0:T(8,128)(2,1)} %get-tuple-element.37), channel_id=1, source_target_pairs={{0,1},{1,0},{2,3},{3,2},{4,5},{5,4},{6,7},{7,6},{8,9},{9,8},{10,11... | collective-permute-start | bytes 3145736 | tf_op jit(solution)/shard_map/ppermute | solution.py:57
  122.3 6.4 %collective-permute-start.13 = (bf16[128,4096]{1,0:T(8,128)(2,1)S(1)}, bf16[128,4096]{1,0:T(8,128)(2,1)}, u32[]{:S(2)}, u32[]{:S(2)}) collective-permute-start(bf16[128,4096]{1,0:T(8,128)(2,1)S(1)} %get-tuple-element.40), channel_id=1, source_target_pairs={{0,1},{1,0},{2,3},{3,2},{4,5},{5,4},{6,7},{7,6},{8,9},{9,8},{10,11... | collective-permute-start | bytes 3145736 | tf_op jit(solution)/shard_map/ppermute | solution.py:57
  123.8 8.8 %collective-permute-start.10 = (bf16[32,4096]{1,0:T(8,128)(2,1)S(1)}, bf16[32,4096]{1,0:T(8,128)(2,1)S(1)}, u32[]{:S(2)}, u32[]{:S(2)}) collective-permute-start(bf16[32,4096]{1,0:T(8,128)(2,1)S(1)} %get-tuple-element.43), channel_id=1, source_target_pairs={{0,2},{1,3},{2,4},{3,5},{4,6},{5,7},{6,0},{7,1},{8,10},{9,11},{10,... | collective-permute-start | bytes 786440 | tf_op jit(solution)/shard_map/ppermute | solution.py:57
  125.1 14.1 %collective-permute-start.12 = (bf16[32,4096]{1,0:T(8,128)(2,1)S(1)}, bf16[32,4096]{1,0:T(8,128)(2,1)S(1)}, u32[]{:S(2)}, u32[]{:S(2)}) collective-permute-start(bf16[32,4096]{1,0:T(8,128)(2,1)S(1)} %get-tuple-element.44), channel_id=1, source_target_pairs={{0,4},{1,5},{2,6},{3,7},{4,0},{5,1},{6,2},{7,3},{8,12},{9,13},{10,... | collective-permute-start | bytes 786440 | tf_op jit(solution)/shard_map/ppermute | solution.py:57
  127.6 11.7 %collective-permute-start.11 = (bf16[32,4096]{1,0:T(8,128)(2,1)S(1)}, bf16[32,4096]{1,0:T(8,128)(2,1)S(1)}, u32[]{:S(2)}, u32[]{:S(2)}) collective-permute-start(bf16[32,4096]{1,0:T(8,128)(2,1)S(1)} %get-tuple-element.45), channel_id=1, source_target_pairs={{0,6},{1,7},{2,0},{3,1},{4,2},{5,3},{6,4},{7,5},{8,14},{9,15},{10,... | collective-permute-start | bytes 786440 | tf_op jit(solution)/shard_map/ppermute | solution.py:57
  130.0 14.3 %collective-permute-start.14 = (bf16[32,4096]{1,0:T(8,128)(2,1)S(1)}, bf16[32,4096]{1,0:T(8,128)(2,1)S(1)}, u32[]{:S(2)}, u32[]{:S(2)}) collective-permute-start(bf16[32,4096]{1,0:T(8,128)(2,1)S(1)} %get-tuple-element.46), channel_id=1, source_target_pairs={{0,2},{1,3},{2,4},{3,5},{4,6},{5,7},{6,0},{7,1},{8,10},{9,11},{10,... | collective-permute-start | bytes 786440 | tf_op jit(solution)/shard_map/ppermute | solution.py:57
  130.4 20.1 %collective-permute-start.16 = (bf16[32,4096]{1,0:T(8,128)(2,1)S(1)}, bf16[32,4096]{1,0:T(8,128)(2,1)S(1)}, u32[]{:S(2)}, u32[]{:S(2)}) collective-permute-start(bf16[32,4096]{1,0:T(8,128)(2,1)S(1)} %get-tuple-element.47), channel_id=1, source_target_pairs={{0,4},{1,5},{2,6},{3,7},{4,0},{5,1},{6,2},{7,3},{8,12},{9,13},{10,... | collective-permute-start | bytes 786440 | tf_op jit(solution)/shard_map/ppermute | solution.py:57
  132.6 17.9 %collective-permute-start.15 = (bf16[32,4096]{1,0:T(8,128)(2,1)S(1)}, bf16[32,4096]{1,0:T(8,128)(2,1)S(1)}, u32[]{:S(2)}, u32[]{:S(2)}) collective-permute-start(bf16[32,4096]{1,0:T(8,128)(2,1)S(1)} %get-tuple-element.48), channel_id=1, source_target_pairs={{0,6},{1,7},{2,0},{3,1},{4,2},{5,3},{6,4},{7,5},{8,14},{9,15},{10,... | collective-permute-start | bytes 786440 | tf_op jit(solution)/shard_map/ppermute | solution.py:57
where the time goes:
time: 153 us; the launch traced here: 152 us
  Pallas kernels  70 us (46%)
  starting transfers between devices  45.6 us (30%)
  waiting for transfers between devices  23.3 us (15%)
  other arithmetic  8.98 us (6%)
  local copies, waits for them, and re-layouts  4.11 us (3%)
    pallas_call x5, Pallas kernels, attend(): pl.pallas_call(functools.partial(attend_kernel, n_home, n_kv, bases, stat...  59.4 us
    ppermute x17, starting transfers between devices, move(): return lax.ppermute(value, AXES, pairs(kind, shift))  45.6 us
    ppermute x17, waiting for transfers between devices, move(): return lax.ppermute(value, AXES, pairs(kind, shift))  23.3 us
    pallas_call x2, Pallas kernels, project(): pl.pallas_call(functools.partial(project_kernel, 0 if merged else len(par...  10.7 us
  transfers between devices with their start and end apart: 17, of which 6 were waited for; matrix products, arithmetic and copies ran while one was open for 5% of the time, Pallas kernels for 31%

commit v1 on v0

--- a/solution.py
+++ b/solution.py
@@ -66,8 +66,9 @@
     return lax.dot_general(a, b, (((1,), (1,)), ((), ())), preferred_element_type=F32)
 
 
-def attend_kernel(n_home, n_kv, bases, resume, final, flags, *refs):
+def attend_kernel(n_home, n_kv, first_kv, resume, final, *refs):
     refs = list(refs)
+    flags = [refs.pop(0) for _ in range(n_home)]
     q_refs = [refs.pop(0) for _ in range(n_home)]
     kv_refs = [refs.pop(0) for _ in range(n_kv)]
     if resume:
@@ -75,8 +76,8 @@
     if final:
         outs = [refs.pop(0) for _ in range(n_home)]
     else:
-        acc_out, ml_out = refs.pop(0), refs.pop(0)
-    k_scr, v_scr, meta_scr, q_scr, qpos_scr, m_scr, acc_scr, sems = refs
+        acc_out, ml_out = refs[-10:-8]
+    k_scr, v_scr, meta_scr, q_scr, qpos_scr, m_scr, acc_scr, sems = refs[-8:]
     home_id = pl.program_id(0)
     tokens = NEW
     blocks = NEW // QB
@@ -169,9 +170,12 @@
 
     def cached(item, carry):
         j, block = item // blocks, item % blocks
-        at = ((bases[0] + home_id) * SIDE + bases[1] + j) * blocks + block
-
-        @pl.when(flags[at] > 0)
+        at = (first_kv + j) * blocks + block
+        hit = flags[0][at]
+        for home in range(1, n_home):
+            hit = jnp.where(home_id == home, flags[home][at], hit)
+
+        @pl.when(hit > 0)
         def _():
             rows = pl.ds(pl.multiple_of(block * QB, QB), QB)
             for first in range(0, GROUP, per_pass):
@@ -227,12 +231,14 @@
             pl.when(home_id == home)(functools.partial(emit, outs[home]))
 
 
-def attend(flags, q_list, kv_list, bases, state=None, final=False):
+def attend(flags, q_list, kv_list, first_kv, state=None, final=False, into=None):
     n_home, n_kv = len(q_list), len(kv_list)
-    fixed = lambda shape: pl.BlockSpec(shape, lambda i, f: (0,) * len(shape))
-    turn = lambda width: pl.BlockSpec((NEW, width), lambda i, f: (i, 0))
-    in_specs = [fixed((NEW, SEND_W))] * n_home + [pl.BlockSpec(memory_space=pl.ANY)] * n_kv
+    fixed = lambda shape: pl.BlockSpec(shape, lambda i, *f: (0,) * len(shape))
+    turn = lambda width, at=0: pl.BlockSpec((NEW, width), lambda i, *f: (i + at, 0))
+    anywhere = pl.BlockSpec(memory_space=pl.ANY)
+    in_specs = [fixed((NEW, SEND_W))] * n_home + [anywhere] * n_kv
     args = list(q_list) + list(kv_list)
+    aliases = {}
     if state is not None:
         in_specs += [turn(QW), turn(HD)]
         args += list(state)
@@ -240,17 +246,22 @@
         out_shape = [jax.ShapeDtypeStruct((NEW, RET_W), BF)] * n_home
         out_specs = [fixed((NEW, RET_W))] * n_home
     else:
+        places, at, target = into or (n_home, 0, None)
         out_shape = [
-            jax.ShapeDtypeStruct((n_home * NEW, QW), F32),
-            jax.ShapeDtypeStruct((n_home * NEW, HD), F32),
+            jax.ShapeDtypeStruct((places * NEW, QW), F32),
+            jax.ShapeDtypeStruct((places * NEW, HD), F32),
         ]
-        out_specs = [turn(QW), turn(HD)]
+        out_specs = [turn(QW, at), turn(HD, at)]
+        if target is not None:
+            aliases = {n_home + len(args): 0, n_home + len(args) + 1: 1}
+            in_specs += [anywhere, anywhere]
+            args += list(target)
     work = n_home * n_kv * NEW * GROUP * (SEG // 4 + NEW)
     return pl.pallas_call(
-        functools.partial(attend_kernel, n_home, n_kv, bases, state is not None, final),
+        functools.partial(attend_kernel, n_home, n_kv, first_kv, state is not None, final),
         out_shape=out_shape,
         grid_spec=pltpu.PrefetchScalarGridSpec(
-            num_scalar_prefetch=1,
+            num_scalar_prefetch=n_home,
             grid=(n_home,),
             in_specs=in_specs,
             out_specs=out_specs,
@@ -265,13 +276,14 @@
                 pltpu.SemaphoreType.DMA((n_kv, 3)),
             ],
         ),
+        input_output_aliases=aliases,
         compiler_params=pltpu.CompilerParams(vmem_limit_bytes=24 << 20),
         cost_estimate=pl.CostEstimate(
             flops=work * HD * 4 * 2,
             bytes_accessed=n_home * NEW * QW * 8,
             transcendentals=work,
         ),
-    )(flags, *args)
+    )(*flags, *args)
 
 
 def project_kernel(n_parts, core, *refs):
@@ -293,31 +305,31 @@
 
 
 def merge(core, parts, att):
-    for t in range(NEW // PIECE):
-        rows = slice(t * PIECE, (t + 1) * PIECE)
-        logs = []
-        for part in parts:
-            packed = part[rows, QW:].astype(F32)
-            logs.append(
-                packed[:, :GROUP]
-                + packed[:, GROUP : 2 * GROUP]
-                + packed[:, 2 * GROUP : 3 * GROUP]
-            )
-        top = functools.reduce(jnp.maximum, logs)
-        shares = [jnp.exp(log - top) for log in logs]
-        total = functools.reduce(jnp.add, shares)
-        shares = [share / total for share in shares]
-        away = jnp.where(core[0] == t % 2, 0, NEW // 2)
-        at = pl.multiple_of(away + (t // 2) * PIECE, PIECE)
-        for h in range(GROUP):
-            mixed = functools.reduce(
-                jnp.add,
-                [
-                    share[:, h : h + 1] * part[rows, h * HD : (h + 1) * HD].astype(F32)
-                    for share, part in zip(shares, parts)
-                ],
-            )
-            att[pl.ds(at, PIECE), h * HD : (h + 1) * HD] = mixed.astype(BF)
+    logs = []
+    for part in parts:
+        packed = part[:, QW:].astype(F32)
+        logs.append(
+            packed
+            + pltpu.roll(packed, HD - GROUP, axis=1)
+            + pltpu.roll(packed, HD - 2 * GROUP, axis=1)
+        )
+    top = functools.reduce(jnp.maximum, logs)
+    shares = [jnp.exp(log - top) for log in logs]
+    inverse = 1.0 / functools.reduce(jnp.add, shares)
+    shares = [share * inverse for share in shares]
+    for h in range(GROUP):
+        cols = slice(h * HD, (h + 1) * HD)
+        mixed = functools.reduce(
+            jnp.add,
+            [
+                share[:, h : h + 1] * part[:, cols].astype(F32)
+                for share, part in zip(shares, parts)
+            ],
+        ).astype(BF)
+        for t in range(NEW // PIECE):
+            away = jnp.where(core[0] == t % 2, 0, NEW // 2)
+            at = pl.multiple_of(away + (t // 2) * PIECE, PIECE)
+            att[pl.ds(at, PIECE), cols] = mixed[t * PIECE : (t + 1) * PIECE]
 
 
 def project(core, parts, weight, column, columns):
@@ -383,33 +395,42 @@
     along_z = y * SIDE + (z + steps) % SIDE
     segments = jnp.where(core == 0, along_y, along_z).astype(F32)
 
-    def flags_of(rows):
-        named = rows.astype(F32).reshape(-1, 1, NEW // QB, picks.shape[0] * QB // NEW)
-        hits = jnp.any(named == segments[None, :, None, None], axis=-1)
-        return hits.astype(jnp.int32).reshape(-1)
-
-    def state_of(flags, homes, kvs, state=None, final=False):
+    def flags_of(row):
+        named = row.astype(F32).reshape(1, NEW // QB, -1)
+        hits = named == segments[:, None, None]
+        return jnp.sum(hits.astype(jnp.int32), axis=-1).reshape(-1)
+
+    flags = {0: flags_of(picks)}
+
+    def read_flags(offsets, done):
+        for o in offsets:
+            flags[o] = flags_of(after(q_at[o][NEW, : picks.shape[0]], *done))
+
+    def run(homes, kvs, state=None, final=False, into=None):
+        offsets = [order[n] for n in homes]
         return attend(
-            flags,
-            [q_at[order[n]] for n in homes],
+            [flags[o] for o in offsets],
+            [q_at[o] for o in offsets],
             [kv_at[order[n]] for n in kvs],
-            (homes[0], kvs[0]),
+            kvs[0],
             state,
             final,
+            into,
         )
 
-    away, others = (1, 2, 3), (1, 2, 3)
-    own_state = state_of(flags_of(picks[None]), (0,), (0,))
+    own_state = run((0,), (0,))
     for shift in (1, 3):
         kv_at[-shift % SIDE] = move(after(kv_own, *own_state), "k", shift)
-    flags = flags_of(jnp.stack([q_at[o][NEW, : picks.shape[0]] for o in order]))
-    state = state_of(flags, away, (0,))
+    read_flags((1, 3), own_state)
+    state = run((1, 2), (0,), into=(3, 0, None))
+    read_flags((2,), state)
+    state = run((3,), (0,), into=(3, 2, state))
     kv_at[2] = move(after(kv_own, *state), "k", 2)
-    state = state_of(flags, away, (1, 2), state)
-    partials = state_of(flags, away, (3,), state, True)
-    backs = [move(part, "q", order[n]) for n, part in zip(away, partials)]
+    state = run((1, 2, 3), (1, 2), state)
+    partials = run((1, 2, 3), (3,), state, True)
+    backs = [move(part, "q", order[n]) for n, part in zip((1, 2, 3), partials)]
     own_state = [after(value, *partials) for value in own_state]
-    mine = state_of(flags, (0,), others, own_state, True)
+    mine = run((0,), (1, 2, 3), own_state, True)
 
     core_id = core.reshape(1)
     keep0, send0, att = project(core_id, [*mine, *backs], out_weight, 0, 2)
@@ -417,20 +438,21 @@
     keep1, send1 = project(core_id, [att], out_weight, 1, 2)
     other1 = move(send1, "c", 0)
 
-    def finish(keep, other):
+    def finish(keep, other, way):
         def group(shift):
             at = ((x + shift) % XN) * PIECE
             return lax.dynamic_slice_in_dim(keep, at, PIECE, 0).astype(
                 F32
             ) + lax.dynamic_slice_in_dim(other, at, PIECE, 0).astype(F32)
 
-        arrived = [move(group(shift).astype(BF), "x", shift) for shift in (1, 3, 2)]
-        result = group(0)
-        for value in arrived:
-            result = result + value.astype(F32)
-        return result.astype(BF)
-
-    return jnp.concatenate([finish(keep0, other0), finish(keep1, other1)], axis=1)
+        back = -way % XN
+        relay = move(group(2).astype(BF), "x", way)
+        direct = move(group(back).astype(BF), "x", back)
+        joined = (group(way) + relay.astype(F32)).astype(BF)
+        joint = move(joined, "x", way)
+        return (group(0) + direct.astype(F32) + joint.astype(F32)).astype(BF)
+
+    return jnp.concatenate([finish(keep0, other0, 1), finish(keep1, other1, 3)], axis=1)
 
 
 def solution(mesh):

time: 153 us -> 159 us (1.039)
  local copies, waits for them, and re-layouts: 4.11 us -> 14.7 us
  waiting for transfers between devices: 23.3 us -> 17.2 us
  other arithmetic: 8.98 us -> 10.8 us
  starting transfers between devices: 45.6 us -> 44 us
    unnamed x26 -> x42, local copies, waits for them, and re-layouts: 1.15 us -> 11.7 us
    ppermute x17, waiting for transfers between devices: 23.3 us -> 17.2 us  [move(): return lax.ppermute(value, AXES, pairs(kind, shift))]
    slice x4 -> x0, local copies, waits for them, and re-layouts: 2.09 us -> none  [per_device(): flags = flags_of(jnp.stack([q_at[o][NEW, :picks.shape[0]] for o in order]))]
    squeeze x0 -> x3, local copies, waits for them, and re-layouts: none -> 2.05 us  [read_flags(): flags[o] = flags_of(after(q_at[o][NEW, :picks.shape[0]], *done))]
    convert_element_type x8 -> x7, other arithmetic: 5.58 us -> 7.29 us  [the longest x2 2.32 us: finish(): direct = move(group(back).astype(BF), 'x', back)]
    pallas_call x5 -> x6, Pallas kernels: 59.4 us -> 61.1 us  [attend(): pl.pallas_call(functools.partial(attend_kernel, n_home, n_kv, first_kv, s...]
    ppermute x17, starting transfers between devices: 45.6 us -> 44 us  [move(): return lax.ppermute(value, AXES, pairs(kind, shift))]
  transfers between devices with their start and end apart: 17 -> 17, of which waited for: 6 -> 6; matrix products, arithmetic and copies ran while one was open for 5% -> 6% of each run, Pallas kernels for 31% -> 31%
where the time goes in v1:
time: 159 us; the launch traced here: 157 us
  Pallas kernels  70.4 us (44%)
  starting transfers between devices  44 us (28%)
  waiting for transfers between devices  17.2 us (11%)
  local copies, waits for them, and re-layouts  14.7 us (9%)
  other arithmetic  10.8 us (7%)
    pallas_call x6, Pallas kernels, attend(): pl.pallas_call(functools.partial(attend_kernel, n_home, n_kv, first_kv, s...  61.1 us
    ppermute x17, starting transfers between devices, move(): return lax.ppermute(value, AXES, pairs(kind, shift))  44 us
    ppermute x17, waiting for transfers between devices, move(): return lax.ppermute(value, AXES, pairs(kind, shift))  17.2 us
    unnamed x42, local copies, waits for them, and re-layouts  11.7 us
    pallas_call x2, Pallas kernels, project(): pl.pallas_call(functools.partial(project_kernel, 0 if merged else len(par...  9.32 us
  transfers between devices with their start and end apart: 17, of which 6 were waited for; matrix products, arithmetic and copies ran while one was open for 6% of the time, Pallas kernels for 31%

profile of v1, /device:TPU:1, one launch (start us, length us, event | category | flops | bytes accessed | tf_op | source)
XLA Modules:
  0.0 157.4 jit_solution(13606720042966635911)
XLA Ops:
  0.0 0.8 and_select_fusion.3
  0.8 0.7 fusion.12
  1.4 0.1 convert_element_type.139
  1.5 0.1 reshape.37
  1.6 0.1 copy.21
  1.8 1.2 fusion.4.refs_1_
  3.0 2.2 %collective-permute-start.4 = (bf16[272,1152]{1,0:T(8,128)(2,1)S(1)}, bf16[272,1152]{1,0:T(8,128)(2,1)}, u32[]{:S(2)}, u32[]{:S(2)}) collective-permute-start(bf16[272,1152]{1,0:T(8,128)(2,1)S(1)} %fusion.4.refs_1_), channel_id=1, source_target_pairs={{0,8},{1,33},{2,10},{3,35},{4,12},{5,37},{6,14},{7,39},{8,16},{9,4... | collective-permute-start | bytes 1880072 | tf_op jit(solution)/shard_map/ppermute | solution.py:57
  5.2 1.5 collective-permute-start.3
  6.7 1.6 collective-permute-start.2
  8.4 0.2 convert_reduce_fusion.3
  8.7 0.1 reshape.36.refs_0_
  8.8 4.3 %shard_map.91 = (f32[256,1024]{1,0:T(8,128)S(1)}, f32[256,128]{1,0:T(8,128)S(1)}) custom-call(s32[16]{0:T(128)S(1)} %reshape.36.refs_0_, bf16[272,1152]{1,0:T(8,128)(2,1)S(1)} %fusion.4.refs_1_, bf16[4624,128]{1,0:T(8,128)(2,1)S(1)} %constant_dynamic-update-slice_fusion.refs_2_.refs_4_), custom_call_target="tpu_custom_call" | custom-call | flops 1610612736 | bytes 2097152 | tf_op jit(solution)/shard_map/pallas_call | solution.py:260
  13.2 1.0 copy-done.8
  14.2 1.6 %collective-permute-start.1 = (bf16[4624,128]{1,0:T(8,128)(2,1)S(1)}, bf16[4624,128]{1,0:T(8,128)(2,1)S(1)}, u32[]{:S(2)}, u32[]{:S(2)}) collective-permute-start(bf16[4624,128]{1,0:T(8,128)(2,1)S(1)} %constant_dynamic-update-slice_fusion.refs_2_.refs_4_), channel_id=1, source_target_pairs={{0,32},{1,9},{2,34},{3,11},{4,36},{5,13},{6,38},{7,15},{8,40},{9,1... | collective-permute-start | bytes 3551240 | tf_op jit(solution)/shard_map/ppermute | solution.py:57
  15.8 2.1 %collective-permute-start = (bf16[4624,128]{1,0:T(8,128)(2,1)S(1)}, bf16[4624,128]{1,0:T(8,128)(2,1)}, u32[]{:S(2)}, u32[]{:S(2)}) collective-permute-start(bf16[4624,128]{1,0:T(8,128)(2,1)S(1)} %constant_dynamic-update-slice_fusion.refs_2_.refs_4_), channel_id=1, source_target_pairs={{0,96},{1,25},{2,98},{3,27},{4,100},{5,29},{6,102},{7,31},{8,104},... | collective-permute-start | bytes 3551240 | tf_op jit(solution)/shard_map/ppermute | solution.py:57
  17.9 0.7 slice_bitcast_fusion
  18.6 1.9 %collective-permute-done.3.refs_2_.refs_3_ = bf16[272,1152]{1,0:T(8,128)(2,1)} collective-permute-done((bf16[272,1152]{1,0:T(8,128)(2,1)S(1)}, bf16[272,1152]{1,0:T(8,128)(2,1)}, u32[]{:S(2)}, u32[]{:S(2)}) %collective-permute-start.3) | collective-permute-done | bytes 626720 | tf_op jit(solution)/shard_map/ppermute | solution.py:57
  20.5 0.7 slice_bitcast_fusion.1
  21.2 0.1 reshape.41
  21.3 0.1 reshape.42
  21.4 0.3 convert_reduce_fusion.1
  21.7 0.1 reshape.39.refs_1_
  21.7 0.1 reshape.38.refs_0_
  21.8 0.7 collective-permute-done.2.refs_1_.refs_5_
  22.6 0.7 slice_bitcast_fusion.2
  23.3 9.2 %shard_map.92 = (f32[768,1024]{1,0:T(8,128)S(1)}, f32[768,128]{1,0:T(8,128)S(1)}) custom-call(s32[16]{0:T(128)S(1)} %reshape.38.refs_0_, s32[16]{0:T(128)S(1)} %reshape.39.refs_1_, bf16[272,1152]{1,0:T(8,128)(2,1)} %collective-permute-done.3.refs_2_.refs_3_, bf16[272,1152]{1,0:T(8,128)(2,1)} %collective-permute-done.4.refs_3_.refs_4_, ...), custom_call_target="tpu_custom_call" | custom-call | flops 3221225472 | bytes 4194304 | tf_op jit(solution)/shard_map/pallas_call | solution.py:260
  32.4 1.6 %copy-done = f32[768,1024]{1,0:T(8,128)} copy-done((f32[768,1024]{1,0:T(8,128)}, f32[768,1024]{1,0:T(8,128)S(1)}, u32[]{:S(2)}) %copy-start) | copy-done | bytes 3145752
  34.1 0.7 copy-done.4
  34.8 0.1 reshape.43
  34.9 0.2 convert_reduce_fusion
  35.1 0.1 reshape.40.refs_0_.refs_2_
  35.2 1.9 %copy-done.1 = f32[768,1024]{1,0:T(8,128)S(1)} copy-done((f32[768,1024]{1,0:T(8,128)S(1)}, f32[768,1024]{1,0:T(8,128)}, u32[]{:S(2)}) %copy-start.1) | copy-done | bytes 3145752
  37.1 1.0 copy-done.5
  38.1 5.4 %shard_map.93 = (f32[768,1024]{1,0:T(8,128)S(1)}, f32[768,128]{1,0:T(8,128)S(1)}) custom-call(s32[16]{0:T(128)S(1)} %reshape.40.refs_0_.refs_2_, bf16[272,1152]{1,0:T(8,128)(2,1)} %collective-permute-done.2.refs_1_.refs_5_, bf16[4624,128]{1,0:T(8,128)(2,1)S(1)} %constant_dynamic-update-slice_fusion.refs_2_.refs_4_, ...), custom_call_target="tpu_custom_call", output_to_operand_aliasing={{0}: (3, {}), {1}: (4, {})} | custom-call | flops 1610612736 | bytes 2097152 | tf_op jit(solution)/shard_map/pallas_call | solution.py:260
  43.5 1.6 %copy-done.2 = f32[768,1024]{1,0:T(8,128)} copy-done((f32[768,1024]{1,0:T(8,128)}, f32[768,1024]{1,0:T(8,128)S(1)}, u32[]{:S(2)}) %copy-start.2) | copy-done | bytes 3145752
  45.1 0.7 copy-done.6
  45.9 3.8 %collective-permute-start.5 = (bf16[4624,128]{1,0:T(8,128)(2,1)S(1)}, bf16[4624,128]{1,0:T(8,128)(2,1)S(1)}, u32[]{:S(2)}, u32[]{:S(2)}) collective-permute-start(bf16[4624,128]{1,0:T(8,128)(2,1)S(1)} %constant_dynamic-update-slice_fusion.refs_2_.refs_4_), channel_id=1, source_target_pairs={{0,64},{1,17},{2,66},{3,19},{4,68},{5,21},{6,70},{7,23},{8,72},{9,... | collective-permute-start | bytes 3551240 | tf_op jit(solution)/shard_map/ppermute | solution.py:57
  49.7 1.9 %copy-done.3 = f32[768,1024]{1,0:T(8,128)S(1)} copy-done((f32[768,1024]{1,0:T(8,128)S(1)}, f32[768,1024]{1,0:T(8,128)}, u32[]{:S(2)}) %copy-start.3) | copy-done | bytes 3145752
  51.6 1.0 copy-done.7
  52.6 19.5 %shard_map.94 = (f32[768,1024]{1,0:T(8,128)S(1)}, f32[768,128]{1,0:T(8,128)S(1)}) custom-call(s32[16]{0:T(128)S(1)} %reshape.38.refs_0_, s32[16]{0:T(128)S(1)} %reshape.39.refs_1_, s32[16]{0:T(128)S(1)} %reshape.40.refs_0_.refs_2_, bf16[272,1152]{1,0:T(8,128)(2,1)} %collective-permute-done.3.refs_2_.refs_3_, ...), custom_call_target="tpu_custom_call" | custom-call | flops 9663676416 | bytes 6291456 | tf_op jit(solution)/shard_map/pallas_call | solution.py:260
  72.1 15.1 %shard_map.95 = (bf16[256,1152]{1,0:T(8,128)(2,1)S(1)}, bf16[256,1152]{1,0:T(8,128)(2,1)S(1)}, bf16[256,1152]{1,0:T(8,128)(2,1)S(1)}) custom-call(s32[16]{0:T(128)S(1)} %reshape.38.refs_0_, s32[16]{0:T(128)S(1)} %reshape.39.refs_1_, s32[16]{0:T(128)S(1)} %reshape.40.refs_0_.refs_2_, bf16[272,1152]{1,0:T(8,128)(2,1)} %collective-permute-done.3.refs_2_.refs_3_, ...), custom_call_target="tpu_custom_call" | custom-call | flops 4831838208 | bytes 6291456 | tf_op jit(solution)/shard_map/pallas_call | solution.py:260
  87.2 4.3 %collective-permute-start.6 = (bf16[256,1152]{1,0:T(8,128)(2,1)S(1)}, bf16[256,1152]{1,0:T(8,128)(2,1)S(1)}, u32[]{:S(2)}, u32[]{:S(2)}) collective-permute-start(bf16[256,1152]{1,0:T(8,128)(2,1)S(1)} %get-tuple-element.41), channel_id=1, source_target_pairs={{0,8},{1,33},{2,10},{3,35},{4,12},{5,37},{6,14},{7,39},{8,16},{9,4... | collective-permute-start | bytes 1769480 | tf_op jit(solution)/shard_map/ppermute | solution.py:57
  91.5 1.7 %collective-permute-start.7 = (bf16[256,1152]{1,0:T(8,128)(2,1)S(1)}, bf16[256,1152]{1,0:T(8,128)(2,1)S(1)}, u32[]{:S(2)}, u32[]{:S(2)}) collective-permute-start(bf16[256,1152]{1,0:T(8,128)(2,1)S(1)} %get-tuple-element.42), channel_id=1, source_target_pairs={{0,24},{1,97},{2,26},{3,99},{4,28},{5,101},{6,30},{7,103},{8,0},{9... | collective-permute-start | bytes 1769480 | tf_op jit(solution)/shard_map/ppermute | solution.py:57
  93.2 12.0 %collective-permute-start.8 = (bf16[256,1152]{1,0:T(8,128)(2,1)S(1)}, bf16[256,1152]{1,0:T(8,128)(2,1)S(1)}, u32[]{:S(2)}, u32[]{:S(2)}) collective-permute-start(bf16[256,1152]{1,0:T(8,128)(2,1)S(1)} %get-tuple-element.43), channel_id=1, source_target_pairs={{0,16},{1,65},{2,18},{3,67},{4,20},{5,69},{6,22},{7,71},{8,24},{9,... | collective-permute-start | bytes 1769480 | tf_op jit(solution)/shard_map/ppermute | solution.py:57
  105.2 7.6 %shard_map.96.refs_0_ = bf16[256,1152]{1,0:T(8,128)(2,1)S(1)} custom-call(s32[16]{0:T(128)S(1)} %reshape.36.refs_0_, bf16[272,1152]{1,0:T(8,128)(2,1)S(1)} %fusion.4.refs_1_, bf16[4624,128]{1,0:T(8,128)(2,1)} %collective-permute-done.refs_6_.refs_2_, bf16[4624,128]{1,0:T(8,128)(2,1)S(1)} %collective-permute-done.1.refs_7_.refs_3_, ...), custom_call_target="tpu_custom_call" | custom-call | flops 4831838208 | bytes 2097152 | tf_op jit(solution)/shard_map/pallas_call | solution.py:260
  112.9 4.8 %collective-permute-done.8.refs_3_ = bf16[256,1152]{1,0:T(8,128)(2,1)S(1)} collective-permute-done((bf16[256,1152]{1,0:T(8,128)(2,1)S(1)}, bf16[256,1152]{1,0:T(8,128)(2,1)S(1)}, u32[]{:S(2)}, u32[]{:S(2)}) %collective-permute-start.8) | collective-permute-done | bytes 589856 | tf_op jit(solution)/shard_map/ppermute | solution.py:57
  117.6 5.8 %shard_map.97 = (bf16[128,4096]{1,0:T(8,128)(2,1)S(1)}, bf16[128,4096]{1,0:T(8,128)(2,1)}, bf16[256,1024]{1,0:T(8,128)(2,1)S(1)}) custom-call(s32[1]{0:T(128)} %bitcast.core, bf16[256,1152]{1,0:T(8,128)(2,1)S(1)} %shard_map.96.refs_0_, bf16[256,1152]{1,0:T(8,128)(2,1)S(1)} %collective-permute-done.6.refs_1_, ...), custom_call_target="tpu_custom_call" | custom-call | flops 4294967296 | bytes 10485760 | tf_op jit(solution)/shard_map/pallas_call | solution.py:347
  123.4 4.1 %collective-permute-start.9 = (bf16[128,4096]{1,0:T(8,128)(2,1)}, bf16[128,4096]{1,0:T(8,128)(2,1)}, u32[]{:S(2)}, u32[]{:S(2)}) collective-permute-start(bf16[128,4096]{1,0:T(8,128)(2,1)} %get-tuple-element.47), channel_id=1, source_target_pairs={{0,1},{1,0},{2,3},{3,2},{4,5},{5,4},{6,7},{7,6},{8,9},{9,8},{10,11... | collective-permute-start | bytes 3145736 | tf_op jit(solution)/shard_map/ppermute | solution.py:57
  127.5 3.5 %shard_map.98 = (bf16[128,4096]{1,0:T(8,128)(2,1)S(1)}, bf16[128,4096]{1,0:T(8,128)(2,1)S(1)}) custom-call(s32[1]{0:T(128)} %bitcast.core, bf16[256,1024]{1,0:T(8,128)(2,1)S(1)} %get-tuple-element.48.refs_0_, bf16[1024,8192]{1,0:T(8,128)(2,1)S(1)} %bitcast.12), custom_call_target="tpu_custom_call" | custom-call | flops 4294967296 | bytes 10485760 | tf_op jit(solution)/shard_map/pallas_call | solution.py:347
  131.1 0.1 collective-permute-start.13
  131.3 1.2 add_convert_fusion.7
  132.4 2.5 %collective-permute-start.10 = (bf16[32,4096]{1,0:T(8,128)(2,1)S(1)}, bf16[32,4096]{1,0:T(8,128)(2,1)S(1)}, u32[]{:S(2)}, u32[]{:S(2)}) collective-permute-start(bf16[32,4096]{1,0:T(8,128)(2,1)S(1)} %get-tuple-element.55), channel_id=1, source_target_pairs={{0,6},{1,7},{2,0},{3,1},{4,2},{5,3},{6,4},{7,5},{8,14},{9,15},{10,... | collective-permute-start | bytes 786440 | tf_op jit(solution)/shard_map/ppermute | solution.py:57
  135.0 1.2 add_convert_fusion.3
  136.1 0.3 collective-permute-start.14
  136.4 2.6 %collective-permute-start.15 = (bf16[32,4096]{1,0:T(8,128)(2,1)S(1)}, bf16[32,4096]{1,0:T(8,128)(2,1)S(1)}, u32[]{:S(2)}, u32[]{:S(2)}) collective-permute-start(bf16[32,4096]{1,0:T(8,128)(2,1)S(1)} %get-tuple-element.58), channel_id=1, source_target_pairs={{0,6},{1,7},{2,0},{3,1},{4,2},{5,3},{6,4},{7,5},{8,14},{9,15},{10,... | collective-permute-start | bytes 786440 | tf_op jit(solution)/shard_map/ppermute | solution.py:57
  139.0 4.4 %collective-permute-done.11 = bf16[32,4096]{1,0:T(8,128)(2,1)S(1)} collective-permute-done((bf16[32,4096]{1,0:T(8,128)(2,1)S(1)}, bf16[32,4096]{1,0:T(8,128)(2,1)S(1)}, u32[]{:S(2)}, u32[]{:S(2)}) %collective-permute-start.11) | collective-permute-done | bytes 262176 | tf_op jit(solution)/shard_map/ppermute | solution.py:57
  143.4 1.0 add_convert_fusion.5
  144.5 1.4 collective-permute-done.15
  145.9 1.1 add_convert_fusion.1
  146.9 3.5 %collective-permute-start.16 = (bf16[32,4096]{1,0:T(8,128)(2,1)S(1)}, bf16[32,4096]{1,0:T(8,128)(2,1)S(1)}, u32[]{:S(2)}, u32[]{:S(2)}) collective-permute-start(bf16[32,4096]{1,0:T(8,128)(2,1)S(1)} %add_convert_fusion.1), channel_id=1, source_target_pairs={{0,6},{1,7},{2,0},{3,1},{4,2},{5,3},{6,4},{7,5},{8,14},{9,15},{10,... | collective-permute-start | bytes 786440 | tf_op jit(solution)/shard_map/ppermute | solution.py:57
  150.4 3.9 %collective-permute-done.12 = bf16[32,4096]{1,0:T(8,128)(2,1)S(1)} collective-permute-done((bf16[32,4096]{1,0:T(8,128)(2,1)S(1)}, bf16[32,4096]{1,0:T(8,128)(2,1)S(1)}, u32[]{:S(2)}, u32[]{:S(2)}) %collective-permute-start.12) | collective-permute-done | bytes 262176 | tf_op jit(solution)/shard_map/ppermute | solution.py:57
  154.3 1.1 add_convert_fusion.4
  155.5 1.1 add_convert_fusion
  156.6 0.8 pad_maximum_fusion
  (52 shorter events, 0.4 us)
Async XLA Ops:
  0.0 8.3 %copy-start.10 = (bf16[2048,128]{1,0:T(8,128)(2,1)S(1)}, bf16[2048,128]{1,0:T(8,128)(2,1)}, u32[]{:S(2)}) copy-start(bf16[2048,128]{1,0:T(8,128)(2,1)} %param.13) | copy-start | bytes 1572868
  1.8 6.5 %copy-start.12 = (bf16[256,128]{1,0:T(8,128)(2,1)S(1)}, bf16[256,128]{1,0:T(8,128)(2,1)}, u32[]{:S(2)}) copy-start(bf16[256,128]{1,0:T(8,128)(2,1)} %param.10) | copy-start | bytes 196612
  1.8 6.5 %copy-start.11 = (bf16[2048,128]{1,0:T(8,128)(2,1)S(1)}, bf16[2048,128]{1,0:T(8,128)(2,1)}, u32[]{:S(2)}) copy-start(bf16[2048,128]{1,0:T(8,128)(2,1)} %param.14) | copy-start | bytes 1572868
  3.0 5.5 %copy-start.14 = (s32[4]{0:T(128)S(1)}, s32[4]{0:T(128)}, u32[]{:S(2)}) copy-start(s32[4]{0:T(128)} %constant.141.clone) | copy-start | bytes 52
  3.0 5.8 %copy-start.13 = (bf16[256,128]{1,0:T(8,128)(2,1)S(1)}, bf16[256,128]{1,0:T(8,128)(2,1)}, u32[]{:S(2)}) copy-start(bf16[256,128]{1,0:T(8,128)(2,1)} %param.11) | copy-start | bytes 196612
  3.0 14.9 %collective-permute-start.4 = (bf16[272,1152]{1,0:T(8,128)(2,1)S(1)}, bf16[272,1152]{1,0:T(8,128)(2,1)}, u32[]{:S(2)}, u32[]{:S(2)}) collective-permute-start(bf16[272,1152]{1,0:T(8,128)(2,1)S(1)} %fusion.4.refs_1_), channel_id=1, source_target_pairs={{0,8},{1,33},{2,10},{3,35},{4,12},{5,37},{6,14},{7,39},{8,16},{9,4... | collective-permute-start | bytes 1880072 | tf_op jit(solution)/shard_map/ppermute | solution.py:57
  5.2 15.3 %collective-permute-start.3 = (bf16[272,1152]{1,0:T(8,128)(2,1)S(1)}, bf16[272,1152]{1,0:T(8,128)(2,1)}, u32[]{:S(2)}, u32[]{:S(2)}) collective-permute-start(bf16[272,1152]{1,0:T(8,128)(2,1)S(1)} %fusion.4.refs_1_), channel_id=1, source_target_pairs={{0,24},{1,97},{2,26},{3,99},{4,28},{5,101},{6,30},{7,103},{8,0},{9... | collective-permute-start | bytes 1880072 | tf_op jit(solution)/shard_map/ppermute | solution.py:57
  6.7 15.9 %collective-permute-start.2 = (bf16[272,1152]{1,0:T(8,128)(2,1)S(1)}, bf16[272,1152]{1,0:T(8,128)(2,1)}, u32[]{:S(2)}, u32[]{:S(2)}) collective-permute-start(bf16[272,1152]{1,0:T(8,128)(2,1)S(1)} %fusion.4.refs_1_), channel_id=1, source_target_pairs={{0,16},{1,65},{2,18},{3,67},{4,20},{5,69},{6,22},{7,71},{8,24},{9,... | collective-permute-start | bytes 1880072 | tf_op jit(solution)/shard_map/ppermute | solution.py:57
  13.2 1.0 copy-start.8
  14.2 35.5 %collective-permute-start.1 = (bf16[4624,128]{1,0:T(8,128)(2,1)S(1)}, bf16[4624,128]{1,0:T(8,128)(2,1)S(1)}, u32[]{:S(2)}, u32[]{:S(2)}) collective-permute-start(bf16[4624,128]{1,0:T(8,128)(2,1)S(1)} %constant_dynamic-update-slice_fusion.refs_2_.refs_4_), channel_id=1, source_target_pairs={{0,32},{1,9},{2,34},{3,11},{4,36},{5,13},{6,38},{7,15},{8,40},{9,1... | collective-permute-start | bytes 3551240 | tf_op jit(solution)/shard_map/ppermute | solution.py:57
  15.8 33.9 %collective-permute-start = (bf16[4624,128]{1,0:T(8,128)(2,1)S(1)}, bf16[4624,128]{1,0:T(8,128)(2,1)}, u32[]{:S(2)}, u32[]{:S(2)}) collective-permute-start(bf16[4624,128]{1,0:T(8,128)(2,1)S(1)} %constant_dynamic-update-slice_fusion.refs_2_.refs_4_), channel_id=1, source_target_pairs={{0,96},{1,25},{2,98},{3,27},{4,100},{5,29},{6,102},{7,31},{8,104},... | collective-permute-start | bytes 3551240 | tf_op jit(solution)/shard_map/ppermute | solution.py:57
  32.4 1.6 %copy-start = (f32[768,1024]{1,0:T(8,128)}, f32[768,1024]{1,0:T(8,128)S(1)}, u32[]{:S(2)}) copy-start(f32[768,1024]{1,0:T(8,128)S(1)} %get-tuple-element.33.refs_3_) | copy-start | bytes 9437188
  34.1 0.7 copy-start.4
  35.2 1.9 %copy-start.1 = (f32[768,1024]{1,0:T(8,128)S(1)}, f32[768,1024]{1,0:T(8,128)}, u32[]{:S(2)}) copy-start(f32[768,1024]{1,0:T(8,128)} %copy-done) | copy-start | bytes 9437188
  37.1 1.0 copy-start.5
  43.5 1.6 %copy-start.2 = (f32[768,1024]{1,0:T(8,128)}, f32[768,1024]{1,0:T(8,128)S(1)}, u32[]{:S(2)}) copy-start(f32[768,1024]{1,0:T(8,128)S(1)} %get-tuple-element.36.refs_8_) | copy-start | bytes 9437188
  45.1 0.7 copy-start.6
  45.9 26.2 %collective-permute-start.5 = (bf16[4624,128]{1,0:T(8,128)(2,1)S(1)}, bf16[4624,128]{1,0:T(8,128)(2,1)S(1)}, u32[]{:S(2)}, u32[]{:S(2)}) collective-permute-start(bf16[4624,128]{1,0:T(8,128)(2,1)S(1)} %constant_dynamic-update-slice_fusion.refs_2_.refs_4_), channel_id=1, source_target_pairs={{0,64},{1,17},{2,66},{3,19},{4,68},{5,21},{6,70},{7,23},{8,72},{9,... | collective-permute-start | bytes 3551240 | tf_op jit(solution)/shard_map/ppermute | solution.py:57
  49.7 1.9 %copy-start.3 = (f32[768,1024]{1,0:T(8,128)S(1)}, f32[768,1024]{1,0:T(8,128)}, u32[]{:S(2)}) copy-start(f32[768,1024]{1,0:T(8,128)} %copy-done.2) | copy-start | bytes 9437188
  51.6 1.0 copy-start.7
  72.1 33.1 %copy-start.9 = (f32[256,1024]{1,0:T(8,128)S(1)}, f32[256,1024]{1,0:T(8,128)}, u32[]{:S(2)}) copy-start(f32[256,1024]{1,0:T(8,128)} %copy-done.8) | copy-start | bytes 3145732
  72.1 45.5 %slice-start = ((s8[16777216]{0:T(1024)(128)(4,1)}), s8[4194304]{0:T(1024)(128)(4,1)S(1)}, s32[]{:S(2)}) async-start(s8[16777216]{0:T(1024)(128)(4,1)} %bitcast.11), calls=%async_computation | async-start | bytes 8388608
  72.1 45.5 %slice-start.1 = ((s8[16777216]{0:T(1024)(128)(4,1)}), s8[4194304]{0:T(1024)(128)(4,1)S(1)}, s32[]{:S(2)}) async-start(s8[16777216]{0:T(1024)(128)(4,1)} %bitcast.11), calls=%async_computation.1 | async-start | bytes 8388608
  87.2 25.6 %collective-permute-start.6 = (bf16[256,1152]{1,0:T(8,128)(2,1)S(1)}, bf16[256,1152]{1,0:T(8,128)(2,1)S(1)}, u32[]{:S(2)}, u32[]{:S(2)}) collective-permute-start(bf16[256,1152]{1,0:T(8,128)(2,1)S(1)} %get-tuple-element.41), channel_id=1, source_target_pairs={{0,8},{1,33},{2,10},{3,35},{4,12},{5,37},{6,14},{7,39},{8,16},{9,4... | collective-permute-start | bytes 1769480 | tf_op jit(solution)/shard_map/ppermute | solution.py:57
  91.5 26.1 %slice-start.2 = ((s8[16777216]{0:T(1024)(128)(4,1)}), s8[4194304]{0:T(1024)(128)(4,1)S(1)}, s32[]{:S(2)}) async-start(s8[16777216]{0:T(1024)(128)(4,1)} %bitcast.11), calls=%async_computation.2 | async-start | bytes 8388608
  91.5 21.3 %collective-permute-start.7 = (bf16[256,1152]{1,0:T(8,128)(2,1)S(1)}, bf16[256,1152]{1,0:T(8,128)(2,1)S(1)}, u32[]{:S(2)}, u32[]{:S(2)}) collective-permute-start(bf16[256,1152]{1,0:T(8,128)(2,1)S(1)} %get-tuple-element.42), channel_id=1, source_target_pairs={{0,24},{1,97},{2,26},{3,99},{4,28},{5,101},{6,30},{7,103},{8,0},{9... | collective-permute-start | bytes 1769480 | tf_op jit(solution)/shard_map/ppermute | solution.py:57
  93.2 24.4 %slice-start.3 = ((s8[16777216]{0:T(1024)(128)(4,1)}), s8[4194304]{0:T(1024)(128)(4,1)S(1)}, s32[]{:S(2)}) async-start(s8[16777216]{0:T(1024)(128)(4,1)} %bitcast.11), calls=%async_computation.3 | async-start | bytes 8388608
  93.2 24.4 %collective-permute-start.8 = (bf16[256,1152]{1,0:T(8,128)(2,1)S(1)}, bf16[256,1152]{1,0:T(8,128)(2,1)S(1)}, u32[]{:S(2)}, u32[]{:S(2)}) collective-permute-start(bf16[256,1152]{1,0:T(8,128)(2,1)S(1)} %get-tuple-element.43), channel_id=1, source_target_pairs={{0,16},{1,65},{2,18},{3,67},{4,20},{5,69},{6,22},{7,71},{8,24},{9,... | collective-permute-start | bytes 1769480 | tf_op jit(solution)/shard_map/ppermute | solution.py:57
  123.4 7.8 %collective-permute-start.9 = (bf16[128,4096]{1,0:T(8,128)(2,1)}, bf16[128,4096]{1,0:T(8,128)(2,1)}, u32[]{:S(2)}, u32[]{:S(2)}) collective-permute-start(bf16[128,4096]{1,0:T(8,128)(2,1)} %get-tuple-element.47), channel_id=1, source_target_pairs={{0,1},{1,0},{2,3},{3,2},{4,5},{5,4},{6,7},{7,6},{8,9},{9,8},{10,11... | collective-permute-start | bytes 3145736 | tf_op jit(solution)/shard_map/ppermute | solution.py:57
  131.1 3.9 %collective-permute-start.13 = (bf16[128,4096]{1,0:T(8,128)(2,1)S(1)}, bf16[128,4096]{1,0:T(8,128)(2,1)}, u32[]{:S(2)}, u32[]{:S(2)}) collective-permute-start(bf16[128,4096]{1,0:T(8,128)(2,1)S(1)} %get-tuple-element.50), channel_id=1, source_target_pairs={{0,1},{1,0},{2,3},{3,2},{4,5},{5,4},{6,7},{7,6},{8,9},{9,8},{10,11... | collective-permute-start | bytes 3145736 | tf_op jit(solution)/shard_map/ppermute | solution.py:57
  132.4 18.0 %collective-permute-start.10 = (bf16[32,4096]{1,0:T(8,128)(2,1)S(1)}, bf16[32,4096]{1,0:T(8,128)(2,1)S(1)}, u32[]{:S(2)}, u32[]{:S(2)}) collective-permute-start(bf16[32,4096]{1,0:T(8,128)(2,1)S(1)} %get-tuple-element.55), channel_id=1, source_target_pairs={{0,6},{1,7},{2,0},{3,1},{4,2},{5,3},{6,4},{7,5},{8,14},{9,15},{10,... | collective-permute-start | bytes 786440 | tf_op jit(solution)/shard_map/ppermute | solution.py:57
  135.0 8.4 %collective-permute-start.11 = (bf16[32,4096]{1,0:T(8,128)(2,1)S(1)}, bf16[32,4096]{1,0:T(8,128)(2,1)S(1)}, u32[]{:S(2)}, u32[]{:S(2)}) collective-permute-start(bf16[32,4096]{1,0:T(8,128)(2,1)S(1)} %get-tuple-element.56), channel_id=1, source_target_pairs={{0,2},{1,3},{2,4},{3,5},{4,6},{5,7},{6,0},{7,1},{8,10},{9,11},{10,... | collective-permute-start | bytes 786440 | tf_op jit(solution)/shard_map/ppermute | solution.py:57
  136.1 19.3 %collective-permute-start.14 = (bf16[32,4096]{1,0:T(8,128)(2,1)S(1)}, bf16[32,4096]{1,0:T(8,128)(2,1)S(1)}, u32[]{:S(2)}, u32[]{:S(2)}) collective-permute-start(bf16[32,4096]{1,0:T(8,128)(2,1)S(1)} %get-tuple-element.57), channel_id=1, source_target_pairs={{0,2},{1,3},{2,4},{3,5},{4,6},{5,7},{6,0},{7,1},{8,10},{9,11},{10,... | collective-permute-start | bytes 786440 | tf_op jit(solution)/shard_map/ppermute | solution.py:57
  136.4 9.5 %collective-permute-start.15 = (bf16[32,4096]{1,0:T(8,128)(2,1)S(1)}, bf16[32,4096]{1,0:T(8,128)(2,1)S(1)}, u32[]{:S(2)}, u32[]{:S(2)}) collective-permute-start(bf16[32,4096]{1,0:T(8,128)(2,1)S(1)} %get-tuple-element.58), channel_id=1, source_target_pairs={{0,6},{1,7},{2,0},{3,1},{4,2},{5,3},{6,4},{7,5},{8,14},{9,15},{10,... | collective-permute-start | bytes 786440 | tf_op jit(solution)/shard_map/ppermute | solution.py:57
  144.4 9.9 %collective-permute-start.12 = (bf16[32,4096]{1,0:T(8,128)(2,1)S(1)}, bf16[32,4096]{1,0:T(8,128)(2,1)S(1)}, u32[]{:S(2)}, u32[]{:S(2)}) collective-permute-start(bf16[32,4096]{1,0:T(8,128)(2,1)S(1)} %add_convert_fusion.5), channel_id=1, source_target_pairs={{0,2},{1,3},{2,4},{3,5},{4,6},{5,7},{6,0},{7,1},{8,10},{9,11},{10,... | collective-permute-start | bytes 786440 | tf_op jit(solution)/shard_map/ppermute | solution.py:57
  146.9 8.5 %collective-permute-start.16 = (bf16[32,4096]{1,0:T(8,128)(2,1)S(1)}, bf16[32,4096]{1,0:T(8,128)(2,1)S(1)}, u32[]{:S(2)}, u32[]{:S(2)}) collective-permute-start(bf16[32,4096]{1,0:T(8,128)(2,1)S(1)} %add_convert_fusion.1), channel_id=1, source_target_pairs={{0,6},{1,7},{2,0},{3,1},{4,2},{5,3},{6,4},{7,5},{8,14},{9,15},{10,... | collective-permute-start | bytes 786440 | tf_op jit(solution)/shard_map/ppermute | solution.py:57

commit v2 on v1

--- a/solution.py
+++ b/solution.py
@@ -76,7 +76,7 @@
     if final:
         outs = [refs.pop(0) for _ in range(n_home)]
     else:
-        acc_out, ml_out = refs[-10:-8]
+        acc_out, ml_out, token = refs[-11:-8]
     k_scr, v_scr, meta_scr, q_scr, qpos_scr, m_scr, acc_scr, sems = refs[-8:]
     home_id = pl.program_id(0)
     tokens = NEW
@@ -209,6 +209,7 @@
             ml = jnp.where(lane == h, m_scr[:, h * HD : (h + 1) * HD], ml)
             ml = jnp.where(lane == GROUP + h, acc_scr[:, h * 2 * HD + HD : (h + 1) * 2 * HD], ml)
         ml_out[...] = ml
+        token[...] = jnp.zeros(token.shape, F32)
         return
 
     def emit(out):
@@ -241,7 +242,7 @@
     aliases = {}
     if state is not None:
         in_specs += [turn(QW), turn(HD)]
-        args += list(state)
+        args += list(state[:2])
     if final:
         out_shape = [jax.ShapeDtypeStruct((NEW, RET_W), BF)] * n_home
         out_specs = [fixed((NEW, RET_W))] * n_home
@@ -250,12 +251,13 @@
         out_shape = [
             jax.ShapeDtypeStruct((places * NEW, QW), F32),
             jax.ShapeDtypeStruct((places * NEW, HD), F32),
+            jax.ShapeDtypeStruct((8, HD), F32),
         ]
-        out_specs = [turn(QW, at), turn(HD, at)]
+        out_specs = [turn(QW, at), turn(HD, at), fixed((8, HD))]
         if target is not None:
             aliases = {n_home + len(args): 0, n_home + len(args) + 1: 1}
             in_specs += [anywhere, anywhere]
-            args += list(target)
+            args += list(target[:2])
     work = n_home * n_kv * NEW * GROUP * (SEG // 4 + NEW)
     return pl.pallas_call(
         functools.partial(attend_kernel, n_home, n_kv, first_kv, state is not None, final),
@@ -363,10 +365,6 @@
     )(core, *parts, weight)
 
 
-def after(value, *others):
-    return lax.optimization_barrier((value, *others))[0]
-
-
 def per_device(
     queries, new_keys, new_values, positions, cache_keys, cache_values, pattern, out_weight
 ):
@@ -395,8 +393,8 @@
     along_z = y * SIDE + (z + steps) % SIDE
     segments = jnp.where(core == 0, along_y, along_z).astype(F32)
 
-    def flags_of(row):
-        named = row.astype(F32).reshape(1, NEW // QB, -1)
+    def flags_of(row, zero=0.0):
+        named = (row.astype(F32) + zero).reshape(1, NEW // QB, -1)
         hits = named == segments[:, None, None]
         return jnp.sum(hits.astype(jnp.int32), axis=-1).reshape(-1)
 
@@ -404,7 +402,7 @@
 
     def read_flags(offsets, done):
         for o in offsets:
-            flags[o] = flags_of(after(q_at[o][NEW, : picks.shape[0]], *done))
+            flags[o] = flags_of(q_at[o][NEW, : picks.shape[0]], done[0, 0])
 
     def run(homes, kvs, state=None, final=False, into=None):
         offsets = [order[n] for n in homes]
@@ -420,16 +418,15 @@
 
     own_state = run((0,), (0,))
     for shift in (1, 3):
-        kv_at[-shift % SIDE] = move(after(kv_own, *own_state), "k", shift)
-    read_flags((1, 3), own_state)
+        kv_at[-shift % SIDE] = move(kv_own, "k", shift)
+    read_flags((1, 3), own_state[2])
     state = run((1, 2), (0,), into=(3, 0, None))
-    read_flags((2,), state)
+    read_flags((2,), state[2])
     state = run((3,), (0,), into=(3, 2, state))
-    kv_at[2] = move(after(kv_own, *state), "k", 2)
+    kv_at[2] = move(kv_own, "k", 2)
     state = run((1, 2, 3), (1, 2), state)
     partials = run((1, 2, 3), (3,), state, True)
     backs = [move(part, "q", order[n]) for n, part in zip((1, 2, 3), partials)]
-    own_state = [after(value, *partials) for value in own_state]
     mine = run((0,), (1, 2, 3), own_state, True)
 
     core_id = core.reshape(1)

time: 159 us -> 170 us (1.069)
  other arithmetic: 10.8 us -> 14.8 us
  waiting for transfers between devices: 17.2 us -> 21.2 us
  Pallas kernels: 70.4 us -> 73.3 us
    ppermute x17, waiting for transfers between devices: 17.2 us -> 21.2 us  [move(): return lax.ppermute(value, AXES, pairs(kind, shift))]
    add x0 -> x3, other arithmetic: none -> 4.03 us  [flags_of(): named = (row.astype(F32) + zero).reshape(1, NEW // QB, -1)]
    pallas_call x6, Pallas kernels: 61.1 us -> 64 us  [attend(): pl.pallas_call(functools.partial(attend_kernel, n_home, n_kv, first_kv, s...]
    squeeze x3 -> x0, local copies, waits for them, and re-layouts: 2.05 us -> none  [read_flags(): flags[o] = flags_of(after(q_at[o][NEW, :picks.shape[0]], *done))]
  transfers between devices with their start and end apart: 17 -> 17, of which waited for: 6 -> 5; matrix products, arithmetic and copies ran while one was open for 6% -> 7% of each run, Pallas kernels for 31% -> 30%
where the time goes in v2:
time: 170 us; the launch traced here: 168 us
  Pallas kernels  73.3 us (43%)
  starting transfers between devices  45 us (26%)
  waiting for transfers between devices  21.2 us (12%)
  other arithmetic  14.8 us (9%)
  local copies, waits for them, and re-layouts  13.7 us (8%)
    pallas_call x6, Pallas kernels, attend(): pl.pallas_call(functools.partial(attend_kernel, n_home, n_kv, first_kv, s...  64 us
    ppermute x17, starting transfers between devices, move(): return lax.ppermute(value, AXES, pairs(kind, shift))  45 us
    ppermute x17, waiting for transfers between devices, move(): return lax.ppermute(value, AXES, pairs(kind, shift))  21.2 us
    unnamed x42, local copies, waits for them, and re-layouts  11.7 us
    pallas_call x2, Pallas kernels, project(): pl.pallas_call(functools.partial(project_kernel, 0 if merged else len(par...  9.34 us
    add x3, other arithmetic, flags_of(): named = (row.astype(F32) + zero).reshape(1, NEW // QB, -1)  4.03 us
  transfers between devices with their start and end apart: 17, of which 5 were waited for; matrix products, arithmetic and copies ran while one was open for 7% of the time, Pallas kernels for 30%

profile of v2, /device:TPU:1, one launch (start us, length us, event | category | flops | bytes accessed | tf_op | source)
XLA Modules:
  0.0 168.5 jit_solution(14645956751864151214)
XLA Ops:
  0.0 0.8 and_select_fusion.3
  0.8 0.7 fusion.18
  1.4 0.1 convert_element_type.160
  1.5 0.1 reshape.61
  1.6 0.1 copy.21
  1.8 1.2 fusion.4.refs_1_
  3.0 3.8 %collective-permute-start.5 = (bf16[272,1152]{1,0:T(8,128)(2,1)S(1)}, bf16[272,1152]{1,0:T(8,128)(2,1)}, u32[]{:S(2)}, u32[]{:S(2)}) collective-permute-start(bf16[272,1152]{1,0:T(8,128)(2,1)S(1)} %fusion.4.refs_1_), channel_id=1, source_target_pairs={{0,16},{1,65},{2,18},{3,67},{4,20},{5,69},{6,22},{7,71},{8,24},{9,... | collective-permute-start | bytes 1880072 | tf_op jit(solution)/shard_map/ppermute | solution.py:57
  6.8 0.4 collective-permute-start.4
  7.2 2.3 %collective-permute-start.3 = (bf16[272,1152]{1,0:T(8,128)(2,1)S(1)}, bf16[272,1152]{1,0:T(8,128)(2,1)}, u32[]{:S(2)}, u32[]{:S(2)}) collective-permute-start(bf16[272,1152]{1,0:T(8,128)(2,1)S(1)} %fusion.4.refs_1_), channel_id=1, source_target_pairs={{0,24},{1,97},{2,26},{3,99},{4,28},{5,101},{6,30},{7,103},{8,0},{9... | collective-permute-start | bytes 1880072 | tf_op jit(solution)/shard_map/ppermute | solution.py:57
  9.7 1.7 %collective-permute-start.1 = (bf16[4624,128]{1,0:T(8,128)(2,1)S(1)}, bf16[4624,128]{1,0:T(8,128)(2,1)S(1)}, u32[]{:S(2)}, u32[]{:S(2)}) collective-permute-start(bf16[4624,128]{1,0:T(8,128)(2,1)S(1)} %constant_dynamic-update-slice_fusion.refs_2_.refs_4_), channel_id=1, source_target_pairs={{0,32},{1,9},{2,34},{3,11},{4,36},{5,13},{6,38},{7,15},{8,40},{9,1... | collective-permute-start | bytes 3551240 | tf_op jit(solution)/shard_map/ppermute | solution.py:57
  11.4 2.2 %collective-permute-start = (bf16[4624,128]{1,0:T(8,128)(2,1)S(1)}, bf16[4624,128]{1,0:T(8,128)(2,1)}, u32[]{:S(2)}, u32[]{:S(2)}) collective-permute-start(bf16[4624,128]{1,0:T(8,128)(2,1)S(1)} %constant_dynamic-update-slice_fusion.refs_2_.refs_4_), channel_id=1, source_target_pairs={{0,96},{1,25},{2,98},{3,27},{4,100},{5,29},{6,102},{7,31},{8,104},... | collective-permute-start | bytes 3551240 | tf_op jit(solution)/shard_map/ppermute | solution.py:57
  13.6 0.2 convert_reduce_fusion.3
  13.8 0.1 reshape.60.refs_0_
  13.9 4.4 %shard_map.91 = (f32[256,1024]{1,0:T(8,128)S(1)}, f32[256,128]{1,0:T(8,128)S(1)}, f32[8,128]{1,0:T(8,128)S(1)}) custom-call(s32[16]{0:T(128)S(1)} %reshape.60.refs_0_, bf16[272,1152]{1,0:T(8,128)(2,1)S(1)} %fusion.4.refs_1_, bf16[4624,128]{1,0:T(8,128)(2,1)S(1)} %constant_dynamic-update-slice_fusion.refs_2_.refs_4_), custom_call_target="tpu_custom_call" | custom-call | flops 1610612736 | bytes 2097152 | tf_op jit(solution)/shard_map/pallas_call | solution.py:262
  18.3 1.0 copy-done.8
  19.3 0.5 slice.17
  19.8 7.5 %collective-permute-done.3.refs_2_.refs_3_ = bf16[272,1152]{1,0:T(8,128)(2,1)} collective-permute-done((bf16[272,1152]{1,0:T(8,128)(2,1)S(1)}, bf16[272,1152]{1,0:T(8,128)(2,1)}, u32[]{:S(2)}, u32[]{:S(2)}) %collective-permute-start.3) | collective-permute-done | bytes 626720 | tf_op jit(solution)/shard_map/ppermute | solution.py:57
  27.2 7.6 %collective-permute-start.2 = (bf16[4624,128]{1,0:T(8,128)(2,1)S(1)}, bf16[4624,128]{1,0:T(8,128)(2,1)}, u32[]{:S(2)}, u32[]{:S(2)}) collective-permute-start(bf16[4624,128]{1,0:T(8,128)(2,1)S(1)} %constant_dynamic-update-slice_fusion.refs_2_.refs_4_), channel_id=1, source_target_pairs={{0,64},{1,17},{2,66},{3,19},{4,68},{5,21},{6,70},{7,23},{8,72},{9,... | collective-permute-start | bytes 3551240 | tf_op jit(solution)/shard_map/ppermute | solution.py:57
  34.8 1.3 fusion.17
  36.1 0.1 add.205
  36.2 1.3 fusion.15
  37.5 0.1 add.207
  37.6 0.3 convert_reduce_fusion.1
  37.9 0.1 reshape.63.refs_1_
  38.0 0.1 reshape.62.refs_0_
  38.1 9.2 %shard_map.93 = (f32[768,1024]{1,0:T(8,128)S(1)}, f32[768,128]{1,0:T(8,128)S(1)}, f32[8,128]{1,0:T(8,128)S(1)}) custom-call(s32[16]{0:T(128)S(1)} %reshape.62.refs_0_, s32[16]{0:T(128)S(1)} %reshape.63.refs_1_, bf16[272,1152]{1,0:T(8,128)(2,1)} %collective-permute-done.3.refs_2_.refs_3_, bf16[272,1152]{1,0:T(8,128)(2,1)} %collective-permute-done.4.refs_3_.refs_4_, ...), custom_call_target="tpu_custom_call" | custom-call | flops 3221225472 | bytes 4194304 | tf_op jit(solution)/shard_map/pallas_call | solution.py:262
  47.3 1.6 copy-done
  48.9 0.7 copy-done.4
  49.7 0.6 slice.20
  50.3 1.4 fusion.13
  51.6 0.1 add.210
  51.7 0.2 convert_reduce_fusion
  51.9 0.1 reshape.64.refs_0_.refs_2_
  52.0 1.9 %copy-done.1 = f32[768,1024]{1,0:T(8,128)S(1)} copy-done((f32[768,1024]{1,0:T(8,128)S(1)}, f32[768,1024]{1,0:T(8,128)}, u32[]{:S(2)}) %copy-start.1) | copy-done | bytes 3145752
  53.9 1.0 copy-done.5
  54.9 5.8 %shard_map.94 = (f32[768,1024]{1,0:T(8,128)S(1)}, f32[768,128]{1,0:T(8,128)S(1)}, f32[8,128]{1,0:T(8,128)}) custom-call(s32[16]{0:T(128)S(1)} %reshape.64.refs_0_.refs_2_, bf16[272,1152]{1,0:T(8,128)(2,1)} %collective-permute-done.5.refs_1_.refs_5_, ...), custom_call_target="tpu_custom_call", output_to_operand_aliasing={{0}: (3, {}), {1}: (4, {})} | custom-call | flops 1610612736 | bytes 2097152 | tf_op jit(solution)/shard_map/pallas_call | solution.py:262
  60.7 1.6 copy-done.2
  62.3 0.7 copy-done.6
  63.1 1.9 %copy-done.3 = f32[768,1024]{1,0:T(8,128)S(1)} copy-done((f32[768,1024]{1,0:T(8,128)S(1)}, f32[768,1024]{1,0:T(8,128)}, u32[]{:S(2)}) %copy-start.3) | copy-done | bytes 3145752
  65.0 1.0 copy-done.7
  66.0 20.0 %shard_map.95 = (f32[768,1024]{1,0:T(8,128)S(1)}, f32[768,128]{1,0:T(8,128)S(1)}, f32[8,128]{1,0:T(8,128)}) custom-call(s32[16]{0:T(128)S(1)} %reshape.62.refs_0_, s32[16]{0:T(128)S(1)} %reshape.63.refs_1_, s32[16]{0:T(128)S(1)} %reshape.64.refs_0_.refs_2_, bf16[272,1152]{1,0:T(8,128)(2,1)} %collective-permute-done.3.refs_2_.refs_3_, ...), custom_call_target="tpu_custom_call" | custom-call | flops 9663676416 | bytes 6291456 | tf_op jit(solution)/shard_map/pallas_call | solution.py:262
  86.0 16.3 %shard_map.96 = (bf16[256,1152]{1,0:T(8,128)(2,1)S(1)}, bf16[256,1152]{1,0:T(8,128)(2,1)S(1)}, bf16[256,1152]{1,0:T(8,128)(2,1)S(1)}) custom-call(s32[16]{0:T(128)S(1)} %reshape.62.refs_0_, s32[16]{0:T(128)S(1)} %reshape.63.refs_1_, s32[16]{0:T(128)S(1)} %reshape.64.refs_0_.refs_2_, bf16[272,1152]{1,0:T(8,128)(2,1)} %collective-permute-done.3.refs_2_.refs_3_, ...), custom_call_target="tpu_custom_call" | custom-call | flops 4831838208 | bytes 6291456 | tf_op jit(solution)/shard_map/pallas_call | solution.py:262
  102.4 6.7 %collective-permute-start.7 = (bf16[256,1152]{1,0:T(8,128)(2,1)S(1)}, bf16[256,1152]{1,0:T(8,128)(2,1)S(1)}, u32[]{:S(2)}, u32[]{:S(2)}) collective-permute-start(bf16[256,1152]{1,0:T(8,128)(2,1)S(1)} %get-tuple-element.34), channel_id=1, source_target_pairs={{0,24},{1,97},{2,26},{3,99},{4,28},{5,101},{6,30},{7,103},{8,0},{9... | collective-permute-start | bytes 1769480 | tf_op jit(solution)/shard_map/ppermute | solution.py:57
  109.1 3.9 %collective-permute-start.8 = (bf16[256,1152]{1,0:T(8,128)(2,1)S(1)}, bf16[256,1152]{1,0:T(8,128)(2,1)S(1)}, u32[]{:S(2)}, u32[]{:S(2)}) collective-permute-start(bf16[256,1152]{1,0:T(8,128)(2,1)S(1)} %get-tuple-element.35), channel_id=1, source_target_pairs={{0,16},{1,65},{2,18},{3,67},{4,20},{5,69},{6,22},{7,71},{8,24},{9,... | collective-permute-start | bytes 1769480 | tf_op jit(solution)/shard_map/ppermute | solution.py:57
  112.9 8.4 %shard_map.92.refs_0_ = bf16[256,1152]{1,0:T(8,128)(2,1)S(1)} custom-call(s32[16]{0:T(128)S(1)} %reshape.60.refs_0_, bf16[272,1152]{1,0:T(8,128)(2,1)S(1)} %fusion.4.refs_1_, bf16[4624,128]{1,0:T(8,128)(2,1)} %collective-permute-done.refs_2_.refs_6_, bf16[4624,128]{1,0:T(8,128)(2,1)S(1)} %collective-permute-done.1.refs_3_.refs_7_, ...), custom_call_target="tpu_custom_call" | custom-call | flops 4831838208 | bytes 2097152 | tf_op jit(solution)/shard_map/pallas_call | solution.py:262
  121.4 4.0 %collective-permute-done.8.refs_3_ = bf16[256,1152]{1,0:T(8,128)(2,1)S(1)} collective-permute-done((bf16[256,1152]{1,0:T(8,128)(2,1)S(1)}, bf16[256,1152]{1,0:T(8,128)(2,1)S(1)}, u32[]{:S(2)}, u32[]{:S(2)}) %collective-permute-start.8) | collective-permute-done | bytes 589856 | tf_op jit(solution)/shard_map/ppermute | solution.py:57
  125.4 5.8 %shard_map.97 = (bf16[128,4096]{1,0:T(8,128)(2,1)S(1)}, bf16[128,4096]{1,0:T(8,128)(2,1)}, bf16[256,1024]{1,0:T(8,128)(2,1)S(1)}) custom-call(s32[1]{0:T(128)} %bitcast.core, bf16[256,1152]{1,0:T(8,128)(2,1)S(1)} %shard_map.92.refs_0_, bf16[256,1152]{1,0:T(8,128)(2,1)S(1)} %collective-permute-done.6.refs_1_, ...), custom_call_target="tpu_custom_call" | custom-call | flops 4294967296 | bytes 10485760 | tf_op jit(solution)/shard_map/pallas_call | solution.py:349
  131.2 7.4 %collective-permute-start.9 = (bf16[128,4096]{1,0:T(8,128)(2,1)}, bf16[128,4096]{1,0:T(8,128)(2,1)}, u32[]{:S(2)}, u32[]{:S(2)}) collective-permute-start(bf16[128,4096]{1,0:T(8,128)(2,1)} %get-tuple-element.37), channel_id=1, source_target_pairs={{0,1},{1,0},{2,3},{3,2},{4,5},{5,4},{6,7},{7,6},{8,9},{9,8},{10,11... | collective-permute-start | bytes 3145736 | tf_op jit(solution)/shard_map/ppermute | solution.py:57
  138.6 3.5 %shard_map.98 = (bf16[128,4096]{1,0:T(8,128)(2,1)S(1)}, bf16[128,4096]{1,0:T(8,128)(2,1)S(1)}) custom-call(s32[1]{0:T(128)} %bitcast.core, bf16[256,1024]{1,0:T(8,128)(2,1)S(1)} %get-tuple-element.38.refs_0_, bf16[1024,8192]{1,0:T(8,128)(2,1)S(1)} %bitcast.8), custom_call_target="tpu_custom_call" | custom-call | flops 4294967296 | bytes 10485760 | tf_op jit(solution)/shard_map/pallas_call | solution.py:349
  142.2 0.1 collective-permute-start.13
  142.4 1.2 add_convert_fusion.7
  143.5 2.6 %collective-permute-start.10 = (bf16[32,4096]{1,0:T(8,128)(2,1)S(1)}, bf16[32,4096]{1,0:T(8,128)(2,1)S(1)}, u32[]{:S(2)}, u32[]{:S(2)}) collective-permute-start(bf16[32,4096]{1,0:T(8,128)(2,1)S(1)} %get-tuple-element.45), channel_id=1, source_target_pairs={{0,6},{1,7},{2,0},{3,1},{4,2},{5,3},{6,4},{7,5},{8,14},{9,15},{10,... | collective-permute-start | bytes 786440 | tf_op jit(solution)/shard_map/ppermute | solution.py:57
  146.1 1.2 add_convert_fusion.3
  147.2 0.3 collective-permute-start.14
  147.5 2.6 %collective-permute-start.15 = (bf16[32,4096]{1,0:T(8,128)(2,1)S(1)}, bf16[32,4096]{1,0:T(8,128)(2,1)S(1)}, u32[]{:S(2)}, u32[]{:S(2)}) collective-permute-start(bf16[32,4096]{1,0:T(8,128)(2,1)S(1)} %get-tuple-element.48), channel_id=1, source_target_pairs={{0,6},{1,7},{2,0},{3,1},{4,2},{5,3},{6,4},{7,5},{8,14},{9,15},{10,... | collective-permute-start | bytes 786440 | tf_op jit(solution)/shard_map/ppermute | solution.py:57
  150.1 4.4 %collective-permute-done.11 = bf16[32,4096]{1,0:T(8,128)(2,1)S(1)} collective-permute-done((bf16[32,4096]{1,0:T(8,128)(2,1)S(1)}, bf16[32,4096]{1,0:T(8,128)(2,1)S(1)}, u32[]{:S(2)}, u32[]{:S(2)}) %collective-permute-start.11) | collective-permute-done | bytes 262176 | tf_op jit(solution)/shard_map/ppermute | solution.py:57
  154.5 1.0 add_convert_fusion.5
  155.6 1.4 collective-permute-done.15
  157.0 1.1 add_convert_fusion.1
  158.0 3.5 %collective-permute-start.16 = (bf16[32,4096]{1,0:T(8,128)(2,1)S(1)}, bf16[32,4096]{1,0:T(8,128)(2,1)S(1)}, u32[]{:S(2)}, u32[]{:S(2)}) collective-permute-start(bf16[32,4096]{1,0:T(8,128)(2,1)S(1)} %add_convert_fusion.1), channel_id=1, source_target_pairs={{0,6},{1,7},{2,0},{3,1},{4,2},{5,3},{6,4},{7,5},{8,14},{9,15},{10,... | collective-permute-start | bytes 786440 | tf_op jit(solution)/shard_map/ppermute | solution.py:57
  161.5 3.9 %collective-permute-done.12 = bf16[32,4096]{1,0:T(8,128)(2,1)S(1)} collective-permute-done((bf16[32,4096]{1,0:T(8,128)(2,1)S(1)}, bf16[32,4096]{1,0:T(8,128)(2,1)S(1)}, u32[]{:S(2)}, u32[]{:S(2)}) %collective-permute-start.12) | collective-permute-done | bytes 262176 | tf_op jit(solution)/shard_map/ppermute | solution.py:57
  165.5 1.1 add_convert_fusion.4
  166.6 1.1 add_convert_fusion
  167.7 0.8 pad_maximum_fusion
  (54 shorter events, 0.4 us)
Async XLA Ops:
  0.0 9.5 %copy-start.10 = (bf16[2048,128]{1,0:T(8,128)(2,1)S(1)}, bf16[2048,128]{1,0:T(8,128)(2,1)}, u32[]{:S(2)}) copy-start(bf16[2048,128]{1,0:T(8,128)(2,1)} %param.13) | copy-start | bytes 1572868
  1.6 7.9 %copy-start.12 = (bf16[256,128]{1,0:T(8,128)(2,1)S(1)}, bf16[256,128]{1,0:T(8,128)(2,1)}, u32[]{:S(2)}) copy-start(bf16[256,128]{1,0:T(8,128)(2,1)} %param.10) | copy-start | bytes 196612
  1.8 7.7 %copy-start.11 = (bf16[2048,128]{1,0:T(8,128)(2,1)S(1)}, bf16[2048,128]{1,0:T(8,128)(2,1)}, u32[]{:S(2)}) copy-start(bf16[2048,128]{1,0:T(8,128)(2,1)} %param.14) | copy-start | bytes 1572868
  3.0 6.7 %copy-start.13 = (bf16[256,128]{1,0:T(8,128)(2,1)S(1)}, bf16[256,128]{1,0:T(8,128)(2,1)}, u32[]{:S(2)}) copy-start(bf16[256,128]{1,0:T(8,128)(2,1)} %param.11) | copy-start | bytes 196612
  3.0 10.6 %copy-start.14 = (s32[4]{0:T(128)S(1)}, s32[4]{0:T(128)}, u32[]{:S(2)}) copy-start(s32[4]{0:T(128)} %constant.141.clone) | copy-start | bytes 52
  3.0 47.3 %collective-permute-start.5 = (bf16[272,1152]{1,0:T(8,128)(2,1)S(1)}, bf16[272,1152]{1,0:T(8,128)(2,1)}, u32[]{:S(2)}, u32[]{:S(2)}) collective-permute-start(bf16[272,1152]{1,0:T(8,128)(2,1)S(1)} %fusion.4.refs_1_), channel_id=1, source_target_pairs={{0,16},{1,65},{2,18},{3,67},{4,20},{5,69},{6,22},{7,71},{8,24},{9,... | collective-permute-start | bytes 1880072 | tf_op jit(solution)/shard_map/ppermute | solution.py:57
  6.8 29.4 %collective-permute-start.4 = (bf16[272,1152]{1,0:T(8,128)(2,1)S(1)}, bf16[272,1152]{1,0:T(8,128)(2,1)}, u32[]{:S(2)}, u32[]{:S(2)}) collective-permute-start(bf16[272,1152]{1,0:T(8,128)(2,1)S(1)} %fusion.4.refs_1_), channel_id=1, source_target_pairs={{0,8},{1,33},{2,10},{3,35},{4,12},{5,37},{6,14},{7,39},{8,16},{9,4... | collective-permute-start | bytes 1880072 | tf_op jit(solution)/shard_map/ppermute | solution.py:57
  7.2 20.0 %collective-permute-start.3 = (bf16[272,1152]{1,0:T(8,128)(2,1)S(1)}, bf16[272,1152]{1,0:T(8,128)(2,1)}, u32[]{:S(2)}, u32[]{:S(2)}) collective-permute-start(bf16[272,1152]{1,0:T(8,128)(2,1)S(1)} %fusion.4.refs_1_), channel_id=1, source_target_pairs={{0,24},{1,97},{2,26},{3,99},{4,28},{5,101},{6,30},{7,103},{8,0},{9... | collective-permute-start | bytes 1880072 | tf_op jit(solution)/shard_map/ppermute | solution.py:57
  9.7 53.4 %collective-permute-start.1 = (bf16[4624,128]{1,0:T(8,128)(2,1)S(1)}, bf16[4624,128]{1,0:T(8,128)(2,1)S(1)}, u32[]{:S(2)}, u32[]{:S(2)}) collective-permute-start(bf16[4624,128]{1,0:T(8,128)(2,1)S(1)} %constant_dynamic-update-slice_fusion.refs_2_.refs_4_), channel_id=1, source_target_pairs={{0,32},{1,9},{2,34},{3,11},{4,36},{5,13},{6,38},{7,15},{8,40},{9,1... | collective-permute-start | bytes 3551240 | tf_op jit(solution)/shard_map/ppermute | solution.py:57
  11.4 51.7 %collective-permute-start = (bf16[4624,128]{1,0:T(8,128)(2,1)S(1)}, bf16[4624,128]{1,0:T(8,128)(2,1)}, u32[]{:S(2)}, u32[]{:S(2)}) collective-permute-start(bf16[4624,128]{1,0:T(8,128)(2,1)S(1)} %constant_dynamic-update-slice_fusion.refs_2_.refs_4_), channel_id=1, source_target_pairs={{0,96},{1,25},{2,98},{3,27},{4,100},{5,29},{6,102},{7,31},{8,104},... | collective-permute-start | bytes 3551240 | tf_op jit(solution)/shard_map/ppermute | solution.py:57
  18.3 1.0 copy-start.8
  27.2 58.8 %collective-permute-start.2 = (bf16[4624,128]{1,0:T(8,128)(2,1)S(1)}, bf16[4624,128]{1,0:T(8,128)(2,1)}, u32[]{:S(2)}, u32[]{:S(2)}) collective-permute-start(bf16[4624,128]{1,0:T(8,128)(2,1)S(1)} %constant_dynamic-update-slice_fusion.refs_2_.refs_4_), channel_id=1, source_target_pairs={{0,64},{1,17},{2,66},{3,19},{4,68},{5,21},{6,70},{7,23},{8,72},{9,... | collective-permute-start | bytes 3551240 | tf_op jit(solution)/shard_map/ppermute | solution.py:57
  47.3 1.6 copy-start
  48.9 0.7 copy-start.4
  52.0 1.9 %copy-start.1 = (f32[768,1024]{1,0:T(8,128)S(1)}, f32[768,1024]{1,0:T(8,128)}, u32[]{:S(2)}) copy-start(f32[768,1024]{1,0:T(8,128)} %copy-done) | copy-start | bytes 9437188
  53.9 1.0 copy-start.5
  60.7 1.6 copy-start.2
  62.3 0.7 copy-start.6
  63.1 1.9 %copy-start.3 = (f32[768,1024]{1,0:T(8,128)S(1)}, f32[768,1024]{1,0:T(8,128)}, u32[]{:S(2)}) copy-start(f32[768,1024]{1,0:T(8,128)} %copy-done.2) | copy-start | bytes 9437188
  65.0 1.0 copy-start.7
  86.0 26.9 %copy-start.9 = (f32[256,1024]{1,0:T(8,128)S(1)}, f32[256,1024]{1,0:T(8,128)}, u32[]{:S(2)}) copy-start(f32[256,1024]{1,0:T(8,128)} %copy-done.8) | copy-start | bytes 3145732
  86.0 39.4 %slice-start = ((s8[16777216]{0:T(1024)(128)(4,1)}), s8[4194304]{0:T(1024)(128)(4,1)S(1)}, s32[]{:S(2)}) async-start(s8[16777216]{0:T(1024)(128)(4,1)} %bitcast.7), calls=%async_computation | async-start | bytes 8388608
  86.0 39.3 %slice-start.1 = ((s8[16777216]{0:T(1024)(128)(4,1)}), s8[4194304]{0:T(1024)(128)(4,1)S(1)}, s32[]{:S(2)}) async-start(s8[16777216]{0:T(1024)(128)(4,1)} %bitcast.7), calls=%async_computation.1 | async-start | bytes 8388608
  102.3 19.0 %collective-permute-start.6 = (bf16[256,1152]{1,0:T(8,128)(2,1)S(1)}, bf16[256,1152]{1,0:T(8,128)(2,1)S(1)}, u32[]{:S(2)}, u32[]{:S(2)}) collective-permute-start(bf16[256,1152]{1,0:T(8,128)(2,1)S(1)} %get-tuple-element.33), channel_id=1, source_target_pairs={{0,8},{1,33},{2,10},{3,35},{4,12},{5,37},{6,14},{7,39},{8,16},{9,4... | collective-permute-start | bytes 1769480 | tf_op jit(solution)/shard_map/ppermute | solution.py:57
  102.4 19.0 %collective-permute-start.7 = (bf16[256,1152]{1,0:T(8,128)(2,1)S(1)}, bf16[256,1152]{1,0:T(8,128)(2,1)S(1)}, u32[]{:S(2)}, u32[]{:S(2)}) collective-permute-start(bf16[256,1152]{1,0:T(8,128)(2,1)S(1)} %get-tuple-element.34), channel_id=1, source_target_pairs={{0,24},{1,97},{2,26},{3,99},{4,28},{5,101},{6,30},{7,103},{8,0},{9... | collective-permute-start | bytes 1769480 | tf_op jit(solution)/shard_map/ppermute | solution.py:57
  109.1 16.3 %slice-start.2 = ((s8[16777216]{0:T(1024)(128)(4,1)}), s8[4194304]{0:T(1024)(128)(4,1)S(1)}, s32[]{:S(2)}) async-start(s8[16777216]{0:T(1024)(128)(4,1)} %bitcast.7), calls=%async_computation.2 | async-start | bytes 8388608
  109.1 16.3 %collective-permute-start.8 = (bf16[256,1152]{1,0:T(8,128)(2,1)S(1)}, bf16[256,1152]{1,0:T(8,128)(2,1)S(1)}, u32[]{:S(2)}, u32[]{:S(2)}) collective-permute-start(bf16[256,1152]{1,0:T(8,128)(2,1)S(1)} %get-tuple-element.35), channel_id=1, source_target_pairs={{0,16},{1,65},{2,18},{3,67},{4,20},{5,69},{6,22},{7,71},{8,24},{9,... | collective-permute-start | bytes 1769480 | tf_op jit(solution)/shard_map/ppermute | solution.py:57
  112.9 12.4 %slice-start.3 = ((s8[16777216]{0:T(1024)(128)(4,1)}), s8[4194304]{0:T(1024)(128)(4,1)S(1)}, s32[]{:S(2)}) async-start(s8[16777216]{0:T(1024)(128)(4,1)} %bitcast.7), calls=%async_computation.3 | async-start | bytes 8388608
  131.2 11.2 %collective-permute-start.9 = (bf16[128,4096]{1,0:T(8,128)(2,1)}, bf16[128,4096]{1,0:T(8,128)(2,1)}, u32[]{:S(2)}, u32[]{:S(2)}) collective-permute-start(bf16[128,4096]{1,0:T(8,128)(2,1)} %get-tuple-element.37), channel_id=1, source_target_pairs={{0,1},{1,0},{2,3},{3,2},{4,5},{5,4},{6,7},{7,6},{8,9},{9,8},{10,11... | collective-permute-start | bytes 3145736 | tf_op jit(solution)/shard_map/ppermute | solution.py:57
  142.2 3.9 %collective-permute-start.13 = (bf16[128,4096]{1,0:T(8,128)(2,1)S(1)}, bf16[128,4096]{1,0:T(8,128)(2,1)}, u32[]{:S(2)}, u32[]{:S(2)}) collective-permute-start(bf16[128,4096]{1,0:T(8,128)(2,1)S(1)} %get-tuple-element.40), channel_id=1, source_target_pairs={{0,1},{1,0},{2,3},{3,2},{4,5},{5,4},{6,7},{7,6},{8,9},{9,8},{10,11... | collective-permute-start | bytes 3145736 | tf_op jit(solution)/shard_map/ppermute | solution.py:57
  143.5 18.0 %collective-permute-start.10 = (bf16[32,4096]{1,0:T(8,128)(2,1)S(1)}, bf16[32,4096]{1,0:T(8,128)(2,1)S(1)}, u32[]{:S(2)}, u32[]{:S(2)}) collective-permute-start(bf16[32,4096]{1,0:T(8,128)(2,1)S(1)} %get-tuple-element.45), channel_id=1, source_target_pairs={{0,6},{1,7},{2,0},{3,1},{4,2},{5,3},{6,4},{7,5},{8,14},{9,15},{10,... | collective-permute-start | bytes 786440 | tf_op jit(solution)/shard_map/ppermute | solution.py:57
  146.1 8.4 %collective-permute-start.11 = (bf16[32,4096]{1,0:T(8,128)(2,1)S(1)}, bf16[32,4096]{1,0:T(8,128)(2,1)S(1)}, u32[]{:S(2)}, u32[]{:S(2)}) collective-permute-start(bf16[32,4096]{1,0:T(8,128)(2,1)S(1)} %get-tuple-element.46), channel_id=1, source_target_pairs={{0,2},{1,3},{2,4},{3,5},{4,6},{5,7},{6,0},{7,1},{8,10},{9,11},{10,... | collective-permute-start | bytes 786440 | tf_op jit(solution)/shard_map/ppermute | solution.py:57
  147.2 19.3 %collective-permute-start.14 = (bf16[32,4096]{1,0:T(8,128)(2,1)S(1)}, bf16[32,4096]{1,0:T(8,128)(2,1)S(1)}, u32[]{:S(2)}, u32[]{:S(2)}) collective-permute-start(bf16[32,4096]{1,0:T(8,128)(2,1)S(1)} %get-tuple-element.47), channel_id=1, source_target_pairs={{0,2},{1,3},{2,4},{3,5},{4,6},{5,7},{6,0},{7,1},{8,10},{9,11},{10,... | collective-permute-start | bytes 786440 | tf_op jit(solution)/shard_map/ppermute | solution.py:57
  147.5 9.5 %collective-permute-start.15 = (bf16[32,4096]{1,0:T(8,128)(2,1)S(1)}, bf16[32,4096]{1,0:T(8,128)(2,1)S(1)}, u32[]{:S(2)}, u32[]{:S(2)}) collective-permute-start(bf16[32,4096]{1,0:T(8,128)(2,1)S(1)} %get-tuple-element.48), channel_id=1, source_target_pairs={{0,6},{1,7},{2,0},{3,1},{4,2},{5,3},{6,4},{7,5},{8,14},{9,15},{10,... | collective-permute-start | bytes 786440 | tf_op jit(solution)/shard_map/ppermute | solution.py:57
  155.5 9.9 %collective-permute-start.12 = (bf16[32,4096]{1,0:T(8,128)(2,1)S(1)}, bf16[32,4096]{1,0:T(8,128)(2,1)S(1)}, u32[]{:S(2)}, u32[]{:S(2)}) collective-permute-start(bf16[32,4096]{1,0:T(8,128)(2,1)S(1)} %add_convert_fusion.5), channel_id=1, source_target_pairs={{0,2},{1,3},{2,4},{3,5},{4,6},{5,7},{6,0},{7,1},{8,10},{9,11},{10,... | collective-permute-start | bytes 786440 | tf_op jit(solution)/shard_map/ppermute | solution.py:57
  158.0 8.5 %collective-permute-start.16 = (bf16[32,4096]{1,0:T(8,128)(2,1)S(1)}, bf16[32,4096]{1,0:T(8,128)(2,1)S(1)}, u32[]{:S(2)}, u32[]{:S(2)}) collective-permute-start(bf16[32,4096]{1,0:T(8,128)(2,1)S(1)} %add_convert_fusion.1), channel_id=1, source_target_pairs={{0,6},{1,7},{2,0},{3,1},{4,2},{5,3},{6,4},{7,5},{8,14},{9,15},{10,... | collective-permute-start | bytes 786440 | tf_op jit(solution)/shard_map/ppermute | solution.py:57

commit v3 on v1

--- a/solution.py
+++ b/solution.py
@@ -68,7 +68,8 @@
 
 def attend_kernel(n_home, n_kv, first_kv, resume, final, *refs):
     refs = list(refs)
-    flags = [refs.pop(0) for _ in range(n_home)]
+    segments = refs.pop(0)
+    named = [refs.pop(0) for _ in range(n_home)]
     q_refs = [refs.pop(0) for _ in range(n_home)]
     kv_refs = [refs.pop(0) for _ in range(n_kv)]
     if resume:
@@ -167,15 +168,18 @@
         return carry
 
     per_pass = STEP_ROWS // QB
+    picks = SIDE
 
     def cached(item, carry):
         j, block = item // blocks, item % blocks
-        at = (first_kv + j) * blocks + block
-        hit = flags[0][at]
-        for home in range(1, n_home):
-            hit = jnp.where(home_id == home, flags[home][at], hit)
-
-        @pl.when(hit > 0)
+        segment = segments[first_kv + j]
+        hit = False
+        for home in range(n_home):
+            for pick in range(picks):
+                same = named[home][block * picks + pick] == segment
+                hit = jnp.logical_or(hit, jnp.logical_and(home_id == home, same))
+
+        @pl.when(hit)
         def _():
             rows = pl.ds(pl.multiple_of(block * QB, QB), QB)
             for first in range(0, GROUP, per_pass):
@@ -231,7 +235,7 @@
             pl.when(home_id == home)(functools.partial(emit, outs[home]))
 
 
-def attend(flags, q_list, kv_list, first_kv, state=None, final=False, into=None):
+def attend(segments, named, q_list, kv_list, first_kv, state=None, final=False, into=None, room=61):
     n_home, n_kv = len(q_list), len(kv_list)
     fixed = lambda shape: pl.BlockSpec(shape, lambda i, *f: (0,) * len(shape))
     turn = lambda width, at=0: pl.BlockSpec((NEW, width), lambda i, *f: (i + at, 0))
@@ -253,7 +257,7 @@
         ]
         out_specs = [turn(QW, at), turn(HD, at)]
         if target is not None:
-            aliases = {n_home + len(args): 0, n_home + len(args) + 1: 1}
+            aliases = {n_home + 1 + len(args): 0, n_home + 2 + len(args): 1}
             in_specs += [anywhere, anywhere]
             args += list(target)
     work = n_home * n_kv * NEW * GROUP * (SEG // 4 + NEW)
@@ -261,7 +265,7 @@
         functools.partial(attend_kernel, n_home, n_kv, first_kv, state is not None, final),
         out_shape=out_shape,
         grid_spec=pltpu.PrefetchScalarGridSpec(
-            num_scalar_prefetch=n_home,
+            num_scalar_prefetch=n_home + 1,
             grid=(n_home,),
             in_specs=in_specs,
             out_specs=out_specs,
@@ -277,13 +281,13 @@
             ],
         ),
         input_output_aliases=aliases,
-        compiler_params=pltpu.CompilerParams(vmem_limit_bytes=24 << 20),
+        compiler_params=pltpu.CompilerParams(vmem_limit_bytes=room << 20),
         cost_estimate=pl.CostEstimate(
             flops=work * HD * 4 * 2,
             bytes_accessed=n_home * NEW * QW * 8,
             transcendentals=work,
         ),
-    )(*flags, *args)
+    )(segments, *named, *args)
 
 
 def project_kernel(n_parts, core, *refs):
@@ -354,17 +358,13 @@
             + [pl.BlockSpec((QW, tile), lambda n, c: (0, column * steps + n))],
             out_specs=out_specs,
         ),
-        compiler_params=pltpu.CompilerParams(vmem_limit_bytes=24 << 20),
+        compiler_params=pltpu.CompilerParams(vmem_limit_bytes=63 << 20),
         cost_estimate=pl.CostEstimate(
             flops=4 * NEW * QW * width,
             bytes_accessed=QW * width * 2 + NEW * width * 2,
             transcendentals=0,
         ),
     )(core, *parts, weight)
-
-
-def after(value, *others):
-    return lax.optimization_barrier((value, *others))[0]
 
 
 def per_device(
@@ -393,44 +393,36 @@
     steps = jnp.array(order, jnp.int32)
     along_y = ((y + steps) % SIDE) * SIDE + z
     along_z = y * SIDE + (z + steps) % SIDE
-    segments = jnp.where(core == 0, along_y, along_z).astype(F32)
-
-    def flags_of(row):
-        named = row.astype(F32).reshape(1, NEW // QB, -1)
-        hits = named == segments[:, None, None]
-        return jnp.sum(hits.astype(jnp.int32), axis=-1).reshape(-1)
-
-    flags = {0: flags_of(picks)}
-
-    def read_flags(offsets, done):
-        for o in offsets:
-            flags[o] = flags_of(after(q_at[o][NEW, : picks.shape[0]], *done))
-
-    def run(homes, kvs, state=None, final=False, into=None):
+    segments = jnp.where(core == 0, along_y, along_z)
+
+    lengths = {1: 16, 3: 16, 2: 24}
+    named = {o: q_at[o][NEW, :n].astype(jnp.int32) for o, n in lengths.items()}
+    named[0] = pattern.reshape(-1)
+
+    def run(homes, kvs, state=None, final=False, into=None, room=61):
         offsets = [order[n] for n in homes]
         return attend(
-            [flags[o] for o in offsets],
+            segments,
+            [named[o] for o in offsets],
             [q_at[o] for o in offsets],
             [kv_at[order[n]] for n in kvs],
             kvs[0],
             state,
             final,
             into,
+            room,
         )
 
-    own_state = run((0,), (0,))
+    own_state = run((0,), (0,), room=24)
     for shift in (1, 3):
-        kv_at[-shift % SIDE] = move(after(kv_own, *own_state), "k", shift)
-    read_flags((1, 3), own_state)
+        kv_at[-shift % SIDE] = move(kv_own, "k", shift)
     state = run((1, 2), (0,), into=(3, 0, None))
-    read_flags((2,), state)
     state = run((3,), (0,), into=(3, 2, state))
-    kv_at[2] = move(after(kv_own, *state), "k", 2)
+    kv_at[2] = move(kv_own, "k", 2)
     state = run((1, 2, 3), (1, 2), state)
     partials = run((1, 2, 3), (3,), state, True)
     backs = [move(part, "q", order[n]) for n, part in zip((1, 2, 3), partials)]
-    own_state = [after(value, *partials) for value in own_state]
-    mine = run((0,), (1, 2, 3), own_state, True)
+    mine = run((0,), (1, 2, 3), own_state, True, room=24)
 
     core_id = core.reshape(1)
     keep0, send0, att = project(core_id, [*mine, *backs], out_weight, 0, 2)

time: 159 us -> 162 us (1.019)
  Pallas kernels: 70.4 us -> 85.4 us
  local copies, waits for them, and re-layouts: 14.7 us -> 3.85 us
  starting transfers between devices: 44 us -> 36.9 us
  waiting for transfers between devices: 17.2 us -> 22 us
    pallas_call x6, Pallas kernels: 61.1 us -> 70.2 us  [attend(): pl.pallas_call(functools.partial(attend_kernel, n_home, n_kv, first_kv, s...]
    unnamed x42 -> x32, local copies, waits for them, and re-layouts: 11.7 us -> 2.83 us
    ppermute x17, starting transfers between devices: 44 us -> 36.9 us  [move(): return lax.ppermute(value, AXES, pairs(kind, shift))]
    pallas_call x2, Pallas kernels: 9.32 us -> 15.2 us  [project(): pl.pallas_call(functools.partial(project_kernel, 0 if merged else len(par...]
    ppermute x17, waiting for transfers between devices: 17.2 us -> 22 us  [move(): return lax.ppermute(value, AXES, pairs(kind, shift))]
    convert_element_type x2 -> x4, other arithmetic: 0.7 us -> 3.64 us  [the longest x3 3.63 us: per_device(): named = {o: q_at[o][NEW, :n].astype(jnp.int32) for o, n in lengths.items()}]
    squeeze x3 -> x0, local copies, waits for them, and re-layouts: 2.05 us -> none  [read_flags(): flags[o] = flags_of(after(q_at[o][NEW, :picks.shape[0]], *done))]
  transfers between devices with their start and end apart: 17 -> 17, of which waited for: 6 -> 6; matrix products, arithmetic and copies ran while one was open for 6% -> 5% of each run, Pallas kernels for 31% -> 37%
where the time goes in v3:
time: 162 us; the launch traced here: 159 us
  Pallas kernels  85.4 us (53%)
  starting transfers between devices  36.9 us (23%)
  waiting for transfers between devices  22 us (14%)
  other arithmetic  10.8 us (7%)
  local copies, waits for them, and re-layouts  3.85 us (2%)
    pallas_call x6, Pallas kernels, attend(): pl.pallas_call(functools.partial(attend_kernel, n_home, n_kv, first_kv, s...  70.2 us
    ppermute x17, starting transfers between devices, move(): return lax.ppermute(value, AXES, pairs(kind, shift))  36.9 us
    ppermute x17, waiting for transfers between devices, move(): return lax.ppermute(value, AXES, pairs(kind, shift))  22 us
    pallas_call x2, Pallas kernels, project(): pl.pallas_call(functools.partial(project_kernel, 0 if merged else len(par...  15.2 us
    convert_element_type x3, other arithmetic, per_device(): named = {o: q_at[o][NEW, :n].astype(jnp.int32) for o, n in lengths.items()}  3.63 us
  transfers between devices with their start and end apart: 17, of which 6 were waited for; matrix products, arithmetic and copies ran while one was open for 5% of the time, Pallas kernels for 37%

profile of v3, /device:TPU:1, one launch (start us, length us, event | category | flops | bytes accessed | tf_op | source)
XLA Modules:
  0.0 159.3 jit_solution(18048879459326494643)
XLA Ops:
  0.0 0.8 and_select_fusion.3
  0.8 0.1 copy.19
  0.9 0.8 reshape.20.refs_1_
  1.7 0.1 reshape.21
  1.8 0.0 copy-start.10
  1.8 1.2 fusion.4.refs_2_
  3.0 0.0 copy-start.12
  3.0 2.2 %collective-permute-start.4 = (bf16[272,1152]{1,0:T(8,128)(2,1)S(1)}, bf16[272,1152]{1,0:T(8,128)(2,1)}, u32[]{:S(2)}, u32[]{:S(2)}) collective-permute-start(bf16[272,1152]{1,0:T(8,128)(2,1)S(1)} %fusion.4.refs_2_), channel_id=1, source_target_pairs={{0,8},{1,33},{2,10},{3,35},{4,12},{5,37},{6,14},{7,39},{8,16},{9,4... | collective-permute-start | bytes 1880072 | tf_op jit(solution)/shard_map/ppermute | solution.py:57
  5.2 1.5 collective-permute-start.3
  6.7 1.6 collective-permute-start.5
  8.3 0.1 constant_dynamic-update-slice_fusion.2
  8.5 3.8 %collective-permute-start = (bf16[4624,128]{1,0:T(8,128)(2,1)S(1)}, bf16[4624,128]{1,0:T(8,128)(2,1)S(1)}, u32[]{:S(2)}, u32[]{:S(2)}) collective-permute-start(bf16[4624,128]{1,0:T(8,128)(2,1)S(1)} %constant_dynamic-update-slice_fusion.refs_3_.refs_5_), channel_id=1, source_target_pairs={{0,96},{1,25},{2,98},{3,27},{4,100},{5,29},{6,102},{7,31},{8,104},... | collective-permute-start | bytes 3551240 | tf_op jit(solution)/shard_map/ppermute | solution.py:57
  12.3 0.0 collective-permute-start.1
  12.3 0.6 broadcast_select_fusion.refs_0_
  12.9 1.8 %collective-permute-done.4.refs_4_.refs_5_ = bf16[272,1152]{1,0:T(8,128)(2,1)} collective-permute-done((bf16[272,1152]{1,0:T(8,128)(2,1)S(1)}, bf16[272,1152]{1,0:T(8,128)(2,1)}, u32[]{:S(2)}, u32[]{:S(2)}) %collective-permute-start.4) | collective-permute-done | bytes 626720 | tf_op jit(solution)/shard_map/ppermute | solution.py:57
  14.7 3.3 %collective-permute-start.2 = (bf16[4624,128]{1,0:T(8,128)(2,1)S(1)}, bf16[4624,128]{1,0:T(8,128)(2,1)}, u32[]{:S(2)}, u32[]{:S(2)}) collective-permute-start(bf16[4624,128]{1,0:T(8,128)(2,1)S(1)} %constant_dynamic-update-slice_fusion.refs_3_.refs_5_), channel_id=1, source_target_pairs={{0,64},{1,17},{2,66},{3,19},{4,68},{5,21},{6,70},{7,23},{8,72},{9,... | collective-permute-start | bytes 3551240 | tf_op jit(solution)/shard_map/ppermute | solution.py:57
  18.0 1.2 fusion.12.refs_2_
  19.2 0.0 collective-permute-done.3.refs_3_.refs_4_
  19.2 1.2 fusion.13.refs_1_
  20.4 11.0 %shard_map.93 = (f32[768,1024]{1,0:T(8,128)}, f32[768,128]{1,0:T(8,128)}) custom-call(s32[4]{0:T(128)} %broadcast_select_fusion.refs_0_, s32[16]{0:T(128)} %fusion.13.refs_1_, s32[16]{0:T(128)} %fusion.12.refs_2_, bf16[272,1152]{1,0:T(8,128)(2,1)} %collective-permute-done.3.refs_3_.refs_4_, bf16[272,1152]{1,0:T(8,128)(2,1)} %collective-permute-done.4.refs_4_.refs_5_, ...), custom_call_target="tpu_custom_call" | custom-call | flops 3221225472 | bytes 4194304 | tf_op jit(solution)/shard_map/pallas_call | solution.py:264
  31.4 0.0 collective-permute-done.5.refs_2_.refs_6_
  31.4 1.2 fusion.11.refs_1_.refs_3_
  32.6 7.1 %shard_map.94 = (f32[768,1024]{1,0:T(8,128)}, f32[768,128]{1,0:T(8,128)}) custom-call(s32[4]{0:T(128)} %broadcast_select_fusion.refs_0_, s32[24]{0:T(128)} %fusion.11.refs_1_.refs_3_, bf16[272,1152]{1,0:T(8,128)(2,1)} %collective-permute-done.5.refs_2_.refs_6_, bf16[4624,128]{1,0:T(8,128)(2,1)} %copy-done.1, ...), custom_call_target="tpu_custom_call", output_to_operand_aliasing={{0}: (4, {}), {1}: (5, {})} | custom-call | flops 1610612736 | bytes 2097152 | tf_op jit(solution)/shard_map/pallas_call | solution.py:264
  39.7 8.5 %collective-permute-done.refs_3_.refs_7_ = bf16[4624,128]{1,0:T(8,128)(2,1)S(1)} collective-permute-done((bf16[4624,128]{1,0:T(8,128)(2,1)S(1)}, bf16[4624,128]{1,0:T(8,128)(2,1)S(1)}, u32[]{:S(2)}, u32[]{:S(2)}) %collective-permute-start) | collective-permute-done | bytes 1183776 | tf_op jit(solution)/shard_map/ppermute | solution.py:57
  48.1 0.0 collective-permute-done.1.refs_4_.refs_8_
  48.1 1.0 copy-done.4
  49.2 21.8 %shard_map.95 = (f32[768,1024]{1,0:T(8,128)}, f32[768,128]{1,0:T(8,128)}) custom-call(s32[4]{0:T(128)} %broadcast_select_fusion.refs_0_, s32[16]{0:T(128)} %fusion.13.refs_1_, s32[16]{0:T(128)} %fusion.12.refs_2_, s32[24]{0:T(128)} %fusion.11.refs_1_.refs_3_, bf16[272,1152]{1,0:T(8,128)(2,1)} %collective-permute-done.3.refs_3_.refs_4_, ...), custom_call_target="tpu_custom_call" | custom-call | flops 9663676416 | bytes 6291456 | tf_op jit(solution)/shard_map/pallas_call | solution.py:264
  70.9 0.0 collective-permute-done.2.refs_5_.refs_7_
  71.0 17.4 %shard_map.96 = (bf16[256,1152]{1,0:T(8,128)(2,1)}, bf16[256,1152]{1,0:T(8,128)(2,1)}, bf16[256,1152]{1,0:T(8,128)(2,1)}) custom-call(s32[4]{0:T(128)} %broadcast_select_fusion.refs_0_, s32[16]{0:T(128)} %fusion.13.refs_1_, s32[16]{0:T(128)} %fusion.12.refs_2_, s32[24]{0:T(128)} %fusion.11.refs_1_.refs_3_, ...), custom_call_target="tpu_custom_call" | custom-call | flops 4831838208 | bytes 6291456 | tf_op jit(solution)/shard_map/pallas_call | solution.py:264
  88.4 3.1 %collective-permute-start.6 = (bf16[256,1152]{1,0:T(8,128)(2,1)}, bf16[256,1152]{1,0:T(8,128)(2,1)S(1)}, u32[]{:S(2)}, u32[]{:S(2)}) collective-permute-start(bf16[256,1152]{1,0:T(8,128)(2,1)} %get-tuple-element.29), channel_id=1, source_target_pairs={{0,8},{1,33},{2,10},{3,35},{4,12},{5,37},{6,14},{7,39},{8,16},{9,4... | collective-permute-start | bytes 1769480 | tf_op jit(solution)/shard_map/ppermute | solution.py:57
  91.5 1.5 collective-permute-start.7
  93.0 8.4 %collective-permute-start.8 = (bf16[256,1152]{1,0:T(8,128)(2,1)}, bf16[256,1152]{1,0:T(8,128)(2,1)}, u32[]{:S(2)}, u32[]{:S(2)}) collective-permute-start(bf16[256,1152]{1,0:T(8,128)(2,1)} %get-tuple-element.31), channel_id=1, source_target_pairs={{0,16},{1,65},{2,18},{3,67},{4,20},{5,69},{6,22},{7,71},{8,24},{9,... | collective-permute-start | bytes 1769480 | tf_op jit(solution)/shard_map/ppermute | solution.py:57
  101.3 4.3 %shard_map.91 = (f32[256,1024]{1,0:T(8,128)S(1)}, f32[256,128]{1,0:T(8,128)S(1)}) custom-call(s32[4]{0:T(128)S(1)} %copy-done.3, s32[16]{0:T(128)S(1)} %reshape.20.refs_1_, bf16[272,1152]{1,0:T(8,128)(2,1)S(1)} %fusion.4.refs_2_, bf16[4624,128]{1,0:T(8,128)(2,1)S(1)} %copy-done.2), custom_call_target="tpu_custom_call" | custom-call | flops 1610612736 | bytes 2097152 | tf_op jit(solution)/shard_map/pallas_call | solution.py:264
  105.7 8.6 %shard_map.92.refs_0_ = bf16[256,1152]{1,0:T(8,128)(2,1)S(1)} custom-call(s32[4]{0:T(128)S(1)} %copy-done.3, s32[16]{0:T(128)S(1)} %reshape.20.refs_1_, bf16[272,1152]{1,0:T(8,128)(2,1)S(1)} %fusion.4.refs_2_, bf16[4624,128]{1,0:T(8,128)(2,1)S(1)} %copy-done.5, bf16[4624,128]{1,0:T(8,128)(2,1)} %collective-permute-done.1.refs_4_.refs_8_, ...), custom_call_target="tpu_custom_call" | custom-call | flops 4831838208 | bytes 2097152 | tf_op jit(solution)/shard_map/pallas_call | solution.py:264
  114.3 0.8 copy-done
  115.2 0.0 collective-permute-done.6.refs_1_
  115.2 0.0 collective-permute-done.7.refs_2_
  115.2 0.0 collective-permute-done.8.refs_3_
  115.2 0.8 copy-done.8
  116.0 8.6 %shard_map.97 = (bf16[128,4096]{1,0:T(8,128)(2,1)}, bf16[128,4096]{1,0:T(8,128)(2,1)}, bf16[256,1024]{1,0:T(8,128)(2,1)}) custom-call(s32[1]{0:T(128)} %bitcast.core, bf16[256,1152]{1,0:T(8,128)(2,1)} %copy-done, bf16[256,1152]{1,0:T(8,128)(2,1)} %copy-done.8, bf16[256,1152]{1,0:T(8,128)(2,1)} %collective-permute-done.7.refs_2_, ...), custom_call_target="tpu_custom_call" | custom-call | flops 4294967296 | bytes 10485760 | tf_op jit(solution)/shard_map/pallas_call | solution.py:351
  124.6 4.4 %collective-permute-start.9 = (bf16[128,4096]{1,0:T(8,128)(2,1)}, bf16[128,4096]{1,0:T(8,128)(2,1)}, u32[]{:S(2)}, u32[]{:S(2)}) collective-permute-start(bf16[128,4096]{1,0:T(8,128)(2,1)} %get-tuple-element.33), channel_id=1, source_target_pairs={{0,1},{1,0},{2,3},{3,2},{4,5},{5,4},{6,7},{7,6},{8,9},{9,8},{10,11... | collective-permute-start | bytes 3145736 | tf_op jit(solution)/shard_map/ppermute | solution.py:57
  129.0 6.6 %shard_map.98 = (bf16[128,4096]{1,0:T(8,128)(2,1)}, bf16[128,4096]{1,0:T(8,128)(2,1)}) custom-call(s32[1]{0:T(128)} %bitcast.core, bf16[256,1024]{1,0:T(8,128)(2,1)} %get-tuple-element.34.refs_0_, bf16[1024,8192]{1,0:T(8,128)(2,1)} %refs_1_.1), custom_call_target="tpu_custom_call" | custom-call | flops 4294967296 | bytes 10485760 | tf_op jit(solution)/shard_map/pallas_call | solution.py:351
  135.6 0.0 collective-permute-start.13
  135.7 0.0 collective-permute-done.9
  135.7 1.4 add_convert_fusion.7
  137.1 1.3 collective-permute-start.11
  138.4 1.5 collective-permute-start.10
  139.8 0.0 collective-permute-done.13
  139.8 0.1 add_convert_fusion.3
  140.0 1.3 collective-permute-start.15
  141.3 0.2 collective-permute-start.14
  141.5 4.4 %collective-permute-done.11 = bf16[32,4096]{1,0:T(8,128)(2,1)S(1)} collective-permute-done((bf16[32,4096]{1,0:T(8,128)(2,1)S(1)}, bf16[32,4096]{1,0:T(8,128)(2,1)S(1)}, u32[]{:S(2)}, u32[]{:S(2)}) %collective-permute-start.11) | collective-permute-done | bytes 262176 | tf_op jit(solution)/shard_map/ppermute | solution.py:57
  145.9 1.0 add_convert_fusion.5
  146.9 0.1 collective-permute-start.12
  147.0 4.2 %collective-permute-done.15 = bf16[32,4096]{1,0:T(8,128)(2,1)S(1)} collective-permute-done((bf16[32,4096]{1,0:T(8,128)(2,1)S(1)}, bf16[32,4096]{1,0:T(8,128)(2,1)S(1)}, u32[]{:S(2)}, u32[]{:S(2)}) %collective-permute-start.15) | collective-permute-done | bytes 262176 | tf_op jit(solution)/shard_map/ppermute | solution.py:57
  151.2 0.1 add_convert_fusion.1
  151.3 2.7 %collective-permute-start.16 = (bf16[32,4096]{1,0:T(8,128)(2,1)S(1)}, bf16[32,4096]{1,0:T(8,128)(2,1)S(1)}, u32[]{:S(2)}, u32[]{:S(2)}) collective-permute-start(bf16[32,4096]{1,0:T(8,128)(2,1)S(1)} %add_convert_fusion.1), channel_id=1, source_target_pairs={{0,6},{1,7},{2,0},{3,1},{4,2},{5,3},{6,4},{7,5},{8,14},{9,15},{10,... | collective-permute-start | bytes 786440 | tf_op jit(solution)/shard_map/ppermute | solution.py:57
  154.1 0.0 collective-permute-done.10
  154.1 2.8 %collective-permute-done.12 = bf16[32,4096]{1,0:T(8,128)(2,1)S(1)} collective-permute-done((bf16[32,4096]{1,0:T(8,128)(2,1)S(1)}, bf16[32,4096]{1,0:T(8,128)(2,1)S(1)}, u32[]{:S(2)}, u32[]{:S(2)}) %collective-permute-start.12) | collective-permute-done | bytes 262176 | tf_op jit(solution)/shard_map/ppermute | solution.py:57
  156.9 1.1 add_convert_fusion.4
  157.9 0.0 collective-permute-done.14
  158.0 0.3 collective-permute-done.16
  158.3 0.1 add_convert_fusion
  158.4 0.8 pad_maximum_fusion
  (31 shorter events, 0.2 us)
Async XLA Ops:
  0.0 8.3 %copy-start.9 = (bf16[2048,128]{1,0:T(8,128)(2,1)S(1)}, bf16[2048,128]{1,0:T(8,128)(2,1)}, u32[]{:S(2)}) copy-start(bf16[2048,128]{1,0:T(8,128)(2,1)} %param.13) | copy-start | bytes 1572868
  1.7 6.6 %copy-start.11 = (bf16[256,128]{1,0:T(8,128)(2,1)S(1)}, bf16[256,128]{1,0:T(8,128)(2,1)}, u32[]{:S(2)}) copy-start(bf16[256,128]{1,0:T(8,128)(2,1)} %param.10) | copy-start | bytes 196612
  1.8 6.5 %copy-start.10 = (bf16[2048,128]{1,0:T(8,128)(2,1)S(1)}, bf16[2048,128]{1,0:T(8,128)(2,1)}, u32[]{:S(2)}) copy-start(bf16[2048,128]{1,0:T(8,128)(2,1)} %param.14) | copy-start | bytes 1572868
  3.0 5.5 %copy-start.12 = (bf16[256,128]{1,0:T(8,128)(2,1)S(1)}, bf16[256,128]{1,0:T(8,128)(2,1)}, u32[]{:S(2)}) copy-start(bf16[256,128]{1,0:T(8,128)(2,1)} %param.11) | copy-start | bytes 196612
  3.0 11.7 %collective-permute-start.4 = (bf16[272,1152]{1,0:T(8,128)(2,1)S(1)}, bf16[272,1152]{1,0:T(8,128)(2,1)}, u32[]{:S(2)}, u32[]{:S(2)}) collective-permute-start(bf16[272,1152]{1,0:T(8,128)(2,1)S(1)} %fusion.4.refs_2_), channel_id=1, source_target_pairs={{0,8},{1,33},{2,10},{3,35},{4,12},{5,37},{6,14},{7,39},{8,16},{9,4... | collective-permute-start | bytes 1880072 | tf_op jit(solution)/shard_map/ppermute | solution.py:57
  5.2 14.0 %collective-permute-start.3 = (bf16[272,1152]{1,0:T(8,128)(2,1)S(1)}, bf16[272,1152]{1,0:T(8,128)(2,1)}, u32[]{:S(2)}, u32[]{:S(2)}) collective-permute-start(bf16[272,1152]{1,0:T(8,128)(2,1)S(1)} %fusion.4.refs_2_), channel_id=1, source_target_pairs={{0,24},{1,97},{2,26},{3,99},{4,28},{5,101},{6,30},{7,103},{8,0},{9... | collective-permute-start | bytes 1880072 | tf_op jit(solution)/shard_map/ppermute | solution.py:57
  6.7 24.7 %collective-permute-start.5 = (bf16[272,1152]{1,0:T(8,128)(2,1)S(1)}, bf16[272,1152]{1,0:T(8,128)(2,1)}, u32[]{:S(2)}, u32[]{:S(2)}) collective-permute-start(bf16[272,1152]{1,0:T(8,128)(2,1)S(1)} %fusion.4.refs_2_), channel_id=1, source_target_pairs={{0,16},{1,65},{2,18},{3,67},{4,20},{5,69},{6,22},{7,71},{8,24},{9,... | collective-permute-start | bytes 1880072 | tf_op jit(solution)/shard_map/ppermute | solution.py:57
  8.3 4.0 %copy-start.13 = (s32[4]{0:T(128)S(1)}, s32[4]{0:T(128)}, u32[]{:S(2)}) copy-start(s32[4]{0:T(128)} %constant.141.clone) | copy-start | bytes 52
  8.5 11.9 %copy-start.1 = (bf16[4624,128]{1,0:T(8,128)(2,1)}, bf16[4624,128]{1,0:T(8,128)(2,1)S(1)}, u32[]{:S(2)}) copy-start(bf16[4624,128]{1,0:T(8,128)(2,1)S(1)} %constant_dynamic-update-slice_fusion.refs_3_.refs_5_) | copy-start | bytes 3551236
  8.5 39.7 %collective-permute-start = (bf16[4624,128]{1,0:T(8,128)(2,1)S(1)}, bf16[4624,128]{1,0:T(8,128)(2,1)S(1)}, u32[]{:S(2)}, u32[]{:S(2)}) collective-permute-start(bf16[4624,128]{1,0:T(8,128)(2,1)S(1)} %constant_dynamic-update-slice_fusion.refs_3_.refs_5_), channel_id=1, source_target_pairs={{0,96},{1,25},{2,98},{3,27},{4,100},{5,29},{6,102},{7,31},{8,104},... | collective-permute-start | bytes 3551240 | tf_op jit(solution)/shard_map/ppermute | solution.py:57
  12.3 35.8 %collective-permute-start.1 = (bf16[4624,128]{1,0:T(8,128)(2,1)S(1)}, bf16[4624,128]{1,0:T(8,128)(2,1)}, u32[]{:S(2)}, u32[]{:S(2)}) collective-permute-start(bf16[4624,128]{1,0:T(8,128)(2,1)S(1)} %constant_dynamic-update-slice_fusion.refs_3_.refs_5_), channel_id=1, source_target_pairs={{0,32},{1,9},{2,34},{3,11},{4,36},{5,13},{6,38},{7,15},{8,40},{9,1... | collective-permute-start | bytes 3551240 | tf_op jit(solution)/shard_map/ppermute | solution.py:57
  14.7 56.3 %collective-permute-start.2 = (bf16[4624,128]{1,0:T(8,128)(2,1)S(1)}, bf16[4624,128]{1,0:T(8,128)(2,1)}, u32[]{:S(2)}, u32[]{:S(2)}) collective-permute-start(bf16[4624,128]{1,0:T(8,128)(2,1)S(1)} %constant_dynamic-update-slice_fusion.refs_3_.refs_5_), channel_id=1, source_target_pairs={{0,64},{1,17},{2,66},{3,19},{4,68},{5,21},{6,70},{7,23},{8,72},{9,... | collective-permute-start | bytes 3551240 | tf_op jit(solution)/shard_map/ppermute | solution.py:57
  48.1 1.0 copy-start.4
  70.9 30.4 %copy-start.2 = (bf16[4624,128]{1,0:T(8,128)(2,1)S(1)}, bf16[4624,128]{1,0:T(8,128)(2,1)}, u32[]{:S(2)}) copy-start(bf16[4624,128]{1,0:T(8,128)(2,1)} %copy-done.1) | copy-start | bytes 3551236
  71.0 30.4 %copy-start.3 = (s32[4]{0:T(128)S(1)}, s32[4]{0:T(128)}, u32[]{:S(2)}) copy-start(s32[4]{0:T(128)} %broadcast_select_fusion.refs_0_) | copy-start | bytes 52
  88.4 26.8 %collective-permute-start.6 = (bf16[256,1152]{1,0:T(8,128)(2,1)}, bf16[256,1152]{1,0:T(8,128)(2,1)S(1)}, u32[]{:S(2)}, u32[]{:S(2)}) collective-permute-start(bf16[256,1152]{1,0:T(8,128)(2,1)} %get-tuple-element.29), channel_id=1, source_target_pairs={{0,8},{1,33},{2,10},{3,35},{4,12},{5,37},{6,14},{7,39},{8,16},{9,4... | collective-permute-start | bytes 1769480 | tf_op jit(solution)/shard_map/ppermute | solution.py:57
  91.5 23.7 %collective-permute-start.7 = (bf16[256,1152]{1,0:T(8,128)(2,1)}, bf16[256,1152]{1,0:T(8,128)(2,1)}, u32[]{:S(2)}, u32[]{:S(2)}) collective-permute-start(bf16[256,1152]{1,0:T(8,128)(2,1)} %get-tuple-element.30), channel_id=1, source_target_pairs={{0,24},{1,97},{2,26},{3,99},{4,28},{5,101},{6,30},{7,103},{8,0},{9... | collective-permute-start | bytes 1769480 | tf_op jit(solution)/shard_map/ppermute | solution.py:57
  93.0 12.7 %copy-start.5 = (bf16[4624,128]{1,0:T(8,128)(2,1)S(1)}, bf16[4624,128]{1,0:T(8,128)(2,1)}, u32[]{:S(2)}) copy-start(bf16[4624,128]{1,0:T(8,128)(2,1)} %copy-done.4) | copy-start | bytes 3551236
  93.0 22.2 %collective-permute-start.8 = (bf16[256,1152]{1,0:T(8,128)(2,1)}, bf16[256,1152]{1,0:T(8,128)(2,1)}, u32[]{:S(2)}, u32[]{:S(2)}) collective-permute-start(bf16[256,1152]{1,0:T(8,128)(2,1)} %get-tuple-element.31), channel_id=1, source_target_pairs={{0,16},{1,65},{2,18},{3,67},{4,20},{5,69},{6,22},{7,71},{8,24},{9,... | collective-permute-start | bytes 1769480 | tf_op jit(solution)/shard_map/ppermute | solution.py:57
  114.3 0.8 copy-start
  115.2 0.8 copy-start.8
  124.6 11.1 %collective-permute-start.9 = (bf16[128,4096]{1,0:T(8,128)(2,1)}, bf16[128,4096]{1,0:T(8,128)(2,1)}, u32[]{:S(2)}, u32[]{:S(2)}) collective-permute-start(bf16[128,4096]{1,0:T(8,128)(2,1)} %get-tuple-element.33), channel_id=1, source_target_pairs={{0,1},{1,0},{2,3},{3,2},{4,5},{5,4},{6,7},{7,6},{8,9},{9,8},{10,11... | collective-permute-start | bytes 3145736 | tf_op jit(solution)/shard_map/ppermute | solution.py:57
  135.6 4.3 %copy-start.6 = (bf16[128,4096]{1,0:T(8,128)(2,1)S(1)}, bf16[128,4096]{1,0:T(8,128)(2,1)}, u32[]{:S(2)}) copy-start(bf16[128,4096]{1,0:T(8,128)(2,1)} %get-tuple-element.35) | copy-start | bytes 3145732
  135.6 4.3 %collective-permute-start.13 = (bf16[128,4096]{1,0:T(8,128)(2,1)}, bf16[128,4096]{1,0:T(8,128)(2,1)S(1)}, u32[]{:S(2)}, u32[]{:S(2)}) collective-permute-start(bf16[128,4096]{1,0:T(8,128)(2,1)} %get-tuple-element.36), channel_id=1, source_target_pairs={{0,1},{1,0},{2,3},{3,2},{4,5},{5,4},{6,7},{7,6},{8,9},{9,8},{10,11... | collective-permute-start | bytes 3145736 | tf_op jit(solution)/shard_map/ppermute | solution.py:57
  137.1 8.8 %copy-start.7 = (bf16[128,4096]{1,0:T(8,128)(2,1)S(1)}, bf16[128,4096]{1,0:T(8,128)(2,1)}, u32[]{:S(2)}) copy-start(bf16[128,4096]{1,0:T(8,128)(2,1)} %get-tuple-element.32) | copy-start | bytes 3145732
  137.1 8.8 %collective-permute-start.11 = (bf16[32,4096]{1,0:T(8,128)(2,1)S(1)}, bf16[32,4096]{1,0:T(8,128)(2,1)S(1)}, u32[]{:S(2)}, u32[]{:S(2)}) collective-permute-start(bf16[32,4096]{1,0:T(8,128)(2,1)S(1)} %get-tuple-element.38), channel_id=1, source_target_pairs={{0,2},{1,3},{2,4},{3,5},{4,6},{5,7},{6,0},{7,1},{8,10},{9,11},{10,... | collective-permute-start | bytes 786440 | tf_op jit(solution)/shard_map/ppermute | solution.py:57
  138.4 15.7 %collective-permute-start.10 = (bf16[32,4096]{1,0:T(8,128)(2,1)S(1)}, bf16[32,4096]{1,0:T(8,128)(2,1)S(1)}, u32[]{:S(2)}, u32[]{:S(2)}) collective-permute-start(bf16[32,4096]{1,0:T(8,128)(2,1)S(1)} %get-tuple-element.37), channel_id=1, source_target_pairs={{0,6},{1,7},{2,0},{3,1},{4,2},{5,3},{6,4},{7,5},{8,14},{9,15},{10,... | collective-permute-start | bytes 786440 | tf_op jit(solution)/shard_map/ppermute | solution.py:57
  140.0 11.3 %collective-permute-start.15 = (bf16[32,4096]{1,0:T(8,128)(2,1)S(1)}, bf16[32,4096]{1,0:T(8,128)(2,1)S(1)}, u32[]{:S(2)}, u32[]{:S(2)}) collective-permute-start(bf16[32,4096]{1,0:T(8,128)(2,1)S(1)} %get-tuple-element.40), channel_id=1, source_target_pairs={{0,6},{1,7},{2,0},{3,1},{4,2},{5,3},{6,4},{7,5},{8,14},{9,15},{10,... | collective-permute-start | bytes 786440 | tf_op jit(solution)/shard_map/ppermute | solution.py:57
  141.3 16.7 %collective-permute-start.14 = (bf16[32,4096]{1,0:T(8,128)(2,1)S(1)}, bf16[32,4096]{1,0:T(8,128)(2,1)S(1)}, u32[]{:S(2)}, u32[]{:S(2)}) collective-permute-start(bf16[32,4096]{1,0:T(8,128)(2,1)S(1)} %get-tuple-element.39), channel_id=1, source_target_pairs={{0,2},{1,3},{2,4},{3,5},{4,6},{5,7},{6,0},{7,1},{8,10},{9,11},{10,... | collective-permute-start | bytes 786440 | tf_op jit(solution)/shard_map/ppermute | solution.py:57
  146.9 9.9 %collective-permute-start.12 = (bf16[32,4096]{1,0:T(8,128)(2,1)S(1)}, bf16[32,4096]{1,0:T(8,128)(2,1)S(1)}, u32[]{:S(2)}, u32[]{:S(2)}) collective-permute-start(bf16[32,4096]{1,0:T(8,128)(2,1)S(1)} %add_convert_fusion.5), channel_id=1, source_target_pairs={{0,2},{1,3},{2,4},{3,5},{4,6},{5,7},{6,0},{7,1},{8,10},{9,11},{10,... | collective-permute-start | bytes 786440 | tf_op jit(solution)/shard_map/ppermute | solution.py:57
  151.3 6.9 %collective-permute-start.16 = (bf16[32,4096]{1,0:T(8,128)(2,1)S(1)}, bf16[32,4096]{1,0:T(8,128)(2,1)S(1)}, u32[]{:S(2)}, u32[]{:S(2)}) collective-permute-start(bf16[32,4096]{1,0:T(8,128)(2,1)S(1)} %add_convert_fusion.1), channel_id=1, source_target_pairs={{0,6},{1,7},{2,0},{3,1},{4,2},{5,3},{6,4},{7,5},{8,14},{9,15},{10,... | collective-permute-start | bytes 786440 | tf_op jit(solution)/shard_map/ppermute | solution.py:57

commit v4 on v1

--- a/solution.py
+++ b/solution.py
@@ -71,8 +71,7 @@
     flags = [refs.pop(0) for _ in range(n_home)]
     q_refs = [refs.pop(0) for _ in range(n_home)]
     kv_refs = [refs.pop(0) for _ in range(n_kv)]
-    if resume:
-        acc_in, ml_in = refs.pop(0), refs.pop(0)
+    saved = [(refs.pop(0), refs.pop(0)) for _ in resume]
     if final:
         outs = [refs.pop(0) for _ in range(n_home)]
     else:
@@ -111,17 +110,26 @@
             def _(home=home):
                 q_scr[...] = q_refs[home][...]
 
-    for h in range(GROUP):
-        cols = slice(h * HD, (h + 1) * HD)
-        if resume:
+    def load(acc_in, ml_in):
+        for h in range(GROUP):
+            cols = slice(h * HD, (h + 1) * HD)
             m_scr[:, cols] = jnp.broadcast_to(ml_in[:, h : h + 1], (tokens, HD))
             acc_scr[:, h * 2 * HD : h * 2 * HD + HD] = acc_in[:, cols]
             acc_scr[:, h * 2 * HD + HD : (h + 1) * 2 * HD] = jnp.broadcast_to(
                 ml_in[:, GROUP + h : GROUP + h + 1], (tokens, HD)
             )
-        else:
-            m_scr[:, cols] = jnp.full((tokens, HD), NEG, F32)
-            acc_scr[:, h * 2 * HD : (h + 1) * 2 * HD] = jnp.zeros((tokens, 2 * HD), F32)
+
+    if not saved:
+        m_scr[...] = jnp.full((tokens, QW), NEG, F32)
+        acc_scr[...] = jnp.zeros((tokens, 2 * QW), F32)
+    elif len(saved) == 1:
+        load(*saved[0])
+    else:
+        start = 0
+        for count, arrays in zip(resume, saved):
+            inside = jnp.logical_and(home_id >= start, home_id < start + count)
+            pl.when(inside)(functools.partial(load, *arrays))
+            start += count
 
     @pl.when(home_id == 0)
     def _():
@@ -231,34 +239,33 @@
             pl.when(home_id == home)(functools.partial(emit, outs[home]))
 
 
-def attend(flags, q_list, kv_list, first_kv, state=None, final=False, into=None):
+def attend(flags, q_list, kv_list, first_kv, state=(), final=False):
     n_home, n_kv = len(q_list), len(kv_list)
     fixed = lambda shape: pl.BlockSpec(shape, lambda i, *f: (0,) * len(shape))
-    turn = lambda width, at=0: pl.BlockSpec((NEW, width), lambda i, *f: (i + at, 0))
-    anywhere = pl.BlockSpec(memory_space=pl.ANY)
-    in_specs = [fixed((NEW, SEND_W))] * n_home + [anywhere] * n_kv
+    turn = lambda width: pl.BlockSpec((NEW, width), lambda i, *f: (i, 0))
+    in_specs = [fixed((NEW, SEND_W))] * n_home + [pl.BlockSpec(memory_space=pl.ANY)] * n_kv
     args = list(q_list) + list(kv_list)
-    aliases = {}
-    if state is not None:
-        in_specs += [turn(QW), turn(HD)]
-        args += list(state)
+    held, start = [], 0
+    for pair in state:
+        count = pair[0].shape[0] // NEW
+        at = lambda i, *f, start=start, count=count: (jnp.clip(i - start, 0, count - 1), 0)
+        in_specs += [pl.BlockSpec((NEW, QW), at), pl.BlockSpec((NEW, HD), at)]
+        args += list(pair)
+        held.append(count)
+        start += count
+    held = tuple(held)
     if final:
         out_shape = [jax.ShapeDtypeStruct((NEW, RET_W), BF)] * n_home
         out_specs = [fixed((NEW, RET_W))] * n_home
     else:
-        places, at, target = into or (n_home, 0, None)
         out_shape = [
-            jax.ShapeDtypeStruct((places * NEW, QW), F32),
-            jax.ShapeDtypeStruct((places * NEW, HD), F32),
+            jax.ShapeDtypeStruct((n_home * NEW, QW), F32),
+            jax.ShapeDtypeStruct((n_home * NEW, HD), F32),
         ]
-        out_specs = [turn(QW, at), turn(HD, at)]
-        if target is not None:
-            aliases = {n_home + len(args): 0, n_home + len(args) + 1: 1}
-            in_specs += [anywhere, anywhere]
-            args += list(target)
+        out_specs = [turn(QW), turn(HD)]
     work = n_home * n_kv * NEW * GROUP * (SEG // 4 + NEW)
     return pl.pallas_call(
-        functools.partial(attend_kernel, n_home, n_kv, first_kv, state is not None, final),
+        functools.partial(attend_kernel, n_home, n_kv, first_kv, held, final),
         out_shape=out_shape,
         grid_spec=pltpu.PrefetchScalarGridSpec(
             num_scalar_prefetch=n_home,
@@ -276,7 +283,6 @@
                 pltpu.SemaphoreType.DMA((n_kv, 3)),
             ],
         ),
-        input_output_aliases=aliases,
         compiler_params=pltpu.CompilerParams(vmem_limit_bytes=24 << 20),
         cost_estimate=pl.CostEstimate(
             flops=work * HD * 4 * 2,
@@ -363,10 +369,6 @@
     )(core, *parts, weight)
 
 
-def after(value, *others):
-    return lax.optimization_barrier((value, *others))[0]
-
-
 def per_device(
     queries, new_keys, new_values, positions, cache_keys, cache_values, pattern, out_weight
 ):
@@ -404,9 +406,10 @@
 
     def read_flags(offsets, done):
         for o in offsets:
-            flags[o] = flags_of(after(q_at[o][NEW, : picks.shape[0]], *done))
-
-    def run(homes, kvs, state=None, final=False, into=None):
+            row = q_at[o][NEW, : picks.shape[0]]
+            flags[o] = flags_of(lax.optimization_barrier((row, *done))[0])
+
+    def run(homes, kvs, state=(), final=False):
         offsets = [order[n] for n in homes]
         return attend(
             [flags[o] for o in offsets],
@@ -415,22 +418,20 @@
             kvs[0],
             state,
             final,
-            into,
         )
 
     own_state = run((0,), (0,))
     for shift in (1, 3):
-        kv_at[-shift % SIDE] = move(after(kv_own, *own_state), "k", shift)
+        kv_at[-shift % SIDE] = move(kv_own, "k", shift)
     read_flags((1, 3), own_state)
-    state = run((1, 2), (0,), into=(3, 0, None))
-    read_flags((2,), state)
-    state = run((3,), (0,), into=(3, 2, state))
-    kv_at[2] = move(after(kv_own, *state), "k", 2)
-    state = run((1, 2, 3), (1, 2), state)
-    partials = run((1, 2, 3), (3,), state, True)
+    close = run((1, 2), (0,))
+    read_flags((2,), close)
+    distant = run((3,), (0,))
+    kv_at[2] = move(kv_own, "k", 2)
+    state = run((1, 2, 3), (1, 2), [close, distant])
+    partials = run((1, 2, 3), (3,), [state], True)
     backs = [move(part, "q", order[n]) for n, part in zip((1, 2, 3), partials)]
-    own_state = [after(value, *partials) for value in own_state]
-    mine = run((0,), (1, 2, 3), own_state, True)
+    mine = run((0,), (1, 2, 3), [own_state], True)
 
     core_id = core.reshape(1)
     keep0, send0, att = project(core_id, [*mine, *backs], out_weight, 0, 2)

time: 159 us -> 163 us (1.025)
  waiting for transfers between devices: 17.2 us -> 32.2 us
  local copies, waits for them, and re-layouts: 14.7 us -> 6.18 us
  starting transfers between devices: 44 us -> 40.3 us
    ppermute x17, waiting for transfers between devices: 17.2 us -> 32.2 us  [move(): return lax.ppermute(value, AXES, pairs(kind, shift))]
    unnamed x42 -> x34, local copies, waits for them, and re-layouts: 11.7 us -> 3.21 us
    ppermute x17, starting transfers between devices: 44 us -> 40.3 us  [move(): return lax.ppermute(value, AXES, pairs(kind, shift))]
  transfers between devices with their start and end apart: 17 -> 17, of which waited for: 6 -> 5; matrix products, arithmetic and copies ran while one was open for 6% -> 6% of each run, Pallas kernels for 31% -> 31%
where the time goes in v4:
time: 163 us; the launch traced here: 161 us
  Pallas kernels  71.3 us (44%)
  starting transfers between devices  40.3 us (25%)
  waiting for transfers between devices  32.2 us (20%)
  other arithmetic  10.8 us (7%)
  local copies, waits for them, and re-layouts  6.18 us (4%)
    pallas_call x6, Pallas kernels, attend(): pl.pallas_call(functools.partial(attend_kernel, n_home, n_kv, first_kv, h...  62 us
    ppermute x17, starting transfers between devices, move(): return lax.ppermute(value, AXES, pairs(kind, shift))  40.3 us
    ppermute x17, waiting for transfers between devices, move(): return lax.ppermute(value, AXES, pairs(kind, shift))  32.2 us
    pallas_call x2, Pallas kernels, project(): pl.pallas_call(functools.partial(project_kernel, 0 if merged else len(par...  9.33 us
  transfers between devices with their start and end apart: 17, of which 5 were waited for; matrix products, arithmetic and copies ran while one was open for 6% of the time, Pallas kernels for 31%

profile of v4, /device:TPU:1, one launch (start us, length us, event | category | flops | bytes accessed | tf_op | source)
XLA Modules:
  0.0 161.2 jit_solution(10294886824242261623)
XLA Ops:
  0.0 0.8 and_select_fusion.3
  0.8 0.7 fusion.12
  1.4 0.1 convert_element_type.139
  1.5 0.1 reshape.37
  1.6 0.0 copy-start.8
  1.6 0.1 copy.19
  1.8 1.2 fusion.4.refs_1_
  3.0 0.0 copy-start.9
  3.0 0.0 copy-start.10
  3.0 3.8 %collective-permute-start.5 = (bf16[272,1152]{1,0:T(8,128)(2,1)S(1)}, bf16[272,1152]{1,0:T(8,128)(2,1)}, u32[]{:S(2)}, u32[]{:S(2)}) collective-permute-start(bf16[272,1152]{1,0:T(8,128)(2,1)S(1)} %fusion.4.refs_1_), channel_id=1, source_target_pairs={{0,16},{1,65},{2,18},{3,67},{4,20},{5,69},{6,22},{7,71},{8,24},{9,... | collective-permute-start | bytes 1880072 | tf_op jit(solution)/shard_map/ppermute | solution.py:57
  6.8 0.4 collective-permute-start.4
  7.2 2.3 %collective-permute-start.3 = (bf16[272,1152]{1,0:T(8,128)(2,1)S(1)}, bf16[272,1152]{1,0:T(8,128)(2,1)}, u32[]{:S(2)}, u32[]{:S(2)}) collective-permute-start(bf16[272,1152]{1,0:T(8,128)(2,1)S(1)} %fusion.4.refs_1_), channel_id=1, source_target_pairs={{0,24},{1,97},{2,26},{3,99},{4,28},{5,101},{6,30},{7,103},{8,0},{9... | collective-permute-start | bytes 1880072 | tf_op jit(solution)/shard_map/ppermute | solution.py:57
  9.6 0.1 constant_dynamic-update-slice_fusion.2
  9.7 3.7 %collective-permute-start.2 = (bf16[4624,128]{1,0:T(8,128)(2,1)S(1)}, bf16[4624,128]{1,0:T(8,128)(2,1)S(1)}, u32[]{:S(2)}, u32[]{:S(2)}) collective-permute-start(bf16[4624,128]{1,0:T(8,128)(2,1)S(1)} %constant_dynamic-update-slice_fusion.refs_2_.refs_4_), channel_id=1, source_target_pairs={{0,64},{1,17},{2,66},{3,19},{4,68},{5,21},{6,70},{7,23},{8,72},{9,... | collective-permute-start | bytes 3551240 | tf_op jit(solution)/shard_map/ppermute | solution.py:57
  13.4 0.7 collective-permute-start.1
  14.1 0.2 convert_reduce_fusion.3
  14.3 0.1 reshape.36.refs_0_
  14.4 4.3 %shard_map.91 = (f32[256,1024]{1,0:T(8,128)S(1)}, f32[256,128]{1,0:T(8,128)S(1)}) custom-call(s32[16]{0:T(128)S(1)} %reshape.36.refs_0_, bf16[272,1152]{1,0:T(8,128)(2,1)S(1)} %fusion.4.refs_1_, bf16[4624,128]{1,0:T(8,128)(2,1)S(1)} %constant_dynamic-update-slice_fusion.refs_2_.refs_4_), custom_call_target="tpu_custom_call" | custom-call | flops 1610612736 | bytes 2097152 | tf_op jit(solution)/shard_map/pallas_call | solution.py:267
  18.7 1.0 copy-done
  19.7 17.9 %collective-permute-done.4.refs_3_.refs_4_ = bf16[272,1152]{1,0:T(8,128)(2,1)} collective-permute-done((bf16[272,1152]{1,0:T(8,128)(2,1)S(1)}, bf16[272,1152]{1,0:T(8,128)(2,1)}, u32[]{:S(2)}, u32[]{:S(2)}) %collective-permute-start.4) | collective-permute-done | bytes 626720 | tf_op jit(solution)/shard_map/ppermute | solution.py:57
  37.6 7.0 %collective-permute-start = (bf16[4624,128]{1,0:T(8,128)(2,1)S(1)}, bf16[4624,128]{1,0:T(8,128)(2,1)}, u32[]{:S(2)}, u32[]{:S(2)}) collective-permute-start(bf16[4624,128]{1,0:T(8,128)(2,1)S(1)} %constant_dynamic-update-slice_fusion.refs_2_.refs_4_), channel_id=1, source_target_pairs={{0,96},{1,25},{2,98},{3,27},{4,100},{5,29},{6,102},{7,31},{8,104},... | collective-permute-start | bytes 3551240 | tf_op jit(solution)/shard_map/ppermute | solution.py:57
  44.7 0.7 slice_bitcast_fusion.1
  45.4 0.7 slice_bitcast_fusion.2
  46.0 0.1 reshape.41
  46.1 0.1 reshape.42
  46.2 0.3 convert_reduce_fusion.1
  46.5 0.1 reshape.39.refs_1_
  46.6 0.1 reshape.38.refs_0_
  46.7 9.1 %shard_map.93 = (f32[512,1024]{1,0:T(8,128)S(1)}, f32[512,128]{1,0:T(8,128)S(1)}) custom-call(s32[16]{0:T(128)S(1)} %reshape.38.refs_0_, s32[16]{0:T(128)S(1)} %reshape.39.refs_1_, bf16[272,1152]{1,0:T(8,128)(2,1)} %collective-permute-done.3.refs_2_.refs_3_, bf16[272,1152]{1,0:T(8,128)(2,1)} %collective-permute-done.4.refs_3_.refs_4_, ...), custom_call_target="tpu_custom_call" | custom-call | flops 3221225472 | bytes 4194304 | tf_op jit(solution)/shard_map/pallas_call | solution.py:267
  55.8 1.3 copy-done.2
  57.1 0.7 copy-done.4
  57.8 0.7 slice_bitcast_fusion
  58.5 0.1 reshape.43
  58.6 0.2 convert_reduce_fusion
  58.8 0.1 reshape.40.refs_0_.refs_2_
  58.9 5.5 %shard_map.94 = (f32[256,1024]{1,0:T(8,128)S(1)}, f32[256,128]{1,0:T(8,128)S(1)}) custom-call(s32[16]{0:T(128)S(1)} %reshape.40.refs_0_.refs_2_, bf16[272,1152]{1,0:T(8,128)(2,1)} %collective-permute-done.5.refs_1_.refs_5_, bf16[4624,128]{1,0:T(8,128)(2,1)S(1)} %constant_dynamic-update-slice_fusion.refs_2_.refs_4_), custom_call_target="tpu_custom_call" | custom-call | flops 1610612736 | bytes 2097152 | tf_op jit(solution)/shard_map/pallas_call | solution.py:267
  64.4 19.8 %shard_map.95 = (f32[768,1024]{1,0:T(8,128)S(1)}, f32[768,128]{1,0:T(8,128)S(1)}) custom-call(s32[16]{0:T(128)S(1)} %reshape.38.refs_0_, s32[16]{0:T(128)S(1)} %reshape.39.refs_1_, s32[16]{0:T(128)S(1)} %reshape.40.refs_0_.refs_2_, bf16[272,1152]{1,0:T(8,128)(2,1)} %collective-permute-done.3.refs_2_.refs_3_, ...), custom_call_target="tpu_custom_call" | custom-call | flops 9663676416 | bytes 6291456 | tf_op jit(solution)/shard_map/pallas_call | solution.py:267
  84.3 0.0 slice-start
  84.3 15.4 %shard_map.96 = (bf16[256,1152]{1,0:T(8,128)(2,1)S(1)}, bf16[256,1152]{1,0:T(8,128)(2,1)S(1)}, bf16[256,1152]{1,0:T(8,128)(2,1)S(1)}) custom-call(s32[16]{0:T(128)S(1)} %reshape.38.refs_0_, s32[16]{0:T(128)S(1)} %reshape.39.refs_1_, s32[16]{0:T(128)S(1)} %reshape.40.refs_0_.refs_2_, bf16[272,1152]{1,0:T(8,128)(2,1)} %collective-permute-done.3.refs_2_.refs_3_, ...), custom_call_target="tpu_custom_call" | custom-call | flops 4831838208 | bytes 6291456 | tf_op jit(solution)/shard_map/pallas_call | solution.py:267
  99.7 0.1 collective-permute-start.6
  99.8 0.0 slice-start.2
  99.8 6.1 %collective-permute-start.7 = (bf16[256,1152]{1,0:T(8,128)(2,1)S(1)}, bf16[256,1152]{1,0:T(8,128)(2,1)S(1)}, u32[]{:S(2)}, u32[]{:S(2)}) collective-permute-start(bf16[256,1152]{1,0:T(8,128)(2,1)S(1)} %get-tuple-element.36), channel_id=1, source_target_pairs={{0,24},{1,97},{2,26},{3,99},{4,28},{5,101},{6,30},{7,103},{8,0},{9... | collective-permute-start | bytes 1769480 | tf_op jit(solution)/shard_map/ppermute | solution.py:57
  105.9 5.3 %collective-permute-start.8 = (bf16[256,1152]{1,0:T(8,128)(2,1)S(1)}, bf16[256,1152]{1,0:T(8,128)(2,1)S(1)}, u32[]{:S(2)}, u32[]{:S(2)}) collective-permute-start(bf16[256,1152]{1,0:T(8,128)(2,1)S(1)} %get-tuple-element.37), channel_id=1, source_target_pairs={{0,16},{1,65},{2,18},{3,67},{4,20},{5,69},{6,22},{7,71},{8,24},{9,... | collective-permute-start | bytes 1769480 | tf_op jit(solution)/shard_map/ppermute | solution.py:57
  111.2 7.9 %shard_map.92.refs_0_ = bf16[256,1152]{1,0:T(8,128)(2,1)S(1)} custom-call(s32[16]{0:T(128)S(1)} %reshape.36.refs_0_, bf16[272,1152]{1,0:T(8,128)(2,1)S(1)} %fusion.4.refs_1_, bf16[4624,128]{1,0:T(8,128)(2,1)} %collective-permute-done.refs_2_.refs_6_, bf16[4624,128]{1,0:T(8,128)(2,1)} %collective-permute-done.1.refs_3_.refs_7_, ...), custom_call_target="tpu_custom_call" | custom-call | flops 4831838208 | bytes 2097152 | tf_op jit(solution)/shard_map/pallas_call | solution.py:267
  119.1 4.5 %collective-permute-done.8.refs_3_ = bf16[256,1152]{1,0:T(8,128)(2,1)S(1)} collective-permute-done((bf16[256,1152]{1,0:T(8,128)(2,1)S(1)}, bf16[256,1152]{1,0:T(8,128)(2,1)S(1)}, u32[]{:S(2)}, u32[]{:S(2)}) %collective-permute-start.8) | collective-permute-done | bytes 589856 | tf_op jit(solution)/shard_map/ppermute | solution.py:57
  123.6 5.8 %shard_map.97 = (bf16[128,4096]{1,0:T(8,128)(2,1)S(1)}, bf16[128,4096]{1,0:T(8,128)(2,1)}, bf16[256,1024]{1,0:T(8,128)(2,1)S(1)}) custom-call(s32[1]{0:T(128)} %bitcast.core, bf16[256,1152]{1,0:T(8,128)(2,1)S(1)} %shard_map.92.refs_0_, bf16[256,1152]{1,0:T(8,128)(2,1)S(1)} %collective-permute-done.6.refs_1_, ...), custom_call_target="tpu_custom_call" | custom-call | flops 4294967296 | bytes 10485760 | tf_op jit(solution)/shard_map/pallas_call | solution.py:353
  129.4 1.9 %collective-permute-start.9 = (bf16[128,4096]{1,0:T(8,128)(2,1)}, bf16[128,4096]{1,0:T(8,128)(2,1)}, u32[]{:S(2)}, u32[]{:S(2)}) collective-permute-start(bf16[128,4096]{1,0:T(8,128)(2,1)} %get-tuple-element.39), channel_id=1, source_target_pairs={{0,1},{1,0},{2,3},{3,2},{4,5},{5,4},{6,7},{7,6},{8,9},{9,8},{10,11... | collective-permute-start | bytes 3145736 | tf_op jit(solution)/shard_map/ppermute | solution.py:57
  131.3 3.5 %shard_map.98 = (bf16[128,4096]{1,0:T(8,128)(2,1)S(1)}, bf16[128,4096]{1,0:T(8,128)(2,1)S(1)}) custom-call(s32[1]{0:T(128)} %bitcast.core, bf16[256,1024]{1,0:T(8,128)(2,1)S(1)} %get-tuple-element.40.refs_0_, bf16[1024,8192]{1,0:T(8,128)(2,1)S(1)} %bitcast.12), custom_call_target="tpu_custom_call" | custom-call | flops 4294967296 | bytes 10485760 | tf_op jit(solution)/shard_map/pallas_call | solution.py:353
  134.9 0.1 collective-permute-start.13
  135.1 1.2 add_convert_fusion.7
  136.3 2.5 %collective-permute-start.10 = (bf16[32,4096]{1,0:T(8,128)(2,1)S(1)}, bf16[32,4096]{1,0:T(8,128)(2,1)S(1)}, u32[]{:S(2)}, u32[]{:S(2)}) collective-permute-start(bf16[32,4096]{1,0:T(8,128)(2,1)S(1)} %get-tuple-element.47), channel_id=1, source_target_pairs={{0,6},{1,7},{2,0},{3,1},{4,2},{5,3},{6,4},{7,5},{8,14},{9,15},{10,... | collective-permute-start | bytes 786440 | tf_op jit(solution)/shard_map/ppermute | solution.py:57
  138.8 1.2 add_convert_fusion.3
  140.0 0.3 collective-permute-start.14
  140.2 2.6 %collective-permute-start.15 = (bf16[32,4096]{1,0:T(8,128)(2,1)S(1)}, bf16[32,4096]{1,0:T(8,128)(2,1)S(1)}, u32[]{:S(2)}, u32[]{:S(2)}) collective-permute-start(bf16[32,4096]{1,0:T(8,128)(2,1)S(1)} %get-tuple-element.50), channel_id=1, source_target_pairs={{0,6},{1,7},{2,0},{3,1},{4,2},{5,3},{6,4},{7,5},{8,14},{9,15},{10,... | collective-permute-start | bytes 786440 | tf_op jit(solution)/shard_map/ppermute | solution.py:57
  142.8 4.4 %collective-permute-done.11 = bf16[32,4096]{1,0:T(8,128)(2,1)S(1)} collective-permute-done((bf16[32,4096]{1,0:T(8,128)(2,1)S(1)}, bf16[32,4096]{1,0:T(8,128)(2,1)S(1)}, u32[]{:S(2)}, u32[]{:S(2)}) %collective-permute-start.11) | collective-permute-done | bytes 262176 | tf_op jit(solution)/shard_map/ppermute | solution.py:57
  147.2 1.0 add_convert_fusion.5
  148.3 0.1 collective-permute-start.12
  148.3 1.4 collective-permute-done.15
  149.7 1.1 add_convert_fusion.1
  150.8 3.5 %collective-permute-start.16 = (bf16[32,4096]{1,0:T(8,128)(2,1)S(1)}, bf16[32,4096]{1,0:T(8,128)(2,1)S(1)}, u32[]{:S(2)}, u32[]{:S(2)}) collective-permute-start(bf16[32,4096]{1,0:T(8,128)(2,1)S(1)} %add_convert_fusion.1), channel_id=1, source_target_pairs={{0,6},{1,7},{2,0},{3,1},{4,2},{5,3},{6,4},{7,5},{8,14},{9,15},{10,... | collective-permute-start | bytes 786440 | tf_op jit(solution)/shard_map/ppermute | solution.py:57
  154.2 3.9 %collective-permute-done.12 = bf16[32,4096]{1,0:T(8,128)(2,1)S(1)} collective-permute-done((bf16[32,4096]{1,0:T(8,128)(2,1)S(1)}, bf16[32,4096]{1,0:T(8,128)(2,1)S(1)}, u32[]{:S(2)}, u32[]{:S(2)}) %collective-permute-start.12) | collective-permute-done | bytes 262176 | tf_op jit(solution)/shard_map/ppermute | solution.py:57
  158.2 1.1 add_convert_fusion.4
  159.3 1.1 add_convert_fusion
  160.4 0.8 pad_maximum_fusion
  (44 shorter events, 0.2 us)
Async XLA Ops:
  0.0 9.5 %copy-start.6 = (bf16[2048,128]{1,0:T(8,128)(2,1)S(1)}, bf16[2048,128]{1,0:T(8,128)(2,1)}, u32[]{:S(2)}) copy-start(bf16[2048,128]{1,0:T(8,128)(2,1)} %param.13) | copy-start | bytes 1572868
  1.6 7.9 %copy-start.8 = (bf16[256,128]{1,0:T(8,128)(2,1)S(1)}, bf16[256,128]{1,0:T(8,128)(2,1)}, u32[]{:S(2)}) copy-start(bf16[256,128]{1,0:T(8,128)(2,1)} %param.10) | copy-start | bytes 196612
  1.8 7.7 %copy-start.7 = (bf16[2048,128]{1,0:T(8,128)(2,1)S(1)}, bf16[2048,128]{1,0:T(8,128)(2,1)}, u32[]{:S(2)}) copy-start(bf16[2048,128]{1,0:T(8,128)(2,1)} %param.14) | copy-start | bytes 1572868
  3.0 6.7 %copy-start.9 = (bf16[256,128]{1,0:T(8,128)(2,1)S(1)}, bf16[256,128]{1,0:T(8,128)(2,1)}, u32[]{:S(2)}) copy-start(bf16[256,128]{1,0:T(8,128)(2,1)} %param.11) | copy-start | bytes 196612
  3.0 11.1 %copy-start.10 = (s32[4]{0:T(128)S(1)}, s32[4]{0:T(128)}, u32[]{:S(2)}) copy-start(s32[4]{0:T(128)} %constant.141.clone) | copy-start | bytes 52
  3.0 54.8 %collective-permute-start.5 = (bf16[272,1152]{1,0:T(8,128)(2,1)S(1)}, bf16[272,1152]{1,0:T(8,128)(2,1)}, u32[]{:S(2)}, u32[]{:S(2)}) collective-permute-start(bf16[272,1152]{1,0:T(8,128)(2,1)S(1)} %fusion.4.refs_1_), channel_id=1, source_target_pairs={{0,16},{1,65},{2,18},{3,67},{4,20},{5,69},{6,22},{7,71},{8,24},{9,... | collective-permute-start | bytes 1880072 | tf_op jit(solution)/shard_map/ppermute | solution.py:57
  6.8 30.9 %collective-permute-start.4 = (bf16[272,1152]{1,0:T(8,128)(2,1)S(1)}, bf16[272,1152]{1,0:T(8,128)(2,1)}, u32[]{:S(2)}, u32[]{:S(2)}) collective-permute-start(bf16[272,1152]{1,0:T(8,128)(2,1)S(1)} %fusion.4.refs_1_), channel_id=1, source_target_pairs={{0,8},{1,33},{2,10},{3,35},{4,12},{5,37},{6,14},{7,39},{8,16},{9,4... | collective-permute-start | bytes 1880072 | tf_op jit(solution)/shard_map/ppermute | solution.py:57
  7.2 38.2 %collective-permute-start.3 = (bf16[272,1152]{1,0:T(8,128)(2,1)S(1)}, bf16[272,1152]{1,0:T(8,128)(2,1)}, u32[]{:S(2)}, u32[]{:S(2)}) collective-permute-start(bf16[272,1152]{1,0:T(8,128)(2,1)S(1)} %fusion.4.refs_1_), channel_id=1, source_target_pairs={{0,24},{1,97},{2,26},{3,99},{4,28},{5,101},{6,30},{7,103},{8,0},{9... | collective-permute-start | bytes 1880072 | tf_op jit(solution)/shard_map/ppermute | solution.py:57
  9.7 74.6 %collective-permute-start.2 = (bf16[4624,128]{1,0:T(8,128)(2,1)S(1)}, bf16[4624,128]{1,0:T(8,128)(2,1)S(1)}, u32[]{:S(2)}, u32[]{:S(2)}) collective-permute-start(bf16[4624,128]{1,0:T(8,128)(2,1)S(1)} %constant_dynamic-update-slice_fusion.refs_2_.refs_4_), channel_id=1, source_target_pairs={{0,64},{1,17},{2,66},{3,19},{4,68},{5,21},{6,70},{7,23},{8,72},{9,... | collective-permute-start | bytes 3551240 | tf_op jit(solution)/shard_map/ppermute | solution.py:57
  13.4 51.0 %collective-permute-start.1 = (bf16[4624,128]{1,0:T(8,128)(2,1)S(1)}, bf16[4624,128]{1,0:T(8,128)(2,1)}, u32[]{:S(2)}, u32[]{:S(2)}) collective-permute-start(bf16[4624,128]{1,0:T(8,128)(2,1)S(1)} %constant_dynamic-update-slice_fusion.refs_2_.refs_4_), channel_id=1, source_target_pairs={{0,32},{1,9},{2,34},{3,11},{4,36},{5,13},{6,38},{7,15},{8,40},{9,1... | collective-permute-start | bytes 3551240 | tf_op jit(solution)/shard_map/ppermute | solution.py:57
  18.7 1.0 copy-start
  37.6 26.8 %collective-permute-start = (bf16[4624,128]{1,0:T(8,128)(2,1)S(1)}, bf16[4624,128]{1,0:T(8,128)(2,1)}, u32[]{:S(2)}, u32[]{:S(2)}) collective-permute-start(bf16[4624,128]{1,0:T(8,128)(2,1)S(1)} %constant_dynamic-update-slice_fusion.refs_2_.refs_4_), channel_id=1, source_target_pairs={{0,96},{1,25},{2,98},{3,27},{4,100},{5,29},{6,102},{7,31},{8,104},... | collective-permute-start | bytes 3551240 | tf_op jit(solution)/shard_map/ppermute | solution.py:57
  55.8 1.3 copy-start.2
  57.1 0.7 copy-start.4
  58.9 5.5 %copy-start.3 = (f32[512,1024]{1,0:T(8,128)S(1)}, f32[512,1024]{1,0:T(8,128)}, u32[]{:S(2)}) copy-start(f32[512,1024]{1,0:T(8,128)} %copy-done.2) | copy-start | bytes 6291460
  58.9 5.5 %copy-start.5 = (f32[512,128]{1,0:T(8,128)S(1)}, f32[512,128]{1,0:T(8,128)}, u32[]{:S(2)}) copy-start(f32[512,128]{1,0:T(8,128)} %copy-done.4) | copy-start | bytes 786436
  84.3 26.9 %copy-start.1 = (f32[256,1024]{1,0:T(8,128)S(1)}, f32[256,1024]{1,0:T(8,128)}, u32[]{:S(2)}) copy-start(f32[256,1024]{1,0:T(8,128)} %copy-done) | copy-start | bytes 3145732
  84.3 39.3 %slice-start = ((s8[16777216]{0:T(1024)(128)(4,1)}), s8[4194304]{0:T(1024)(128)(4,1)S(1)}, s32[]{:S(2)}) async-start(s8[16777216]{0:T(1024)(128)(4,1)} %bitcast.11), calls=%async_computation | async-start | bytes 8388608
  84.3 39.3 %slice-start.1 = ((s8[16777216]{0:T(1024)(128)(4,1)}), s8[4194304]{0:T(1024)(128)(4,1)S(1)}, s32[]{:S(2)}) async-start(s8[16777216]{0:T(1024)(128)(4,1)} %bitcast.11), calls=%async_computation.1 | async-start | bytes 8388608
  99.7 19.3 %collective-permute-start.6 = (bf16[256,1152]{1,0:T(8,128)(2,1)S(1)}, bf16[256,1152]{1,0:T(8,128)(2,1)S(1)}, u32[]{:S(2)}, u32[]{:S(2)}) collective-permute-start(bf16[256,1152]{1,0:T(8,128)(2,1)S(1)} %get-tuple-element.35), channel_id=1, source_target_pairs={{0,8},{1,33},{2,10},{3,35},{4,12},{5,37},{6,14},{7,39},{8,16},{9,4... | collective-permute-start | bytes 1769480 | tf_op jit(solution)/shard_map/ppermute | solution.py:57
  99.8 23.8 %slice-start.2 = ((s8[16777216]{0:T(1024)(128)(4,1)}), s8[4194304]{0:T(1024)(128)(4,1)S(1)}, s32[]{:S(2)}) async-start(s8[16777216]{0:T(1024)(128)(4,1)} %bitcast.11), calls=%async_computation.2 | async-start | bytes 8388608
  99.8 19.2 %collective-permute-start.7 = (bf16[256,1152]{1,0:T(8,128)(2,1)S(1)}, bf16[256,1152]{1,0:T(8,128)(2,1)S(1)}, u32[]{:S(2)}, u32[]{:S(2)}) collective-permute-start(bf16[256,1152]{1,0:T(8,128)(2,1)S(1)} %get-tuple-element.36), channel_id=1, source_target_pairs={{0,24},{1,97},{2,26},{3,99},{4,28},{5,101},{6,30},{7,103},{8,0},{9... | collective-permute-start | bytes 1769480 | tf_op jit(solution)/shard_map/ppermute | solution.py:57
  105.9 17.7 %slice-start.3 = ((s8[16777216]{0:T(1024)(128)(4,1)}), s8[4194304]{0:T(1024)(128)(4,1)S(1)}, s32[]{:S(2)}) async-start(s8[16777216]{0:T(1024)(128)(4,1)} %bitcast.11), calls=%async_computation.3 | async-start | bytes 8388608
  105.9 17.7 %collective-permute-start.8 = (bf16[256,1152]{1,0:T(8,128)(2,1)S(1)}, bf16[256,1152]{1,0:T(8,128)(2,1)S(1)}, u32[]{:S(2)}, u32[]{:S(2)}) collective-permute-start(bf16[256,1152]{1,0:T(8,128)(2,1)S(1)} %get-tuple-element.37), channel_id=1, source_target_pairs={{0,16},{1,65},{2,18},{3,67},{4,20},{5,69},{6,22},{7,71},{8,24},{9,... | collective-permute-start | bytes 1769480 | tf_op jit(solution)/shard_map/ppermute | solution.py:57
  129.4 5.7 %collective-permute-start.9 = (bf16[128,4096]{1,0:T(8,128)(2,1)}, bf16[128,4096]{1,0:T(8,128)(2,1)}, u32[]{:S(2)}, u32[]{:S(2)}) collective-permute-start(bf16[128,4096]{1,0:T(8,128)(2,1)} %get-tuple-element.39), channel_id=1, source_target_pairs={{0,1},{1,0},{2,3},{3,2},{4,5},{5,4},{6,7},{7,6},{8,9},{9,8},{10,11... | collective-permute-start | bytes 3145736 | tf_op jit(solution)/shard_map/ppermute | solution.py:57
  134.9 3.9 %collective-permute-start.13 = (bf16[128,4096]{1,0:T(8,128)(2,1)S(1)}, bf16[128,4096]{1,0:T(8,128)(2,1)}, u32[]{:S(2)}, u32[]{:S(2)}) collective-permute-start(bf16[128,4096]{1,0:T(8,128)(2,1)S(1)} %get-tuple-element.42), channel_id=1, source_target_pairs={{0,1},{1,0},{2,3},{3,2},{4,5},{5,4},{6,7},{7,6},{8,9},{9,8},{10,11... | collective-permute-start | bytes 3145736 | tf_op jit(solution)/shard_map/ppermute | solution.py:57
  136.3 18.0 %collective-permute-start.10 = (bf16[32,4096]{1,0:T(8,128)(2,1)S(1)}, bf16[32,4096]{1,0:T(8,128)(2,1)S(1)}, u32[]{:S(2)}, u32[]{:S(2)}) collective-permute-start(bf16[32,4096]{1,0:T(8,128)(2,1)S(1)} %get-tuple-element.47), channel_id=1, source_target_pairs={{0,6},{1,7},{2,0},{3,1},{4,2},{5,3},{6,4},{7,5},{8,14},{9,15},{10,... | collective-permute-start | bytes 786440 | tf_op jit(solution)/shard_map/ppermute | solution.py:57
  138.8 8.4 %collective-permute-start.11 = (bf16[32,4096]{1,0:T(8,128)(2,1)S(1)}, bf16[32,4096]{1,0:T(8,128)(2,1)S(1)}, u32[]{:S(2)}, u32[]{:S(2)}) collective-permute-start(bf16[32,4096]{1,0:T(8,128)(2,1)S(1)} %get-tuple-element.48), channel_id=1, source_target_pairs={{0,2},{1,3},{2,4},{3,5},{4,6},{5,7},{6,0},{7,1},{8,10},{9,11},{10,... | collective-permute-start | bytes 786440 | tf_op jit(solution)/shard_map/ppermute | solution.py:57
  140.0 19.3 %collective-permute-start.14 = (bf16[32,4096]{1,0:T(8,128)(2,1)S(1)}, bf16[32,4096]{1,0:T(8,128)(2,1)S(1)}, u32[]{:S(2)}, u32[]{:S(2)}) collective-permute-start(bf16[32,4096]{1,0:T(8,128)(2,1)S(1)} %get-tuple-element.49), channel_id=1, source_target_pairs={{0,2},{1,3},{2,4},{3,5},{4,6},{5,7},{6,0},{7,1},{8,10},{9,11},{10,... | collective-permute-start | bytes 786440 | tf_op jit(solution)/shard_map/ppermute | solution.py:57
  140.2 9.5 %collective-permute-start.15 = (bf16[32,4096]{1,0:T(8,128)(2,1)S(1)}, bf16[32,4096]{1,0:T(8,128)(2,1)S(1)}, u32[]{:S(2)}, u32[]{:S(2)}) collective-permute-start(bf16[32,4096]{1,0:T(8,128)(2,1)S(1)} %get-tuple-element.50), channel_id=1, source_target_pairs={{0,6},{1,7},{2,0},{3,1},{4,2},{5,3},{6,4},{7,5},{8,14},{9,15},{10,... | collective-permute-start | bytes 786440 | tf_op jit(solution)/shard_map/ppermute | solution.py:57
  148.3 9.9 %collective-permute-start.12 = (bf16[32,4096]{1,0:T(8,128)(2,1)S(1)}, bf16[32,4096]{1,0:T(8,128)(2,1)S(1)}, u32[]{:S(2)}, u32[]{:S(2)}) collective-permute-start(bf16[32,4096]{1,0:T(8,128)(2,1)S(1)} %add_convert_fusion.5), channel_id=1, source_target_pairs={{0,2},{1,3},{2,4},{3,5},{4,6},{5,7},{6,0},{7,1},{8,10},{9,11},{10,... | collective-permute-start | bytes 786440 | tf_op jit(solution)/shard_map/ppermute | solution.py:57
  150.8 8.5 %collective-permute-start.16 = (bf16[32,4096]{1,0:T(8,128)(2,1)S(1)}, bf16[32,4096]{1,0:T(8,128)(2,1)S(1)}, u32[]{:S(2)}, u32[]{:S(2)}) collective-permute-start(bf16[32,4096]{1,0:T(8,128)(2,1)S(1)} %add_convert_fusion.1), channel_id=1, source_target_pairs={{0,6},{1,7},{2,0},{3,1},{4,2},{5,3},{6,4},{7,5},{8,14},{9,15},{10,... | collective-permute-start | bytes 786440 | tf_op jit(solution)/shard_map/ppermute | solution.py:57
